TPU v7x, 32 devices: a whole 2x2x4 slice. The times are simulated.
32 devices in a mesh: dev: 32 (over z, y, x, core).
Axes of the slice: x: 2, y: 2, z: 4, core: 2. Of those that a mesh axis runs over, the one named last changes fastest.
Arguments:
- tokens: bfloat16 [10240, 1600], P('dev'), may hold values from -6 to 6
- cotangent: bfloat16 [10240, 1600], P('dev'), may hold values from -6 to 6
- w_qkv: bfloat16 [38400, 200], P('dev')
- w_out: bfloat16 [12800, 200], P('dev'), may hold values from -0.625 to 0.625
- w_fc: bfloat16 [51200, 200], P('dev'), may hold values from -0.15625 to 0.15625
- w_proj: bfloat16 [51200, 200], P('dev'), may hold values from -0.078125 to 0.078125
- ln1_gain: float32 [1600], replicated, may hold values from 0.5 to 1.5
- ln1_bias: float32 [1600], replicated, may hold values from -1.25 to 1.25
- q_bias: float32 [1600], replicated, may hold values from -1.75 to 1.75
- v_bias: float32 [1600], replicated, may hold values from -1.75 to 1.75
- out_bias: float32 [1600], replicated, may hold values from -1.75 to 1.75
- ln2_gain: float32 [1600], replicated, may hold values from 0.5 to 1.5
- ln2_bias: float32 [1600], replicated, may hold values from -1.25 to 1.25
- fc_bias: float32 [6400], replicated, may hold values from -1.75 to 1.75
- proj_bias: float32 [1600], replicated, may hold values from -1.75 to 1.75
- seg_lengths: int32 [4, 13], replicated, may hold values from 1 to 1024, 2560 in all within a row
- parents: int32 [4, 13], replicated, may hold values from 0 to 11, as said below
Outputs:
- output: bfloat16 [10240, 1600], P('dev')
- input_grad: float32 [10240, 1600], P('dev')
- qkv_grad: float32 [38400, 200], P('dev')
- out_grad: float32 [12800, 200], P('dev')
- fc_grad: float32 [51200, 200], P('dev')
- proj_grad: float32 [51200, 200], P('dev')
- ln1_gain_grad: float32 [1600], replicated
- ln1_bias_grad: float32 [1600], replicated
- q_bias_grad: float32 [1600], replicated
- v_bias_grad: float32 [1600], replicated
- out_bias_grad: float32 [1600], replicated
- ln2_gain_grad: float32 [1600], replicated
- ln2_bias_grad: float32 [1600], replicated
- fc_bias_grad: float32 [6400], replicated
- proj_bias_grad: float32 [1600], replicated
- logit_max: float32 [25], replicated
- clipped_qkv: bfloat16 [38400, 200], P('dev')
Inputs may be any that keep to these rules, and one draw needn't show every extreme that they name: `seg_lengths`: the 13 lengths of a tree sum to 2560. parents[t, 0] is 0 and marks the root; for s >= 1, parents[t, s] < s.
All inputs are finite; a program needn't handle non-finite values.
Results may differ from a plain program's by a relative error of at most 0.013.
The roundings to bfloat16 on the way count: a program that leaves them out, or rounds other values in their place, can miss the bound.
Values may be sent and summed in bfloat16 or wider, within the bound.
No kernel may reach another device: no remote copies, remote signals or barrier semaphores. Data moves between devices by JAX's collectives and lax.ppermute only.
A program may use at most 448 MiB of HBM per device.

v0:
```python
from functools import partial

import jax
import jax.numpy as jnp
from jax import lax
from jax.sharding import PartitionSpec as P

HEAD_DIM = 64
TREE_TOK = 2560


EPS = 1e-05
TAU = 7.0
NEGATIVE = -1e30


def passed_along(value, axis, steps):
    count = lax.axis_size(axis)
    leading, last = (max(0, -steps), min(count, count - steps))
    return lax.ppermute(value, axis, [(source, source + steps) for source in range(leading, last)])


def norm_forward(values, norm_gain, norm_shift):
    row_mean = jnp.mean(values, axis=-1, keepdims=True)
    centered = values - row_mean
    inv_std = lax.rsqrt(jnp.mean(centered * centered, axis=-1, keepdims=True) + EPS)
    normed = centered * inv_std
    return (normed * norm_gain + norm_shift, normed, inv_std)


def norm_backward(upstream, normed, inv_std, norm_gain):
    scaled = upstream * norm_gain
    inner = (
        scaled
        - jnp.mean(scaled, axis=-1, keepdims=True)
        - normed * jnp.mean(scaled * normed, axis=-1, keepdims=True)
    )
    return (inner * inv_std, jnp.sum(upstream * normed, axis=0), jnp.sum(upstream, axis=0))


def tree_tables(lengths, parent_row):
    seg_count = lengths.shape[0]
    segment_ends = jnp.cumsum(lengths)
    numbers = jnp.arange(seg_count, dtype=jnp.int32)
    ancestry = (numbers[:, None] == numbers[None, :]).astype(jnp.float32)
    cursor = numbers
    for stride in range(seg_count - 1):
        cursor = jnp.sum(
            jnp.where(cursor[:, None] == numbers[None, :], parent_row[None, :], 0), axis=1
        )
        ancestry = jnp.maximum(ancestry, (cursor[:, None] == numbers[None, :]).astype(jnp.float32))
    return (segment_ends, ancestry)


def segment_hot(position, segment_ends):
    segment = jnp.sum((position[:, None] >= segment_ends[None, :]).astype(jnp.int32), axis=1)
    numbers = jnp.arange(segment_ends.shape[0], dtype=jnp.int32)
    return (segment[:, None] == numbers[None, :]).astype(jnp.float32)


def fetch_weights(w_qkv, w_out, w_fc, w_proj, model_width, hidden):
    full_qkv, full_out, full_fc, full_proj = (
        lax.all_gather(w_qkv, "dev", axis=0, tiled=True),
        lax.all_gather(w_out, "dev", axis=0, tiled=True),
        lax.all_gather(w_fc, "dev", axis=0, tiled=True),
        lax.all_gather(w_proj, "dev", axis=0, tiled=True),
    )
    return (
        full_qkv.reshape(model_width, 3 * model_width),
        full_out.reshape(model_width, model_width),
        full_fc.reshape(model_width, hidden),
        full_proj.reshape(hidden, model_width),
    )


def fetch_blocks(key_heads, value_heads, block_count):
    blocks = [(key_heads, value_heads)]
    for stride in range(1, block_count):
        moved = passed_along((key_heads, value_heads), "dev", stride)
        blocks.append((moved[0], moved[1]))
    return blocks


def block_scores(query_heads, key_heads, allowed, score_scale):
    raw = (
        jnp.einsum("qhd,khd->hqk", query_heads, key_heads, preferred_element_type=jnp.float32)
        * score_scale
    )
    return jnp.where(allowed[None, :, :], raw, NEGATIVE)


def on_device(
    tokens,
    cotangent,
    w_qkv,
    w_out,
    w_fc,
    w_proj,
    ln1_gain,
    ln1_bias,
    q_bias,
    v_bias,
    out_bias,
    ln2_gain,
    ln2_bias,
    fc_bias,
    proj_bias,
    seg_lengths,
    parents,
):
    tok_dev, model_width = tokens.shape
    hidden = fc_bias.shape[0]
    flat_cols = w_qkv.shape[1]
    head_count = model_width // HEAD_DIM
    score_scale = HEAD_DIM ** (-0.5)
    block_count = TREE_TOK // tok_dev
    device_index = lax.axis_index("dev")
    first_row = device_index * tok_dev
    tree_index = first_row // TREE_TOK
    offset = first_row % TREE_TOK
    last_live = offset // tok_dev
    lengths = lax.dynamic_slice_in_dim(seg_lengths, tree_index, 1, 0)[0]
    parent_row = lax.dynamic_slice_in_dim(parents, tree_index, 1, 0)[0]
    segment_ends, ancestry = tree_tables(lengths, parent_row)
    query_pos = offset + jnp.arange(tok_dev, dtype=jnp.int32)
    query_paths = jnp.dot(
        segment_hot(query_pos, segment_ends), ancestry, precision=lax.Precision.HIGHEST
    )
    block_masks = []
    for stride in range(block_count):
        key_pos = query_pos - stride * tok_dev
        linked = (
            jnp.dot(
                query_paths, segment_hot(key_pos, segment_ends).T, precision=lax.Precision.HIGHEST
            )
            > 0.5
        )
        block_masks.append(
            linked & (key_pos[None, :] <= query_pos[:, None]) & (key_pos[None, :] >= 0)
        )
    fore_weights = fetch_weights(w_qkv, w_out, w_fc, w_proj, model_width, hidden)
    w_qkv_full, w_out_full, w_fc_full, w_proj_full = fore_weights
    residual_in = tokens.astype(jnp.float32)
    first_norm, normed_one, inv_one = norm_forward(residual_in, ln1_gain, ln1_bias)
    first_low = first_norm.astype(jnp.bfloat16)
    qkv_bias = jnp.concatenate([q_bias, jnp.zeros_like(q_bias), v_bias])
    projected = (
        jnp.dot(first_low, w_qkv_full, preferred_element_type=jnp.float32) + qkv_bias
    ).astype(jnp.bfloat16)
    query_heads = projected[:, :model_width].reshape(tok_dev, head_count, HEAD_DIM)
    key_heads = projected[:, model_width : 2 * model_width].reshape(tok_dev, head_count, HEAD_DIM)
    value_heads = projected[:, 2 * model_width :].reshape(tok_dev, head_count, HEAD_DIM)
    blocks = fetch_blocks(key_heads, value_heads, block_count)
    run_max = jnp.full((head_count, tok_dev), NEGATIVE, jnp.float32)
    run_sum = jnp.zeros((head_count, tok_dev), jnp.float32)
    for stride in range(block_count):

        def max_step(carry, keys=blocks[stride][0], allowed=block_masks[stride]):
            old_max, old_sum = carry
            score = block_scores(query_heads, keys, allowed, score_scale)
            new_max = jnp.maximum(old_max, jnp.max(score, axis=2))
            new_sum = old_sum * jnp.exp(old_max - new_max) + jnp.sum(
                jnp.exp(score - new_max[:, :, None]), axis=2
            )
            return (new_max, new_sum)

        run_max, run_sum = lax.cond(
            stride <= last_live, max_step, lambda carry: carry, (run_max, run_sum)
        )
    attended = jnp.zeros((tok_dev, head_count, HEAD_DIM), jnp.float32)
    for stride in range(block_count):

        def value_step(
            total, keys=blocks[stride][0], values=blocks[stride][1], allowed=block_masks[stride]
        ):
            score = block_scores(query_heads, keys, allowed, score_scale)
            probs_low = (jnp.exp(score - run_max[:, :, None]) / run_sum[:, :, None]).astype(
                jnp.bfloat16
            )
            return total + jnp.einsum(
                "hqk,khd->qhd", probs_low, values, preferred_element_type=jnp.float32
            )

        attended = lax.cond(stride <= last_live, value_step, lambda total: total, attended)
    logit_max = lax.pmax(jnp.max(run_max, axis=1), "dev")
    attn_low = attended.reshape(tok_dev, model_width).astype(jnp.bfloat16)
    middle = (
        residual_in + jnp.dot(attn_low, w_out_full, preferred_element_type=jnp.float32) + out_bias
    )
    second_norm, normed_two, inv_two = norm_forward(middle, ln2_gain, ln2_bias)
    second_low = second_norm.astype(jnp.bfloat16)
    pre_act = jnp.dot(second_low, w_fc_full, preferred_element_type=jnp.float32) + fc_bias
    activated, gelu_pull = jax.vjp(partial(jax.nn.gelu, approximate=True), pre_act)
    act_low = activated.astype(jnp.bfloat16)
    branch_two = jnp.dot(act_low, w_proj_full, preferred_element_type=jnp.float32) + proj_bias
    output = (middle + branch_two).astype(jnp.bfloat16)
    back_weights = fetch_weights(w_qkv, w_out, w_fc, w_proj, model_width, hidden)
    w_qkv_back, w_out_back, w_fc_back, w_proj_back = back_weights
    grad_out = cotangent.astype(jnp.float32)
    proj_bias_grad = jnp.sum(grad_out, axis=0)
    proj_grad = jnp.einsum("tf,td->fd", act_low, cotangent, preferred_element_type=jnp.float32)
    act_back = jnp.einsum("td,fd->tf", cotangent, w_proj_back, preferred_element_type=jnp.float32)
    pre_low = gelu_pull(act_back)[0].astype(jnp.bfloat16)
    fc_bias_grad = jnp.sum(pre_low.astype(jnp.float32), axis=0)
    fc_grad = jnp.einsum("td,tf->df", second_low, pre_low, preferred_element_type=jnp.float32)
    norm_back = jnp.einsum("tf,df->td", pre_low, w_fc_back, preferred_element_type=jnp.float32)
    mid_part, ln2_gain_grad, ln2_bias_grad = norm_backward(norm_back, normed_two, inv_two, ln2_gain)
    middle_grad = grad_out + mid_part
    branch_low = middle_grad.astype(jnp.bfloat16)
    out_bias_grad = jnp.sum(branch_low.astype(jnp.float32), axis=0)
    out_grad = jnp.einsum("td,te->de", attn_low, branch_low, preferred_element_type=jnp.float32)
    attn_back = jnp.einsum("te,de->td", branch_low, w_out_back, preferred_element_type=jnp.float32)
    attn_back = attn_back.astype(jnp.bfloat16).reshape(tok_dev, head_count, HEAD_DIM)
    back_blocks = fetch_blocks(key_heads, value_heads, block_count)
    row_delta = jnp.zeros((head_count, tok_dev), jnp.float32)
    for stride in range(block_count):

        def delta_step(
            total,
            keys=back_blocks[stride][0],
            values=back_blocks[stride][1],
            allowed=block_masks[stride],
        ):
            score = block_scores(query_heads, keys, allowed, score_scale)
            probs = jnp.exp(score - run_max[:, :, None]) / run_sum[:, :, None]
            dprobs = jnp.einsum(
                "qhd,khd->hqk", attn_back, values, preferred_element_type=jnp.float32
            )
            return total + jnp.sum(probs * dprobs, axis=2)

        row_delta = lax.cond(stride <= last_live, delta_step, lambda total: total, row_delta)
    query_grad = jnp.zeros((tok_dev, head_count, HEAD_DIM), jnp.float32)
    key_grad = jnp.zeros((tok_dev, head_count, HEAD_DIM), jnp.float32)
    value_grad = jnp.zeros((tok_dev, head_count, HEAD_DIM), jnp.float32)
    empty_part = jnp.zeros((tok_dev, head_count, HEAD_DIM), jnp.float32)
    for stride in range(block_count):

        def grad_step(
            total,
            keys=back_blocks[stride][0],
            values=back_blocks[stride][1],
            allowed=block_masks[stride],
        ):
            score = block_scores(query_heads, keys, allowed, score_scale)
            probs = jnp.exp(score - run_max[:, :, None]) / run_sum[:, :, None]
            dprobs = jnp.einsum(
                "qhd,khd->hqk", attn_back, values, preferred_element_type=jnp.float32
            )
            dscore = (probs * (dprobs - row_delta[:, :, None])).astype(jnp.bfloat16)
            new_total = (
                total
                + jnp.einsum("hqk,khd->qhd", dscore, keys, preferred_element_type=jnp.float32)
                * score_scale
            )
            key_part = (
                jnp.einsum("hqk,qhd->khd", dscore, query_heads, preferred_element_type=jnp.float32)
                * score_scale
            )
            value_part = jnp.einsum(
                "hqk,qhd->khd",
                probs.astype(jnp.bfloat16),
                attn_back,
                preferred_element_type=jnp.float32,
            )
            return (new_total, key_part, value_part)

        def grad_skip(total):
            return (total, empty_part, empty_part)

        query_grad, key_part, value_part = lax.cond(
            stride <= last_live, grad_step, grad_skip, query_grad
        )
        if stride == 0:
            key_grad = key_part
            value_grad = value_part
        else:
            returned = (
                passed_along(key_part.astype(jnp.bfloat16), "dev", -stride).astype(key_part.dtype),
                passed_along(value_part.astype(jnp.bfloat16), "dev", -stride).astype(
                    value_part.dtype
                ),
            )
            key_grad = key_grad + returned[0]
            value_grad = value_grad + returned[1]
    qkv_low = jnp.concatenate(
        [
            query_grad.reshape(tok_dev, model_width),
            key_grad.reshape(tok_dev, model_width),
            value_grad.reshape(tok_dev, model_width),
        ],
        axis=1,
    ).astype(jnp.bfloat16)
    column_sums = jnp.sum(qkv_low.astype(jnp.float32), axis=0)
    q_bias_grad = column_sums[:model_width]
    v_bias_grad = column_sums[2 * model_width :]
    qkv_grad = jnp.einsum("td,te->de", first_low, qkv_low, preferred_element_type=jnp.float32)
    first_back = jnp.einsum("te,de->td", qkv_low, w_qkv_back, preferred_element_type=jnp.float32)
    in_part, ln1_gain_grad, ln1_bias_grad = norm_backward(first_back, normed_one, inv_one, ln1_gain)
    input_grad = middle_grad + in_part
    shards = (
        lax.psum_scatter(qkv_grad.reshape(-1, flat_cols), "dev", scatter_dimension=0, tiled=True),
        lax.psum_scatter(out_grad.reshape(-1, flat_cols), "dev", scatter_dimension=0, tiled=True),
        lax.psum_scatter(fc_grad.reshape(-1, flat_cols), "dev", scatter_dimension=0, tiled=True),
        lax.psum_scatter(proj_grad.reshape(-1, flat_cols), "dev", scatter_dimension=0, tiled=True),
    )
    small = lax.psum(
        (
            ln1_gain_grad,
            ln1_bias_grad,
            q_bias_grad,
            v_bias_grad,
            out_bias_grad,
            ln2_gain_grad,
            ln2_bias_grad,
            fc_bias_grad,
            proj_bias_grad,
        ),
        "dev",
    )
    clip_gain = jnp.sqrt(TAU / jnp.maximum(logit_max, TAU))
    rows_dev = w_qkv.shape[0]
    flat_index = (
        device_index * rows_dev + jnp.arange(rows_dev, dtype=jnp.int32)[:, None]
    ) * flat_cols + jnp.arange(flat_cols, dtype=jnp.int32)[None, :]
    column = flat_index % (3 * model_width)
    head_of = column % model_width // HEAD_DIM
    head_numbers = jnp.arange(head_count, dtype=jnp.int32)
    head_gain = jnp.sum(
        jnp.where(
            head_of[:, :, None] == head_numbers[None, None, :], clip_gain[None, None, :], 0.0
        ),
        axis=2,
    )
    factor = jnp.where(column < 2 * model_width, head_gain, 1.0)
    clipped = (w_qkv.astype(jnp.float32) * factor).astype(jnp.bfloat16)
    return (
        output,
        input_grad,
        shards[0],
        shards[1],
        shards[2],
        shards[3],
        small[0],
        small[1],
        small[2],
        small[3],
        small[4],
        small[5],
        small[6],
        small[7],
        small[8],
        logit_max,
        clipped,
    )


def solution(mesh):
    return jax.shard_map(
        on_device,
        mesh=mesh,
        in_specs=(
            P("dev", None),
            P("dev", None),
            P("dev", None),
            P("dev", None),
            P("dev", None),
            P("dev", None),
            P(),
            P(),
            P(),
            P(),
            P(),
            P(),
            P(),
            P(),
            P(),
            P(),
            P(),
        ),
        out_specs=(
            P("dev", None),
            P("dev", None),
            P("dev", None),
            P("dev", None),
            P("dev", None),
            P("dev", None),
            P(),
            P(),
            P(),
            P(),
            P(),
            P(),
            P(),
            P(),
            P(),
            P(),
            P("dev", None),
        ),
        check_vma=False,
    )
```

profile of v0, /device:TPU:0, one launch (start us, length us, event | category | flops | bytes accessed | tf_op | source)
XLA Modules:
  0.0 3471.6 jit_solution(3735165850242369770)
XLA Ops:
  16.4 110.3 %all-gather.10.cloned.1.call-done = bf16[32,1200,200]{1,2,0:T(8,128)(2,1)} async-done(((bf16[1,1200,200]{1,2,0:T(8,128)(2,1)}), bf16[32,1200,200]{1,2,0:T(8,128)(2,1)}) %all-gather.10.cloned.1.call-update) | async-done | bytes 15360016 | tf_op jit(solution)/shard_map/all_gather | solution.py:63
  126.7 25.7 copy.192
  152.4 32.5 reshape.418
  184.9 11.9 fusion.96
  233.6 13.7 collective-permute-start.1
  247.2 12.6 collective-permute-done.5
  261.2 26.3 collective-permute-done.4
  292.1 62.2 %collective-permute-done.3 = bf16[320,25,64]{0,2,1:T(8,128)(2,1)} collective-permute-done((bf16[320,25,64]{0,2,1:T(8,128)(2,1)S(1)}, bf16[320,25,64]{0,2,1:T(8,128)(2,1)}, u32[]{:S(2)}, u32[]{:S(2)}) %collective-permute-start.3) | collective-permute-done | bytes 1024032 | tf_op jit(solution)/shard_map/ppermute | solution.py:20
  363.8 37.2 %collective-permute-start.13 = (bf16[320,25,64]{0,2,1:T(8,128)(2,1)}, bf16[320,25,64]{0,2,1:T(8,128)(2,1)}, u32[]{:S(2)}, u32[]{:S(2)}) collective-permute-start(bf16[320,25,64]{0,2,1:T(8,128)(2,1)} %bitcast.38), channel_id=1, source_target_pairs={{0,7},{1,8},{2,9},{3,10},{4,11},{5,12},{6,13},{7,14},{8,15},{9,16}... | collective-permute-start | bytes 3072008 | tf_op jit(solution)/shard_map/ppermute | solution.py:20
  401.0 58.4 %collective-permute-start.12 = (bf16[320,25,64]{0,2,1:T(8,128)(2,1)}, bf16[320,25,64]{0,2,1:T(8,128)(2,1)}, u32[]{:S(2)}, u32[]{:S(2)}) collective-permute-start(bf16[320,25,64]{0,2,1:T(8,128)(2,1)} %bitcast.38), channel_id=1, source_target_pairs={{0,6},{1,7},{2,8},{3,9},{4,10},{5,11},{6,12},{7,13},{8,14},{9,15},... | collective-permute-start | bytes 3072008 | tf_op jit(solution)/shard_map/ppermute | solution.py:20
  462.8 7.7 collective-permute-start.10
  470.5 73.0 %collective-permute-start.9 = (bf16[320,25,64]{0,2,1:T(8,128)(2,1)}, bf16[320,25,64]{0,2,1:T(8,128)(2,1)}, u32[]{:S(2)}, u32[]{:S(2)}) collective-permute-start(bf16[320,25,64]{0,2,1:T(8,128)(2,1)} %bitcast.38), channel_id=1, source_target_pairs={{0,3},{1,4},{2,5},{3,6},{4,7},{5,8},{6,9},{7,10},{8,11},{9,12},{10... | collective-permute-start | bytes 3072008 | tf_op jit(solution)/shard_map/ppermute | solution.py:20
  548.4 11.8 reshape.422
  561.8 7.4 conditional.32
  592.5 9.0 conditional.40
  592.5 8.9 fusion.11
  602.8 7.1 conditional.43
  610.0 8.1 conditional.45
  632.2 29.7 copy.205
  661.9 43.4 %reshape.424 = bf16[6400,1600]{1,0:T(8,128)(2,1)} reshape(bf16[32,1600,200]{2,1,0:T(8,128)(2,1)} %copy.205) | data formatting | bytes 40960000 | tf_op jit(solution)/shard_map/reshape | solution.py:72
  705.3 29.0 copy.204
  734.4 48.2 %reshape.423 = bf16[1600,6400]{1,0:T(8,128)(2,1)} reshape(bf16[32,1600,200]{2,1,0:T(8,128)(2,1)} %copy.204) | data formatting | bytes 40960000 | tf_op jit(solution)/shard_map/reshape | solution.py:71
  782.6 14.4 fusion.216
  796.9 19.7 convert_reduce_fusion
  816.6 16.9 multiply_reduce_fusion.8
  847.0 9.9 conditional.48
  867.3 27.1 conditional.56
  934.2 376.0 %collective-permute-done.20 = bf16[320,25,64]{0,2,1:T(8,128)(2,1)S(1)} collective-permute-done((bf16[320,25,64]{0,2,1:T(8,128)(2,1)}, bf16[320,25,64]{0,2,1:T(8,128)(2,1)S(1)}, u32[]{:S(2)}, u32[]{:S(2)}) %collective-permute-start.20) | collective-permute-done | bytes 1024032 | tf_op jit(solution)/shard_map/ppermute | solution.py:20
  1311.5 14.1 collective-permute-done.27
  1330.8 26.4 collective-permute-done.17
  1361.2 19.3 collective-permute-done.14
  1386.1 42.6 %collective-permute-done.24 = bf16[320,25,64]{0,2,1:T(8,128)(2,1)S(1)} collective-permute-done((bf16[320,25,64]{0,2,1:T(8,128)(2,1)}, bf16[320,25,64]{0,2,1:T(8,128)(2,1)S(1)}, u32[]{:S(2)}, u32[]{:S(2)}) %collective-permute-start.24) | collective-permute-done | bytes 1024032 | tf_op jit(solution)/shard_map/ppermute | solution.py:20
  1433.4 16.8 fusion.198
  1450.2 44.5 %reshape.429 = f32[38400,200]{1,0:T(8,128)} reshape(f32[1600,4800]{1,0:T(8,128)} %fusion.198) | data formatting | bytes 61440000 | tf_op jit(solution)/shard_map/reshape | solution.py:301
  1495.9 22.1 fusion.203
  1518.0 58.6 %reshape.432 = f32[51200,200]{1,0:T(8,128)} reshape(f32[6400,1600]{1,0:T(8,128)} %fusion.203) | data formatting | bytes 81920000 | tf_op jit(solution)/shard_map/reshape | solution.py:304
  1578.2 20.4 fusion.202
  1598.6 77.3 %reshape.431 = f32[51200,200]{1,0:T(8,128)} reshape(f32[1600,6400]{1,0:T(8,128)} %fusion.202) | data formatting | bytes 81920000 | tf_op jit(solution)/shard_map/reshape | solution.py:303
  1679.6 18.5 fusion.112
  1698.1 11.0 fusion.195
  1709.1 16.7 reshape.430
  1729.2 227.4 %pmax.7 = f32[25]{0:T(128)S(1)} all-reduce(f32[25]{0:T(128)S(1)} %reduce_max.81), channel_id=1, replica_groups=mesh['dev'=32] {'dev'}, use_global_device_ids=true, to_apply=%region_139.140 | all-reduce | flops 25 | bytes 200 | tf_op jit(solution)/shard_map/pmax | solution.py:185
  1963.1 18.0 fusion.99
  1983.3 54.7 %reduce-scatter.5.cloned.1.call-done = f32[1200,200]{1,0:T(8,128)} async-done(((f32[38400,200]{1,0:T(8,128)}), f32[1200,200]{1,0:T(8,128)}) %reduce-scatter.5.cloned.1.call-update) | async-done | bytes 960016 | tf_op jit(solution)/shard_map/reduce_scatter | solution.py:301
  2040.6 548.3 %reduce-scatter.11.cloned.1.call-done = f32[1600,200]{1,0:T(8,128)} async-done(((f32[51200,200]{1,0:T(8,128)}), f32[1600,200]{1,0:T(8,128)}) %reduce-scatter.11.cloned.1.call-update) | async-done | bytes 1280016 | tf_op jit(solution)/shard_map/reduce_scatter | solution.py:304
  2591.9 558.1 %reduce-scatter.9.cloned.1.call-done = f32[1600,200]{1,0:T(8,128)} async-done(((f32[51200,200]{1,0:T(8,128)}), f32[1600,200]{1,0:T(8,128)}) %reduce-scatter.9.cloned.1.call-update) | async-done | bytes 1280016 | tf_op jit(solution)/shard_map/reduce_scatter | solution.py:303
  3153.0 138.7 %all-reduce.3.cloned.1.call-done = (f32[1600]{0:T(1024)}, f32[1600]{0:T(1024)}, f32[1600]{0:T(1024)}, f32[1600]{0:T(1024)}, f32[1600]{0:T(1024)}, /*index=5*/f32...) async-done(((f32[1600]{0:T(1024)}, f32[1600]{0:T(1024)}, f32[1600]{0:T(1024)}, f32[1600]{0:T(1024)}, f32[1600]{0:T(1024)}, /*index=5*/f32[1600]{0:T(1024)}, ...) | async-done | bytes 76816 | tf_op jit(solution)/shard_map/psum | solution.py:306
  3291.7 161.4 %reduce-scatter.7.cloned.1.call-done = f32[400,200]{1,0:T(8,128)} async-done(((f32[12800,200]{1,0:T(8,128)}), f32[400,200]{1,0:T(8,128)}) %reduce-scatter.7.cloned.1.call-update) | async-done | bytes 320016 | tf_op jit(solution)/shard_map/reduce_scatter | solution.py:302
  (384 shorter events, 285.6 us)
Async XLA Ops:
  7.2 119.5 %all-gather.10.cloned.1.call-start = ((), (), s32[]{:S(2)}) async-start(), calls=%async_computation.9 | async-start | bytes 16896000 | tf_op jit(solution)/shard_map/all_gather | solution.py:63
  8.0 540.5 %all-gather.8.cloned.1.call-start = ((), (), s32[]{:S(2)}) async-start(), calls=%async_computation.4 | async-start | bytes 6758400 | tf_op jit(solution)/shard_map/all_gather | solution.py:64
  8.7 623.5 %all-gather.14.cloned.1.call-start = ((), (), s32[]{:S(2)}) async-start(), calls=%async_computation.11 | async-start | bytes 21964800 | tf_op jit(solution)/shard_map/all_gather | solution.py:66
  9.4 695.9 %all-gather.12.cloned.1.call-start = ((), (), s32[]{:S(2)}) async-start(), calls=%async_computation.10 | async-start | bytes 21964800 | tf_op jit(solution)/shard_map/all_gather | solution.py:65
  10.0 2027.9 %reduce-scatter.5.cloned.1.call-start = ((), (), s32[]{:S(2)}) async-start(), calls=%async_computation.5 | async-start | bytes 40550400 | tf_op jit(solution)/shard_map/reduce_scatter | solution.py:301
  200.0 392.5 %copy-start.15 = (bf16[320,1600]{0,1:T(8,128)(2,1)}, bf16[320,1600]{0,1:T(8,128)(2,1)S(1)}, u32[]{:S(2)}) copy-start(bf16[320,1600]{0,1:T(8,128)(2,1)S(1)} %copy.194) | copy-start | bytes 3072004
  200.0 33.6 collective-permute-start.6
  203.2 56.7 %collective-permute-start.5 = (bf16[320,25,64]{0,2,1:T(8,128)(2,1)S(1)}, bf16[320,25,64]{0,2,1:T(8,128)(2,1)}, u32[]{:S(2)}, u32[]{:S(2)}) collective-permute-start(bf16[320,25,64]{0,2,1:T(8,128)(2,1)S(1)} %bitcast.295), channel_id=1, source_target_pairs={{0,6},{1,7},{2,8},{3,9},{4,10},{5,11},{6,12},{7,13},{8,14},{9,15},... | collective-permute-start | bytes 3072008 | tf_op jit(solution)/shard_map/ppermute | solution.py:20
  207.6 80.0 %collective-permute-start.4 = (bf16[320,25,64]{0,2,1:T(8,128)(2,1)S(1)}, bf16[320,25,64]{0,2,1:T(8,128)(2,1)}, u32[]{:S(2)}, u32[]{:S(2)}) collective-permute-start(bf16[320,25,64]{0,2,1:T(8,128)(2,1)S(1)} %bitcast.296), channel_id=1, source_target_pairs={{0,5},{1,6},{2,7},{3,8},{4,9},{5,10},{6,11},{7,12},{8,13},{9,14},{... | collective-permute-start | bytes 3072008 | tf_op jit(solution)/shard_map/ppermute | solution.py:20
  212.6 141.7 %collective-permute-start.3 = (bf16[320,25,64]{0,2,1:T(8,128)(2,1)S(1)}, bf16[320,25,64]{0,2,1:T(8,128)(2,1)}, u32[]{:S(2)}, u32[]{:S(2)}) collective-permute-start(bf16[320,25,64]{0,2,1:T(8,128)(2,1)S(1)} %bitcast.297), channel_id=1, source_target_pairs={{0,4},{1,5},{2,6},{3,7},{4,8},{5,9},{6,10},{7,11},{8,12},{9,13},{1... | collective-permute-start | bytes 3072008 | tf_op jit(solution)/shard_map/ppermute | solution.py:20
  225.6 138.2 %collective-permute-start.2 = (bf16[320,25,64]{0,2,1:T(8,128)(2,1)S(1)}, bf16[320,25,64]{0,2,1:T(8,128)(2,1)}, u32[]{:S(2)}, u32[]{:S(2)}) collective-permute-start(bf16[320,25,64]{0,2,1:T(8,128)(2,1)S(1)} %bitcast.298), channel_id=1, source_target_pairs={{0,3},{1,4},{2,5},{3,6},{4,7},{5,8},{6,9},{7,10},{8,11},{9,12},{10... | collective-permute-start | bytes 3072008 | tf_op jit(solution)/shard_map/ppermute | solution.py:20
  233.6 167.5 %collective-permute-start.1 = (bf16[320,25,64]{0,2,1:T(8,128)(2,1)S(1)}, bf16[320,25,64]{0,2,1:T(8,128)(2,1)S(1)}, u32[]{:S(2)}, u32[]{:S(2)}) collective-permute-start(bf16[320,25,64]{0,2,1:T(8,128)(2,1)S(1)} %bitcast.299), channel_id=1, source_target_pairs={{0,2},{1,3},{2,4},{3,5},{4,6},{5,7},{6,8},{7,9},{8,10},{9,11},{10,... | collective-permute-start | bytes 3072008 | tf_op jit(solution)/shard_map/ppermute | solution.py:20
  259.9 199.5 %collective-permute-start = (bf16[320,25,64]{0,2,1:T(8,128)(2,1)S(1)}, bf16[320,25,64]{0,2,1:T(8,128)(2,1)S(1)}, u32[]{:S(2)}, u32[]{:S(2)}) collective-permute-start(bf16[320,25,64]{0,2,1:T(8,128)(2,1)S(1)} %bitcast.300), channel_id=1, source_target_pairs={{0,1},{1,2},{2,3},{3,4},{4,5},{5,6},{6,7},{7,8},{8,9},{9,10},{10,1... | collective-permute-start | bytes 3072008 | tf_op jit(solution)/shard_map/ppermute | solution.py:20
  287.6 174.2 %collective-permute-start.8 = (bf16[320,25,64]{0,2,1:T(8,128)(2,1)}, bf16[320,25,64]{0,2,1:T(8,128)(2,1)S(1)}, u32[]{:S(2)}, u32[]{:S(2)}) collective-permute-start(bf16[320,25,64]{0,2,1:T(8,128)(2,1)} %bitcast.38), channel_id=1, source_target_pairs={{0,2},{1,3},{2,4},{3,5},{4,6},{5,7},{6,8},{7,9},{8,10},{9,11},{10,... | collective-permute-start | bytes 3072008 | tf_op jit(solution)/shard_map/ppermute | solution.py:20
  354.3 116.2 %collective-permute-start.7 = (bf16[320,25,64]{0,2,1:T(8,128)(2,1)}, bf16[320,25,64]{0,2,1:T(8,128)(2,1)}, u32[]{:S(2)}, u32[]{:S(2)}) collective-permute-start(bf16[320,25,64]{0,2,1:T(8,128)(2,1)} %bitcast.38), channel_id=1, source_target_pairs={{0,1},{1,2},{2,3},{3,4},{4,5},{5,6},{6,7},{7,8},{8,9},{9,10},{10,1... | collective-permute-start | bytes 3072008 | tf_op jit(solution)/shard_map/ppermute | solution.py:20
  356.6 186.8 %copy-start.85 = (s32[320]{0:T(512)S(1)}, s32[320]{0:T(512)}, u32[]{:S(2)}) copy-start(s32[320]{0:T(512)} %get-tuple-element.1523) | copy-start | bytes 3844
  356.6 186.8 %copy-start.98 = (pred[320]{0:T(512)(128)(4,1)S(1)}, pred[320]{0:T(512)(128)(4,1)}, u32[]{:S(2)}) copy-start(pred[320]{0:T(512)(128)(4,1)} %broadcast_compare_fusion.3) | copy-start | bytes 964
  358.6 186.1 %copy-start.84 = (s32[320]{0:T(512)S(1)}, s32[320]{0:T(512)}, u32[]{:S(2)}) copy-start(s32[320]{0:T(512)} %get-tuple-element.1522) | copy-start | bytes 3844
  358.6 186.1 %copy-start.97 = (pred[320]{0:T(512)(128)(4,1)S(1)}, pred[320]{0:T(512)(128)(4,1)}, u32[]{:S(2)}) copy-start(pred[320]{0:T(512)(128)(4,1)} %broadcast_compare_fusion.4) | copy-start | bytes 964
  360.6 185.3 %copy-start.96 = (pred[320]{0:T(512)(128)(4,1)S(1)}, pred[320]{0:T(512)(128)(4,1)}, u32[]{:S(2)}) copy-start(pred[320]{0:T(512)(128)(4,1)} %broadcast_compare_fusion.5) | copy-start | bytes 964
  363.8 254.2 %collective-permute-start.13 = (bf16[320,25,64]{0,2,1:T(8,128)(2,1)}, bf16[320,25,64]{0,2,1:T(8,128)(2,1)}, u32[]{:S(2)}, u32[]{:S(2)}) collective-permute-start(bf16[320,25,64]{0,2,1:T(8,128)(2,1)} %bitcast.38), channel_id=1, source_target_pairs={{0,7},{1,8},{2,9},{3,10},{4,11},{5,12},{6,13},{7,14},{8,15},{9,16}... | collective-permute-start | bytes 3072008 | tf_op jit(solution)/shard_map/ppermute | solution.py:20
  401.0 217.0 %collective-permute-start.12 = (bf16[320,25,64]{0,2,1:T(8,128)(2,1)}, bf16[320,25,64]{0,2,1:T(8,128)(2,1)}, u32[]{:S(2)}, u32[]{:S(2)}) collective-permute-start(bf16[320,25,64]{0,2,1:T(8,128)(2,1)} %bitcast.38), channel_id=1, source_target_pairs={{0,6},{1,7},{2,8},{3,9},{4,10},{5,11},{6,12},{7,13},{8,14},{9,15},... | collective-permute-start | bytes 3072008 | tf_op jit(solution)/shard_map/ppermute | solution.py:20
  459.4 150.6 %collective-permute-start.11 = (bf16[320,25,64]{0,2,1:T(8,128)(2,1)}, bf16[320,25,64]{0,2,1:T(8,128)(2,1)}, u32[]{:S(2)}, u32[]{:S(2)}) collective-permute-start(bf16[320,25,64]{0,2,1:T(8,128)(2,1)} %bitcast.38), channel_id=1, source_target_pairs={{0,5},{1,6},{2,7},{3,8},{4,9},{5,10},{6,11},{7,12},{8,13},{9,14},{... | collective-permute-start | bytes 3072008 | tf_op jit(solution)/shard_map/ppermute | solution.py:20
  462.8 147.1 %collective-permute-start.10 = (bf16[320,25,64]{0,2,1:T(8,128)(2,1)}, bf16[320,25,64]{0,2,1:T(8,128)(2,1)}, u32[]{:S(2)}, u32[]{:S(2)}) collective-permute-start(bf16[320,25,64]{0,2,1:T(8,128)(2,1)} %bitcast.38), channel_id=1, source_target_pairs={{0,4},{1,5},{2,6},{3,7},{4,8},{5,9},{6,10},{7,11},{8,12},{9,13},{1... | collective-permute-start | bytes 3072008 | tf_op jit(solution)/shard_map/ppermute | solution.py:20
  470.5 132.3 %collective-permute-start.9 = (bf16[320,25,64]{0,2,1:T(8,128)(2,1)}, bf16[320,25,64]{0,2,1:T(8,128)(2,1)}, u32[]{:S(2)}, u32[]{:S(2)}) collective-permute-start(bf16[320,25,64]{0,2,1:T(8,128)(2,1)} %bitcast.38), channel_id=1, source_target_pairs={{0,3},{1,4},{2,5},{3,6},{4,7},{5,8},{6,9},{7,10},{8,11},{9,12},{10... | collective-permute-start | bytes 3072008 | tf_op jit(solution)/shard_map/ppermute | solution.py:20
  631.8 201.7 %copy-start.10 = (f32[320,1600]{1,0:T(8,128)}, f32[320,1600]{1,0:T(8,128)S(1)}, u32[]{:S(2)}) copy-start(f32[320,1600]{1,0:T(8,128)S(1)} %get-tuple-element.1563) | copy-start | bytes 6144004
  631.8 201.7 %copy-start.77 = (f32[320]{0:T(512)}, f32[320]{0:T(512)S(1)}, u32[]{:S(2)}) copy-start(f32[320]{0:T(512)S(1)} %broadcast_multiply_fusion.4) | copy-start | bytes 3844
  632.2 201.3 %copy-start.79 = (f32[320]{0:T(512)}, f32[320]{0:T(512)S(1)}, u32[]{:S(2)}) copy-start(f32[320]{0:T(512)S(1)} %add_rsqrt_fusion) | copy-start | bytes 3844
  927.7 382.5 %collective-permute-start.20 = (bf16[320,25,64]{0,2,1:T(8,128)(2,1)}, bf16[320,25,64]{0,2,1:T(8,128)(2,1)S(1)}, u32[]{:S(2)}, u32[]{:S(2)}) collective-permute-start(bf16[320,25,64]{0,2,1:T(8,128)(2,1)} %get-tuple-element.866), channel_id=1, source_target_pairs={{7,0},{8,1},{9,2},{10,3},{11,4},{12,5},{13,6},{14,7},{15,8},{16,9}... | collective-permute-start | bytes 3072008 | tf_op jit(solution)/shard_map/ppermute | solution.py:20
  929.0 396.6 %collective-permute-start.27 = (bf16[320,25,64]{0,2,1:T(8,128)(2,1)S(1)}, bf16[320,25,64]{0,2,1:T(8,128)(2,1)S(1)}, u32[]{:S(2)}, u32[]{:S(2)}) collective-permute-start(bf16[320,25,64]{0,2,1:T(8,128)(2,1)S(1)} %get-tuple-element.874), channel_id=1, source_target_pairs={{7,0},{8,1},{9,2},{10,3},{11,4},{12,5},{13,6},{14,7},{15,8},{16,9}... | collective-permute-start | bytes 3072008 | tf_op jit(solution)/shard_map/ppermute | solution.py:20
  930.3 396.6 %collective-permute-start.19 = (bf16[320,25,64]{0,2,1:T(8,128)(2,1)}, bf16[320,25,64]{0,2,1:T(8,128)(2,1)S(1)}, u32[]{:S(2)}, u32[]{:S(2)}) collective-permute-start(bf16[320,25,64]{0,2,1:T(8,128)(2,1)} %get-tuple-element.865), channel_id=1, source_target_pairs={{6,0},{7,1},{8,2},{9,3},{10,4},{11,5},{12,6},{13,7},{14,8},{15,9},... | collective-permute-start | bytes 3072008 | tf_op jit(solution)/shard_map/ppermute | solution.py:20
  931.6 396.6 %collective-permute-start.26 = (bf16[320,25,64]{0,2,1:T(8,128)(2,1)}, bf16[320,25,64]{0,2,1:T(8,128)(2,1)S(1)}, u32[]{:S(2)}, u32[]{:S(2)}) collective-permute-start(bf16[320,25,64]{0,2,1:T(8,128)(2,1)} %get-tuple-element.873), channel_id=1, source_target_pairs={{6,0},{7,1},{8,2},{9,3},{10,4},{11,5},{12,6},{13,7},{14,8},{15,9},... | collective-permute-start | bytes 3072008 | tf_op jit(solution)/shard_map/ppermute | solution.py:20
  932.9 396.6 %collective-permute-start.18 = (bf16[320,25,64]{0,2,1:T(8,128)(2,1)}, bf16[320,25,64]{0,2,1:T(8,128)(2,1)S(1)}, u32[]{:S(2)}, u32[]{:S(2)}) collective-permute-start(bf16[320,25,64]{0,2,1:T(8,128)(2,1)} %copy-done.40), channel_id=1, source_target_pairs={{5,0},{6,1},{7,2},{8,3},{9,4},{10,5},{11,6},{12,7},{13,8},{14,9},{... | collective-permute-start | bytes 3072008 | tf_op jit(solution)/shard_map/ppermute | solution.py:20
  1310.3 47.0 %collective-permute-start.17 = (bf16[320,25,64]{0,2,1:T(8,128)(2,1)}, bf16[320,25,64]{0,2,1:T(8,128)(2,1)S(1)}, u32[]{:S(2)}, u32[]{:S(2)}) collective-permute-start(bf16[320,25,64]{0,2,1:T(8,128)(2,1)} %get-tuple-element.863), channel_id=1, source_target_pairs={{4,0},{5,1},{6,2},{7,3},{8,4},{9,5},{10,6},{11,7},{12,8},{13,9},{1... | collective-permute-start | bytes 3072008 | tf_op jit(solution)/shard_map/ppermute | solution.py:20
  1325.6 33.0 collective-permute-start.16
  1326.9 33.0 collective-permute-start.15
  1328.2 52.3 %collective-permute-start.14 = (bf16[320,25,64]{0,2,1:T(8,128)(2,1)}, bf16[320,25,64]{0,2,1:T(8,128)(2,1)S(1)}, u32[]{:S(2)}, u32[]{:S(2)}) collective-permute-start(bf16[320,25,64]{0,2,1:T(8,128)(2,1)} %get-tuple-element.860), channel_id=1, source_target_pairs={{1,0},{2,1},{3,2},{4,3},{5,4},{6,5},{7,6},{8,7},{9,8},{10,9},{11,1... | collective-permute-start | bytes 3072008 | tf_op jit(solution)/shard_map/ppermute | solution.py:20
  1329.5 56.6 %collective-permute-start.25 = (bf16[320,25,64]{0,2,1:T(8,128)(2,1)}, bf16[320,25,64]{0,2,1:T(8,128)(2,1)S(1)}, u32[]{:S(2)}, u32[]{:S(2)}) collective-permute-start(bf16[320,25,64]{0,2,1:T(8,128)(2,1)} %copy-done.39), channel_id=1, source_target_pairs={{5,0},{6,1},{7,2},{8,3},{9,4},{10,5},{11,6},{12,7},{13,8},{14,9},{... | collective-permute-start | bytes 3072008 | tf_op jit(solution)/shard_map/ppermute | solution.py:20
  1357.3 71.5 %collective-permute-start.24 = (bf16[320,25,64]{0,2,1:T(8,128)(2,1)}, bf16[320,25,64]{0,2,1:T(8,128)(2,1)S(1)}, u32[]{:S(2)}, u32[]{:S(2)}) collective-permute-start(bf16[320,25,64]{0,2,1:T(8,128)(2,1)} %get-tuple-element.871), channel_id=1, source_target_pairs={{4,0},{5,1},{6,2},{7,3},{8,4},{9,5},{10,6},{11,7},{12,8},{13,9},{1... | collective-permute-start | bytes 3072008 | tf_op jit(solution)/shard_map/ppermute | solution.py:20
  1358.6 70.2 %collective-permute-start.23 = (bf16[320,25,64]{0,2,1:T(8,128)(2,1)}, bf16[320,25,64]{0,2,1:T(8,128)(2,1)S(1)}, u32[]{:S(2)}, u32[]{:S(2)}) collective-permute-start(bf16[320,25,64]{0,2,1:T(8,128)(2,1)} %copy-done.37), channel_id=1, source_target_pairs={{3,0},{4,1},{5,2},{6,3},{7,4},{8,5},{9,6},{10,7},{11,8},{12,9},{13... | collective-permute-start | bytes 3072008 | tf_op jit(solution)/shard_map/ppermute | solution.py:20
  1359.9 68.9 %collective-permute-start.22 = (bf16[320,25,64]{0,2,1:T(8,128)(2,1)}, bf16[320,25,64]{0,2,1:T(8,128)(2,1)S(1)}, u32[]{:S(2)}, u32[]{:S(2)}) collective-permute-start(bf16[320,25,64]{0,2,1:T(8,128)(2,1)} %get-tuple-element.869), channel_id=1, source_target_pairs={{2,0},{3,1},{4,2},{5,3},{6,4},{7,5},{8,6},{9,7},{10,8},{11,9},{12,... | collective-permute-start | bytes 3072008 | tf_op jit(solution)/shard_map/ppermute | solution.py:20
  1380.5 48.2 %collective-permute-start.21 = (bf16[320,25,64]{0,2,1:T(8,128)(2,1)}, bf16[320,25,64]{0,2,1:T(8,128)(2,1)S(1)}, u32[]{:S(2)}, u32[]{:S(2)}) collective-permute-start(bf16[320,25,64]{0,2,1:T(8,128)(2,1)} %copy-done.36), channel_id=1, source_target_pairs={{1,0},{2,1},{3,2},{4,3},{5,4},{6,5},{7,6},{8,7},{9,8},{10,9},{11,1... | collective-permute-start | bytes 3072008 | tf_op jit(solution)/shard_map/ppermute | solution.py:20
  1494.7 1094.2 %reduce-scatter.11.cloned.1.call-start = ((), (), s32[]{:S(2)}) async-start(), calls=%async_computation.8 | async-start | bytes 54067200 | tf_op jit(solution)/shard_map/reduce_scatter | solution.py:304
  1576.6 1573.4 %reduce-scatter.9.cloned.1.call-start = ((), (), s32[]{:S(2)}) async-start(), calls=%async_computation.7 | async-start | bytes 54067200 | tf_op jit(solution)/shard_map/reduce_scatter | solution.py:303
  1676.0 1615.7 %all-reduce.3.cloned.1.call-start = ((), (), s32[]{:S(2)}) async-start(), calls=%async_computation.12 | async-start | bytes 188416 | tf_op jit(solution)/shard_map/psum | solution.py:306
  1698.1 1755.1 %reduce-scatter.7.cloned.1.call-start = ((), (), s32[]{:S(2)}) async-start(), calls=%async_computation.6 | async-start | bytes 13516800 | tf_op jit(solution)/shard_map/reduce_scatter | solution.py:302
  1726.8 236.3 %copy-start.89 = (f32[1600]{0:T(1024)S(1)}, f32[1600]{0:T(1024)}, u32[]{:S(2)}) copy-start(f32[1600]{0:T(1024)} %param.95) | copy-start | bytes 19204
  2037.9 1426.9 %copy-start.1 = (s32[4,13]{1,0:T(4,128)S(1)}, s32[4,13]{1,0:T(4,128)}, u32[]{:S(2)}) copy-start(s32[4,13]{1,0:T(4,128)} %param.97) | copy-start | bytes 628
  (79 other events, 2088.0 us)
Sparse Core Ops, SparseCore 0:
  10.9 115.7 all-gather.9
  129.5 68.8 all-gather.7
  201.3 260.6 all-gather.13
  464.8 204.1 all-gather.11
  1494.8 543.0 reduce-scatter.4
  2040.1 548.7 reduce-scatter.10
  2591.2 558.7 reduce-scatter.8
  3157.6 134.0 all-reduce.2
  3294.7 158.3 reduce-scatter.6
where the time goes:
time: 3490 us; the launch traced here: 3470 us
  waiting for transfers between devices  2160 us (62%)
  local copies, waits for them, and re-layouts  489 us (14%)
  starting transfers between devices  237 us (7%)
  matrix products  235 us (7%)
  blocking collectives  227 us (7%)
  loops' own time  65.7 us (2%)
  other arithmetic  45.7 us (1%)
    ppermute x28, waiting for transfers between devices, passed_along(): lax.ppermute(value, axis, [(source, source + steps) for source in range(l...  582 us
    reduce_scatter x1, waiting for transfers between devices, on_device(): lax.psum_scatter(fc_grad.reshape(-1, flat_cols), 'dev', scatter_dimension...  558 us
    reduce_scatter x1, waiting for transfers between devices, on_device(): lax.psum_scatter(proj_grad.reshape(-1, flat_cols), 'dev', scatter_dimensi...  548 us
    ppermute x28, starting transfers between devices, passed_along(): lax.ppermute(value, axis, [(source, source + steps) for source in range(l...  236 us
    pmax x1, blocking collectives, on_device(): logit_max = lax.pmax(jnp.max(run_max, axis=1), 'dev')  227 us
    reduce_scatter x1, waiting for transfers between devices, on_device(): lax.psum_scatter(out_grad.reshape(-1, flat_cols), 'dev', scatter_dimensio...  161 us
    psum x1, waiting for transfers between devices, on_device(): lax.psum((ln1_gain_grad, ln1_bias_grad, q_bias_grad, v_bias_grad, out_bia...  139 us
    all_gather x1, waiting for transfers between devices, fetch_weights(): lax.all_gather(w_qkv, 'dev', axis=0, tiled=True)  110 us
  transfers between devices with their start and end apart: 37, of which 15 were waited for; matrix products, arithmetic and copies ran while one was open for 14% of the time, Pallas kernels for 0%

commit v1 on v0

v1 whole, which is shorter than its diff:
```python
from functools import partial

import jax
import jax.numpy as jnp
from jax import lax
from jax.experimental import pallas as pl
from jax.experimental.pallas import tpu as pltpu
from jax.sharding import Mesh, PartitionSpec as P

HEAD_DIM = 64
TREE_TOK = 2560
GROUP = 8

EPS = 1e-05
TAU = 7.0
NEGATIVE = -1e30

BQ = 256
BK = 256
LANES = 128

TREE = "t"
PLANE = ("a", "b", "c")
EVERY = ("t", "a", "b", "c")
BF = jnp.bfloat16
F32 = jnp.float32


def norm_forward(values, norm_gain, norm_shift):
    row_mean = jnp.mean(values, axis=-1, keepdims=True)
    centered = values - row_mean
    inv_std = lax.rsqrt(jnp.mean(centered * centered, axis=-1, keepdims=True) + EPS)
    normed = centered * inv_std
    return (normed * norm_gain + norm_shift, normed, inv_std)


def norm_backward(upstream, normed, inv_std, norm_gain):
    scaled = upstream * norm_gain
    inner = (
        scaled
        - jnp.mean(scaled, axis=-1, keepdims=True)
        - normed * jnp.mean(scaled * normed, axis=-1, keepdims=True)
    )
    return (inner * inv_std, jnp.sum(upstream * normed, axis=0), jnp.sum(upstream, axis=0))


def swap(value, axis):
    return lax.ppermute(value, axis, [(0, 1), (1, 0)])


def plane_gather(own):
    half = own.shape[0] // 2
    from_b, from_a = swap(own, "b"), swap(own, "a")
    diag = jnp.concatenate([swap(from_b[:half], "a"), swap(from_a[half:], "b")], axis=0)
    same = [own, from_b, from_a, diag]
    other = [swap(block, "c") for block in same]
    return [block for pair in zip(same, other) for block in pair]


def plane_scatter(part):
    sums = []
    for r in (6, 2, 4, 0):
        sums.append(part(r).astype(F32) + swap(part(r + 1), "c").astype(F32))
    diag, for_b, for_a, mine = sums
    half = diag.shape[0] // 2
    diag_low = diag.astype(BF)
    top = swap(diag_low[:half], "b")
    bottom = swap(diag_low[half:], "a")
    for_a = jnp.concatenate([for_a[:half] + top.astype(F32), for_a[half:]], axis=0)
    for_b = jnp.concatenate([for_b[:half], for_b[half:] + bottom.astype(F32)], axis=0)
    return (
        mine
        + swap(for_b.astype(BF), "b").astype(F32)
        + swap(for_a.astype(BF), "a").astype(F32)
    )


def block_of(array, index, rows):
    return lax.dynamic_slice_in_dim(array, index * rows, rows, 0)


def xor_order(array, place, rows):
    return jnp.concatenate([block_of(array, place ^ r, rows) for r in range(GROUP)], axis=0)


def tree_tables(lengths, parent_row):
    count = lengths.shape[0]
    numbers = jnp.arange(count, dtype=jnp.int32)
    ends = jnp.sum(jnp.where(numbers[None, :] <= numbers[:, None], lengths[None, :], 0), axis=1)
    starts = ends - lengths
    reach = (
        (numbers[:, None] == numbers[None, :]) | (parent_row[:, None] == numbers[None, :])
    ).astype(F32)
    hops = 1
    while hops < count:
        reach = (
            jnp.sum(reach[:, :, None] * reach[None, :, :], axis=1) > 0.5
        ).astype(F32)
        hops *= 2
    return starts, ends, reach


def block_lists(hot, path, q_blocks, k_blocks):
    q_has = jnp.max(path.reshape(q_blocks, -1, path.shape[1]), axis=1)
    k_has = jnp.max(hot.reshape(k_blocks, -1, hot.shape[1]), axis=1)
    live = jnp.sum(q_has[:, None, :] * k_has[None, :, :], axis=2) > 0.5
    q_first = jnp.arange(q_blocks, dtype=jnp.int32) * (BQ // BK)
    keys = jnp.arange(k_blocks, dtype=jnp.int32)
    live = (live & (keys[None, :] < q_first[:, None])).astype(jnp.int32)
    rank = jnp.sum(
        jnp.where(keys[None, :, None] > keys[None, None, :], live[:, None, :], 0), axis=2
    )
    listed = jnp.sum(
        jnp.where(
            (rank[:, :, None] == keys[None, None, :]) & (live[:, :, None] > 0),
            keys[None, :, None],
            0,
        ),
        axis=1,
    )
    return jnp.sum(live, axis=1).astype(jnp.int32), listed.astype(jnp.int32)


def score_block(kx, qx):
    return lax.dot_general(kx, qx, (((1,), (1,)), ((), ())), preferred_element_type=F32)


def causal(key_first, query_first):
    keys = key_first + lax.broadcasted_iota(jnp.int32, (BK, BQ), 0)
    queries = query_first + lax.broadcasted_iota(jnp.int32, (BK, BQ), 1)
    return keys <= queries


def attend_kernel(count, listed, owned, qx, kx, vt, out, out_wide, lse, top, m_s, l_s, acc_s):
    step = pl.program_id(0)
    q_first = step * BQ
    per = BQ // BK

    @pl.when(step == 0)
    def _():
        top[...] = jnp.full(top.shape, NEGATIVE, F32)

    def one(h, kb, diagonal):
        rows = pl.ds(pl.multiple_of(kb * BK, BK), BK)
        score = score_block(kx[h, rows, :], qx[h])
        if diagonal:
            score = jnp.where(causal(kb * BK, q_first), score, NEGATIVE)
        old = m_s[h : h + 1, :]
        new = jnp.maximum(old, jnp.max(score, axis=0, keepdims=True))
        weight = jnp.exp(score - new)
        shrink = jnp.exp(old - new)
        m_s[h : h + 1, :] = new
        l_s[h : h + 1, :] = l_s[h : h + 1, :] * shrink + jnp.sum(weight, axis=0, keepdims=True)
        acc_s[h] = acc_s[h] * shrink + jnp.dot(
            vt[h, :, rows], weight.astype(BF), preferred_element_type=F32
        )

    def heads(group):
        for h in group:
            m_s[h : h + 1, :] = jnp.full((1, BQ), NEGATIVE, F32)
            l_s[h : h + 1, :] = jnp.zeros((1, BQ), F32)
            acc_s[h] = jnp.zeros((HEAD_DIM, BQ), F32)
        for d in range(per):
            for h in group:
                one(h, step * per + d, True)

        def body(i, carry):
            for h in group:
                one(h, listed[step, i], False)
            return carry

        lax.fori_loop(0, count[step], body, 0)
        for h in group:
            total = l_s[h : h + 1, :]
            wide = acc_s[h] / total
            out_wide[h] = wide
            lse[h : h + 1, :] = m_s[h : h + 1, :] + jnp.log(total)
            top[h : h + 1, :] = jnp.maximum(top[h : h + 1, :], m_s[h : h + 1, :])

    last = acc_s.shape[0] - 1
    heads(range(last))

    @pl.when(owned[step] > 0)
    def _():
        heads([last])

    @pl.when(owned[step] == 0)
    def _():
        out_wide[last] = jnp.zeros((HEAD_DIM, BQ), F32)
        lse[last : last + 1, :] = jnp.zeros((1, BQ), F32)

    for h in range(last + 1):
        out[:, h * HEAD_DIM : (h + 1) * HEAD_DIM] = out_wide[h].T.astype(BF)


def attend(count, listed, owned, qx, kx, vt):
    heads, tokens, width = qx.shape
    steps = tokens // BQ
    spec = lambda shape, index: pl.BlockSpec(shape, index)
    whole = lambda shape: pl.BlockSpec(shape, lambda i, *_: (0,) * len(shape))
    return pl.pallas_call(
        attend_kernel,
        grid_spec=pltpu.PrefetchScalarGridSpec(
            num_scalar_prefetch=3,
            grid=(steps,),
            in_specs=[
                spec((heads, BQ, width), lambda i, *_: (0, i, 0)),
                whole(kx.shape),
                whole(vt.shape),
            ],
            out_specs=[
                spec((BQ, heads * HEAD_DIM), lambda i, *_: (i, 0)),
                spec((heads, HEAD_DIM, BQ), lambda i, *_: (0, 0, i)),
                spec((heads, BQ), lambda i, *_: (0, i)),
                whole((heads, BQ)),
            ],
            scratch_shapes=[
                pltpu.VMEM((heads, BQ), F32),
                pltpu.VMEM((heads, BQ), F32),
                pltpu.VMEM((heads, HEAD_DIM, BQ), F32),
            ],
        ),
        out_shape=[
            jax.ShapeDtypeStruct((tokens, heads * HEAD_DIM), BF),
            jax.ShapeDtypeStruct((heads, HEAD_DIM, tokens), F32),
            jax.ShapeDtypeStruct((heads, tokens), F32),
            jax.ShapeDtypeStruct((heads, BQ), F32),
        ],
        compiler_params=pltpu.CompilerParams(
            dimension_semantics=("arbitrary",), vmem_limit_bytes=48 << 20
        ),
        cost_estimate=pl.CostEstimate(
            flops=heads * tokens * tokens * HEAD_DIM * 4,
            bytes_accessed=heads * tokens * 1024,
            transcendentals=heads * tokens * tokens // 2,
        ),
        name="attend",
    )(count, listed, owned, qx, kx, vt)


def attend_back_kernel(
    count, listed, owned, qx, kx, kt, vs, up, out_wide, lse, grads, dk_s, dv_s, dq_s
):
    step = pl.program_id(0)
    q_first = step * BQ
    per = BQ // BK
    heads_all = dq_s.shape[0]
    last = heads_all - 1
    width = heads_all * HEAD_DIM

    @pl.when(step == 0)
    def _():
        dk_s[...] = jnp.zeros(dk_s.shape, F32)
        dv_s[...] = jnp.zeros(dv_s.shape, F32)

    def heads(group):
        parts = {}
        for h in group:
            rows_up = up[:, h * HEAD_DIM : (h + 1) * HEAD_DIM]
            cols_up = rows_up.astype(F32).T
            delta = jnp.sum(out_wide[h] * cols_up, axis=0, keepdims=True)
            parts[h] = (rows_up, cols_up.astype(BF), delta, lse[h : h + 1, :])
            dq_s[h] = jnp.zeros((HEAD_DIM, BQ), F32)

        def one(h, kb, diagonal):
            rows_up, cols_up, delta, norm = parts[h]
            rows = pl.ds(pl.multiple_of(kb * BK, BK), BK)
            score = score_block(kx[h, rows, :], qx[h])
            probs = jnp.exp(score - norm)
            if diagonal:
                probs = jnp.where(causal(kb * BK, q_first), probs, 0.0)
            dprobs = jnp.dot(vs[h, rows, :], cols_up, preferred_element_type=F32)
            dscore = (probs * (dprobs - delta)).astype(BF)
            dv_s[h, rows, :] += jnp.dot(probs.astype(BF), rows_up, preferred_element_type=F32)
            dk_s[h, rows, :] += jnp.dot(
                dscore, qx[h][:, :HEAD_DIM], preferred_element_type=F32
            )
            dq_s[h] += jnp.dot(kt[h, :, rows], dscore, preferred_element_type=F32)

        for d in range(per):
            for h in group:
                one(h, step * per + d, True)

        def body(i, carry):
            for h in group:
                one(h, listed[step, i], False)
            return carry

        lax.fori_loop(0, count[step], body, 0)

    heads(range(last))

    @pl.when(owned[step] > 0)
    def _():
        heads([last])

    @pl.when(owned[step] == 0)
    def _():
        dq_s[last] = jnp.zeros((HEAD_DIM, BQ), F32)

    here = pl.ds(pl.multiple_of(q_first, BQ), BQ)
    for h in range(heads_all):
        grads[here, h * HEAD_DIM : (h + 1) * HEAD_DIM] = (
            dq_s[h] * (HEAD_DIM ** (-0.5))
        ).T.astype(BF)

    @pl.when(step == pl.num_programs(0) - 1)
    def _():
        for h in range(heads_all):
            at = width + h * HEAD_DIM
            grads[:, at : at + HEAD_DIM] = dk_s[h].astype(BF)
            at = 2 * width + h * HEAD_DIM
            grads[:, at : at + HEAD_DIM] = dv_s[h].astype(BF)


def attend_back(count, listed, owned, qx, kx, kt, vs, up, out_wide, lse):
    heads, tokens, width = qx.shape
    steps = tokens // BQ
    spec = lambda shape, index: pl.BlockSpec(shape, index)
    whole = lambda shape: pl.BlockSpec(shape, lambda i, *_: (0,) * len(shape))
    return pl.pallas_call(
        attend_back_kernel,
        grid_spec=pltpu.PrefetchScalarGridSpec(
            num_scalar_prefetch=3,
            grid=(steps,),
            in_specs=[
                spec((heads, BQ, width), lambda i, *_: (0, i, 0)),
                whole(kx.shape),
                whole(kt.shape),
                whole(vs.shape),
                spec((BQ, heads * HEAD_DIM), lambda i, *_: (i, 0)),
                spec((heads, HEAD_DIM, BQ), lambda i, *_: (0, 0, i)),
                spec((heads, BQ), lambda i, *_: (0, i)),
            ],
            out_specs=whole((tokens, 3 * heads * HEAD_DIM)),
            scratch_shapes=[
                pltpu.VMEM((heads, tokens, HEAD_DIM), F32),
                pltpu.VMEM((heads, tokens, HEAD_DIM), F32),
                pltpu.VMEM((heads, HEAD_DIM, BQ), F32),
            ],
        ),
        out_shape=jax.ShapeDtypeStruct((tokens, 3 * heads * HEAD_DIM), BF),
        compiler_params=pltpu.CompilerParams(
            dimension_semantics=("arbitrary",), vmem_limit_bytes=52 << 20
        ),
        cost_estimate=pl.CostEstimate(
            flops=heads * tokens * tokens * HEAD_DIM * 10,
            bytes_accessed=heads * tokens * 2048,
            transcendentals=heads * tokens * tokens // 2,
        ),
        name="attend_back",
    )(count, listed, owned, qx, kx, kt, vs, up, out_wide, lse)


def head_split(matrix, parts):
    rows, cols = matrix.shape
    heads = cols // (parts * HEAD_DIM)
    each = heads // GROUP
    cube = matrix.reshape(rows, parts, heads, HEAD_DIM)
    own = cube[:, :, : each * GROUP].reshape(rows, parts, GROUP, each, HEAD_DIM)
    rest = jnp.broadcast_to(
        cube[:, :, None, each * GROUP :], (rows, parts, GROUP, heads - each * GROUP, HEAD_DIM)
    )
    joined = jnp.concatenate([own, rest], axis=3)
    return jnp.transpose(joined, (2, 0, 1, 3, 4)).reshape(GROUP, rows, -1)


def head_join(shares, parts, heads):
    group, rows, _ = shares.shape
    each = heads // GROUP
    cube = shares.astype(F32).reshape(group, rows, parts, -1, HEAD_DIM)
    own = jnp.transpose(cube[:, :, :, :each], (1, 2, 0, 3, 4)).reshape(
        rows, parts, each * GROUP, HEAD_DIM
    )
    rest = jnp.sum(cube[:, :, :, each:], axis=0)
    return jnp.concatenate([own, rest], axis=2).reshape(rows, -1)


def hidden_split(matrix, unit):
    rows = matrix.shape[0]
    cube = matrix.reshape(rows, -1, GROUP, unit)
    return jnp.transpose(cube, (2, 0, 1, 3)).reshape(GROUP, rows, -1)


def hidden_join(shares, unit):
    group, rows, _ = shares.shape
    cube = shares.reshape(group, rows, -1, unit)
    return jnp.transpose(cube, (1, 2, 0, 3)).reshape(rows, -1)


def exchange(shares):
    return lax.all_to_all(shares, PLANE, split_axis=0, concat_axis=0, tiled=True)


def take(stack, place):
    return lax.dynamic_index_in_dim(stack, place, 0, keepdims=False)


def columns_in(shard, width, split, place):
    if shard.size % width == 0:
        mine = exchange(split(shard.reshape(-1, width)))
        rows = mine.reshape(-1, mine.shape[-1])
        return lax.all_gather(rows, TREE, axis=0, tiled=True)
    full = lax.all_gather(shard, EVERY, axis=0, tiled=True).reshape(-1, width)
    return take(split(full), place)


def columns_out(grad, join, shard_shape, width, place):
    size = shard_shape[0] * shard_shape[1]
    if size % width == 0:
        rows = lax.psum_scatter(grad.astype(BF), TREE, scatter_dimension=0, tiled=True)
        shares = exchange(rows.reshape(GROUP, -1, rows.shape[-1]))
        return join(shares).astype(F32).reshape(shard_shape)
    spots = jnp.arange(GROUP, dtype=jnp.int32)[:, None, None] == place
    shares = jnp.where(spots, grad.astype(BF)[None], jnp.zeros((), BF))
    full = join(shares).astype(BF).reshape(-1, shard_shape[1])
    return lax.psum_scatter(full, EVERY, scatter_dimension=0, tiled=True).astype(F32)


def on_device(
    tokens,
    cotangent,
    w_qkv,
    w_out,
    w_fc,
    w_proj,
    ln1_gain,
    ln1_bias,
    q_bias,
    v_bias,
    out_bias,
    ln2_gain,
    ln2_bias,
    fc_bias,
    proj_bias,
    seg_lengths,
    parents,
):
    tok_dev, model_width = tokens.shape
    hidden = fc_bias.shape[0]
    flat_cols = w_qkv.shape[1]
    heads = model_width // HEAD_DIM
    each = heads // GROUP
    rest = heads - each * GROUP
    local = each + rest
    tree = lax.axis_index(TREE)
    place = (lax.axis_index("a") * 2 + lax.axis_index("b")) * 2 + lax.axis_index("c")
    device = tree * GROUP + place
    unit = max(1, hidden // lax.axis_size(EVERY))

    starts, ends, reach = tree_tables(take(seg_lengths, tree), take(parents, tree))
    position = jnp.arange(TREE_TOK, dtype=jnp.int32)
    hot = (
        (position[:, None] >= starts[None, :]) & (position[:, None] < ends[None, :])
    ).astype(F32)
    path = jnp.dot(hot, reach, preferred_element_type=F32)
    q_blocks, k_blocks = TREE_TOK // BQ, TREE_TOK // BK
    count, listed = block_lists(hot, path, q_blocks, k_blocks)
    block_numbers = jnp.arange(q_blocks, dtype=jnp.int32)
    turn = q_blocks - 1 - block_numbers
    owner = jnp.where(turn < GROUP, turn, 2 * GROUP - 2 - turn)
    owned = (owner == place).astype(jnp.int32)
    pad = LANES - HEAD_DIM - hot.shape[1]
    key_mark = jnp.pad(hot, ((0, 0), (0, pad))).astype(BF)
    query_mark = jnp.pad((1.0 - path) * NEGATIVE, ((0, 0), (0, pad))).astype(BF)

    w_qkv_l = columns_in(w_qkv, 3 * model_width, partial(head_split, parts=3), place)
    w_out_full = lax.all_gather(w_out, EVERY, axis=0, tiled=True).reshape(model_width, model_width)
    w_out_l = jnp.concatenate(
        [block_of(w_out_full, place, each * HEAD_DIM), w_out_full[each * GROUP * HEAD_DIM :]], axis=0
    )
    w_fc_l = columns_in(w_fc, hidden, partial(hidden_split, unit=unit), place)
    proj_whole = w_proj.size % model_width == 0
    if proj_whole:
        w_proj_l = lax.all_gather(w_proj.reshape(-1, model_width), TREE, axis=0, tiled=True)
    fc_bias_l = take(hidden_split(fc_bias[None], unit), place)[0]
    qkv_bias = jnp.concatenate([q_bias, jnp.zeros_like(q_bias), v_bias])
    qkv_bias_l = take(head_split(qkv_bias[None], 3), place)[0]

    residual_in = tokens.astype(F32)
    first_norm, normed_one, inv_one = norm_forward(residual_in, ln1_gain, ln1_bias)
    first_low = jnp.concatenate(plane_gather(first_norm.astype(BF)), axis=0)
    projected = (jnp.dot(first_low, w_qkv_l, preferred_element_type=F32) + qkv_bias_l).astype(BF)
    projected = xor_order(projected, place, tok_dev)
    cube = projected.reshape(TREE_TOK, 3, local, HEAD_DIM)
    score_scale = jnp.asarray(HEAD_DIM ** (-0.5), BF)
    marks = lambda mark: jnp.broadcast_to(mark[None], (local,) + mark.shape)
    qx = jnp.concatenate(
        [jnp.transpose(cube[:, 0], (1, 0, 2)) * score_scale, marks(query_mark)], axis=2
    )
    kx = jnp.concatenate([jnp.transpose(cube[:, 1], (1, 0, 2)), marks(key_mark)], axis=2)
    kt = jnp.transpose(cube[:, 1], (1, 2, 0))
    vs = jnp.transpose(cube[:, 2], (1, 0, 2))
    vt = jnp.transpose(cube[:, 2], (1, 2, 0))

    attended, out_wide, lse, tops = attend(count, listed, owned, qx, kx, vt)
    top_heads = jnp.max(tops, axis=1)
    spread = jnp.full((GROUP, each), NEGATIVE, F32)
    spread = lax.dynamic_update_slice(spread, top_heads[None, :each], (place, 0))
    logit_max = lax.pmax(jnp.concatenate([spread.reshape(-1), top_heads[each:]]), EVERY)

    attended = xor_order(attended, place, tok_dev)
    branch = jnp.dot(attended, w_out_l, preferred_element_type=F32).astype(BF)
    rows_of = lambda array: lambda r: array[r * tok_dev : (r + 1) * tok_dev]
    middle = residual_in + plane_scatter(rows_of(branch)) + out_bias

    second_norm, normed_two, inv_two = norm_forward(middle, ln2_gain, ln2_bias)
    second_low = jnp.concatenate(plane_gather(second_norm.astype(BF)), axis=0)
    grad_two = jnp.concatenate(plane_gather(cotangent), axis=0)
    if not proj_whole:
        proj_full = lax.all_gather(w_proj, EVERY, axis=0, tiled=True).reshape(hidden, model_width)
        w_proj_l = take(
            jnp.transpose(proj_full.reshape(-1, GROUP, unit, model_width), (1, 0, 2, 3)), place
        ).reshape(-1, model_width)
    pre_act = jnp.dot(second_low, w_fc_l, preferred_element_type=F32) + fc_bias_l
    activated, gelu_pull = jax.vjp(partial(jax.nn.gelu, approximate=True), pre_act)
    act_low = activated.astype(BF)
    branch_two = jnp.dot(act_low, w_proj_l, preferred_element_type=F32).astype(BF)
    output = (middle + plane_scatter(rows_of(branch_two)) + proj_bias).astype(BF)

    act_back = lax.dot_general(
        grad_two, w_proj_l, (((1,), (1,)), ((), ())), preferred_element_type=F32
    )
    pre_low = gelu_pull(act_back)[0].astype(BF)
    norm_back = lax.dot_general(
        pre_low, w_fc_l, (((1,), (1,)), ((), ())), preferred_element_type=F32
    ).astype(BF)
    over_rows = lambda left, right: lax.dot_general(
        left, right, (((0,), (0,)), ((), ())), preferred_element_type=F32
    )
    proj_grad = over_rows(act_low, grad_two)
    fc_grad = over_rows(second_low, pre_low)
    fc_bias_part = jnp.sum(pre_low.astype(F32), axis=0)

    grad_out = cotangent.astype(F32)
    proj_bias_grad = jnp.sum(grad_out, axis=0)
    mid_part, ln2_gain_grad, ln2_bias_grad = norm_backward(
        plane_scatter(rows_of(norm_back)), normed_two, inv_two, ln2_gain
    )
    middle_grad = grad_out + mid_part
    branch_own = middle_grad.astype(BF)
    out_bias_grad = jnp.sum(branch_own.astype(F32), axis=0)
    branch_low = jnp.concatenate(plane_gather(branch_own), axis=0)
    attn_back = lax.dot_general(
        branch_low, w_out_l, (((1,), (1,)), ((), ())), preferred_element_type=F32
    ).astype(BF)
    out_grad = over_rows(attended, branch_low)

    qkv_low = attend_back(
        count, listed, owned, qx, kx, kt, vs, xor_order(attn_back, place, tok_dev), out_wide, lse
    )
    qkv_low = xor_order(qkv_low, place, tok_dev)
    first_back = lax.dot_general(
        qkv_low, w_qkv_l, (((1,), (1,)), ((), ())), preferred_element_type=F32
    ).astype(BF)
    qkv_grad = over_rows(first_low, qkv_low)
    in_part, ln1_gain_grad, ln1_bias_grad = norm_backward(
        plane_scatter(rows_of(first_back)), normed_one, inv_one, ln1_gain
    )
    input_grad = middle_grad + in_part

    qkv_shard = columns_out(
        qkv_grad, partial(head_join, parts=3, heads=heads), w_qkv.shape, 3 * model_width, place
    )
    fc_shard = columns_out(fc_grad, partial(hidden_join, unit=unit), w_fc.shape, hidden, place)
    out_zero = jnp.zeros((each * GROUP * HEAD_DIM, model_width), BF)
    out_low = out_grad.astype(BF)
    out_rows = jnp.concatenate(
        [
            lax.dynamic_update_slice(
                out_zero, out_low[: each * HEAD_DIM], (place * each * HEAD_DIM, 0)
            ),
            out_low[each * HEAD_DIM :],
        ],
        axis=0,
    )
    out_shard = lax.psum_scatter(
        out_rows.reshape(-1, flat_cols), EVERY, scatter_dimension=0, tiled=True
    ).astype(F32)
    if proj_whole:
        proj_shard = (
            lax.psum_scatter(proj_grad.astype(BF), TREE, scatter_dimension=0, tiled=True)
            .astype(F32)
            .reshape(w_proj.shape)
        )
    else:
        spots = jnp.arange(GROUP, dtype=jnp.int32)[None, :, None, None] == place
        proj_rows = jnp.where(
            spots, proj_grad.astype(BF).reshape(-1, 1, unit, model_width), jnp.zeros((), BF)
        ).reshape(-1, flat_cols)
        proj_shard = lax.psum_scatter(proj_rows, EVERY, scatter_dimension=0, tiled=True).astype(F32)

    column_sums = jnp.sum(qkv_low.astype(F32), axis=0).reshape(3, local, HEAD_DIM)
    bias_parts = jnp.zeros((3, GROUP, each, HEAD_DIM), F32)
    bias_parts = lax.dynamic_update_slice(
        bias_parts, column_sums[:, None, :each], (0, place, 0, 0)
    )
    bias_parts = jnp.concatenate(
        [bias_parts.reshape(3, each * GROUP, HEAD_DIM), column_sums[:, each:]], axis=1
    ).reshape(3, model_width)
    fc_parts = jnp.zeros((GROUP, hidden // GROUP), F32)
    fc_parts = lax.dynamic_update_slice(fc_parts, fc_bias_part[None], (place, 0))
    fc_parts = hidden_join(fc_parts[:, None], unit)[0]
    small = lax.psum(
        (
            ln1_gain_grad,
            ln1_bias_grad,
            bias_parts[0],
            bias_parts[2],
            out_bias_grad,
            ln2_gain_grad,
            ln2_bias_grad,
            fc_parts,
            proj_bias_grad,
        ),
        EVERY,
    )

    clip_gain = jnp.sqrt(TAU / jnp.maximum(logit_max, TAU))
    rows_dev = w_qkv.shape[0]
    flat_index = (device * rows_dev + jnp.arange(rows_dev, dtype=jnp.int32)[:, None]) * flat_cols
    flat_index = flat_index + jnp.arange(flat_cols, dtype=jnp.int32)[None, :]
    column = flat_index % (3 * model_width)
    head_of = column % model_width // HEAD_DIM
    head_numbers = jnp.arange(heads, dtype=jnp.int32)
    head_gain = jnp.sum(
        jnp.where(
            head_of[:, :, None] == head_numbers[None, None, :], clip_gain[None, None, :], 0.0
        ),
        axis=2,
    )
    factor = jnp.where(column < 2 * model_width, head_gain, 1.0)
    clipped = (w_qkv.astype(F32) * factor).astype(BF)
    return (
        output,
        input_grad,
        qkv_shard,
        out_shard,
        fc_shard,
        proj_shard,
        *small,
        logit_max,
        clipped,
    )


def solution(mesh):
    split = Mesh(mesh.devices.reshape(-1, 2, 2, 2), EVERY)
    rows = P(EVERY, None)
    return jax.shard_map(
        on_device,
        mesh=split,
        in_specs=(rows,) * 6 + (P(),) * 11,
        out_specs=(rows,) * 6 + (P(),) * 10 + (rows,),
        check_vma=False,
    )
```

time: 3490 us -> 1000 us (0.29)
  waiting for transfers between devices: 2160 us -> 369 us
  local copies, waits for them, and re-layouts: 489 us -> 186 us
  starting transfers between devices: 237 us -> 53.3 us
  blocking collectives: 227 us -> 71.1 us
  matrix products: 235 us -> 129 us
  Pallas kernels: 0 us -> 102 us
  loops' own time: 65.7 us -> 0 us
    reduce_scatter x4 -> x3, waiting for transfers between devices: 1320 us -> 0.02 us  [the longest x2 0.02 us: columns_out(): lax.psum_scatter(grad.astype(BF), TREE, scatter_dimension=0, tiled=True)]
    ppermute x28 -> x64, waiting for transfers between devices: 582 us -> 207 us  [swap(): return lax.ppermute(value, axis, [(0, 1), (1, 0)])]
    reshape x8 -> x19, local copies, waits for them, and re-layouts: 333 us -> 44.7 us  [the longest x1 14.3 us: on_device(): out_rows.reshape(-1, flat_cols)]
    ppermute x28 -> x64, starting transfers between devices: 236 us -> 39.7 us  [swap(): return lax.ppermute(value, axis, [(0, 1), (1, 0)])]
    pmax x1, blocking collectives: 227 us -> 54.5 us  [on_device(): lax.pmax(jnp.concatenate([spread.reshape(-1), top_heads[each:]]), EVERY)]
    all_gather x4, waiting for transfers between devices: 110 us -> 0.03 us  [the longest x1 0.02 us: on_device(): lax.all_gather(w_out, EVERY, axis=0, tiled=True)]
    dot_general x30 -> x13, matrix products: 235 us -> 129 us  [the longest x4 41.7 us: on_device(): lax.dot_general(left, right, (((0,), (0,)), ((), ())), preferred_element_...]
    pallas_call x0 -> x2, Pallas kernels: none -> 102 us  [the longest x1 51.4 us: attend_back(): pl.pallas_call(attend_back_kernel, grid_spec=pltpu.PrefetchScalarGridSpec...]
  transfers between devices with their start and end apart: 37 -> 76, of which waited for: 15 -> 31; matrix products, arithmetic and copies ran while one was open for 14% -> 33% of each run, Pallas kernels for 0% -> 10%
where the time goes in v1:
time: 1000 us; the launch traced here: 997 us
  waiting for transfers between devices  369 us (37%)
  local copies, waits for them, and re-layouts  186 us (19%)
  matrix products  129 us (13%)
  Pallas kernels  102 us (10%)
  other arithmetic  71.3 us (7%)
  blocking collectives  71.1 us (7%)
  starting transfers between devices  53.3 us (5%)
  between operations  16 us (2%)
    ppermute x64, waiting for transfers between devices, swap(): return lax.ppermute(value, axis, [(0, 1), (1, 0)])  207 us
    psum x1, waiting for transfers between devices, on_device(): lax.psum((ln1_gain_grad, ln1_bias_grad, bias_parts[0], bias_parts[2], out...  101 us
    unnamed x173, local copies, waits for them, and re-layouts  87.1 us
    all_to_all x3, waiting for transfers between devices, exchange(): lax.all_to_all(shares, PLANE, split_axis=0, concat_axis=0, tiled=True)  59.8 us
    pmax x1, blocking collectives, on_device(): lax.pmax(jnp.concatenate([spread.reshape(-1), top_heads[each:]]), EVERY)  54.5 us
    pallas_call x1, Pallas kernels, attend_back(): pl.pallas_call(attend_back_kernel, grid_spec=pltpu.PrefetchScalarGridSpec...  51.4 us
    pallas_call x1, Pallas kernels, attend(): pl.pallas_call(attend_kernel, grid_spec=pltpu.PrefetchScalarGridSpec(num_...  50.2 us
    dot_general x4, matrix products, on_device(): lax.dot_general(left, right, (((0,), (0,)), ((), ())), preferred_element_...  41.7 us
  transfers between devices with their start and end apart: 76, of which 31 were waited for; matrix products, arithmetic and copies ran while one was open for 33% of the time, Pallas kernels for 10%

profile of v1, /device:TPU:0, one launch (start us, length us, event | category | flops | bytes accessed | tf_op | source)
XLA Modules:
  0.0 997.0 jit_solution(9375592754361229543)
XLA Ops:
  13.4 16.6 %all_to_all.20 = bf16[8,50,768]{2,1,0:T(8,128)(2,1)S(1)} all-to-all(bf16[8,50,768]{2,1,0:T(8,128)(2,1)S(1)} %reshape.433), channel_id=1, replica_groups=mesh['t'=4,'a'=2,'b'=2,'c'=2] {'a','b','c'}, dimensions={0} | all-to-all | bytes 1228800 | tf_op jit(solution)/shard_map/all_to_all | solution.py:392
  38.1 3.7 all-to-all-start.1
  45.7 16.0 %collective-permute-done.1 = bf16[320,1600]{1,0:T(8,128)(2,1)} collective-permute-done((bf16[320,1600]{1,0:T(8,128)(2,1)}, bf16[320,1600]{1,0:T(8,128)(2,1)}, u32[]{:S(2)}, u32[]{:S(2)}) %collective-permute-start.1) | collective-permute-done | bytes 1024032 | tf_op jit(solution)/shard_map/ppermute | solution.py:48
  62.5 7.0 all-to-all-done.1
  79.2 4.4 collective-permute-done.6
  92.2 10.6 %add_convert_fusion = bf16[2560,768]{1,0:T(8,128)(2,1)S(1)} fusion(bf16[2560,1600]{1,0:T(8,128)(2,1)} %constant_dynamic-update-slice_fusion, bf16[1600,768]{1,0:T(8,128)(2,1)} %all-gather.5.cloned.1.call-done, f32[768]{0:T(1024)S(1)} %fusion.50), kind=kOutput, calls=%fused_computation.18 | convolution fusion | flops 6295388160 | bytes 14584832 | tf_op jit(solution)/shard_map/dot_general | solution.py:483
  109.5 6.5 copy.424
  116.0 4.2 fusion.67
  122.0 4.4 copy.428.kx
  126.4 3.8 copy.462
  135.6 50.2 %attend.1 = (bf16[2560,256]{1,0:T(8,128)(2,1)S(1)}, f32[4,64,2560]{2,1,0:T(8,128)S(1)}, f32[4,2560]{1,0:T(4,128)S(1)}, f32[4,256]{1,0:T(4,128)S(1)}) custom-call(s32[10]{0:T(128)S(1)} %fusion.57.count, s32[10,10]{1,0:T(8,128)S(1)} %select_reduce_fusion.1.listed, s32[10]{0:T(128)S(1)} %compare_convert_fusion.3.owned, ...), custom_call_target="tpu_custom_call" | custom-call | flops 6710886400 | bytes 10485760 | tf_op jit(solution)/shard_map/attend/pallas_call | solution.py:201
  189.0 12.1 %reshape.411 = bf16[1600,1600]{1,0:T(8,128)(2,1)} reshape(bf16[12800,200]{1,0:T(8,128)(2,1)} %all-gather.7.cloned.1.call-done) | data formatting | bytes 10240000 | tf_op jit(solution)/shard_map/reshape | solution.py:468
  227.4 3.0 collective-permute-done.14
  232.1 22.6 %collective-permute-done.11 = bf16[160,1600]{1,0:T(8,128)(2,1)S(1)} collective-permute-done((bf16[160,1600]{1,0:T(8,128)(2,1)}, bf16[160,1600]{1,0:T(8,128)(2,1)S(1)}, u32[]{:S(2)}, u32[]{:S(2)}) %collective-permute-start.11) | collective-permute-done | bytes 512032 | tf_op jit(solution)/shard_map/ppermute | solution.py:48
  265.5 25.8 %collective-permute-done.37 = bf16[160,1600]{1,0:T(8,128)(2,1)S(1)} collective-permute-done((bf16[160,1600]{1,0:T(8,128)(2,1)S(1)}, bf16[160,1600]{1,0:T(8,128)(2,1)S(1)}, u32[]{:S(2)}, u32[]{:S(2)}) %collective-permute-start.37) | collective-permute-done | bytes 512032 | tf_op jit(solution)/shard_map/ppermute | solution.py:48
  301.3 21.0 %collective-permute-done.17 = bf16[320,1600]{1,0:T(8,128)(2,1)S(1)} collective-permute-done((bf16[320,1600]{1,0:T(8,128)(2,1)S(1)}, bf16[320,1600]{1,0:T(8,128)(2,1)S(1)}, u32[]{:S(2)}, u32[]{:S(2)}) %collective-permute-start.17) | collective-permute-done | bytes 1024032 | tf_op jit(solution)/shard_map/ppermute | solution.py:48
  328.1 8.9 collective-permute-done.22
  344.3 13.4 %fusion.72 = f32[2560,800]{0,1:T(8,128)} fusion(bf16[2560,1600]{1,0:T(8,128)(2,1)} %constant_dynamic-update-slice_fusion.9, bf16[1600,800]{1,0:T(8,128)(2,1)} %all-gather.9.cloned.1.call-done), kind=kOutput, calls=%fused_computation.285 | convolution fusion | flops 6553600000 | bytes 18944000 | tf_op jit(solution)/shard_map/dot_general | solution.py:515
  357.7 16.3 %convert_reduce_fusion = (f32[800]{0:T(1024)}, bf16[2560,800]{0,1:T(8,128)(2,1)S(1)}) fusion(f32[2560,800]{0,1:T(8,128)} %fusion.72, f32[800]{0:T(1024)S(1)} %fusion.49, bf16[2560,1600]{1,0:T(8,128)(2,1)} %copy-done.21, bf16[800,1600]{1,0:T(8,128)(2,1)} %all-gather.11.cloned.1.call-done), kind=kOutput, calls=%fused_computation.15 | convolution fusion | flops 6600702976 | bytes 23046400 | tf_op jit(solution)/shard_map/dot_general | solution.py:521
  375.9 13.3 %convolution_convert_fusion.5 = bf16[1600,800]{1,0:T(8,128)(2,1)} fusion(bf16[2560,1600]{1,0:T(8,128)(2,1)} %constant_dynamic-update-slice_fusion.9, bf16[2560,800]{0,1:T(8,128)(2,1)S(1)} %get-tuple-element.162), kind=kOutput, calls=%fused_computation.21 | convolution fusion | flops 6554880000 | bytes 14848000 | tf_op jit(solution)/shard_map/dot_general | solution.py:528
  389.3 12.5 %convolution_convert_fusion.1 = bf16[2560,1600]{1,0:T(8,128)(2,1)S(1)} fusion(bf16[2560,800]{0,1:T(8,128)(2,1)} %copy-done.41, bf16[1600,800]{1,0:T(8,128)(2,1)} %all-gather.9.cloned.1.call-done), kind=kOutput, calls=%fused_computation.5 | convolution fusion | flops 6557696000 | bytes 14848000 | tf_op jit(solution)/shard_map/dot_general | solution.py:525
  404.7 16.0 %convolution_convert_fusion.2 = bf16[2560,1600]{1,0:T(8,128)(2,1)S(1)} fusion(bf16[800,1600]{1,0:T(8,128)(2,1)} %all-gather.11.cloned.1.call-done, f32[2560,800]{0,1:T(8,128)} %fusion.72, f32[800]{0:T(1024)S(1)} %fusion.49), kind=kOutput, calls=%fused_computation.6 | convolution fusion | flops 6578176000 | bytes 18947200 | tf_op jit(solution)/shard_map/dot_general | solution.py:518
  436.4 8.6 collective-permute-done.46
  447.6 12.1 %collective-permute-done.43 = bf16[160,1600]{1,0:T(8,128)(2,1)S(1)} collective-permute-done((bf16[160,1600]{1,0:T(8,128)(2,1)S(1)}, bf16[160,1600]{1,0:T(8,128)(2,1)S(1)}, u32[]{:S(2)}, u32[]{:S(2)}) %collective-permute-start.43) | collective-permute-done | bytes 512032 | tf_op jit(solution)/shard_map/ppermute | solution.py:48
  467.3 3.8 copy.463
  471.2 15.3 %collective-permute-done.47 = bf16[320,1600]{1,0:T(8,128)(2,1)} collective-permute-done((bf16[320,1600]{1,0:T(8,128)(2,1)}, bf16[320,1600]{1,0:T(8,128)(2,1)}, u32[]{:S(2)}, u32[]{:S(2)}) %collective-permute-start.47) | collective-permute-done | bytes 1024032 | tf_op jit(solution)/shard_map/ppermute | solution.py:48
  489.0 4.4 multiply_reduce_fusion
  493.4 14.4 %collective-permute-done.31 = bf16[320,1600]{1,0:T(8,128)(2,1)} collective-permute-done((bf16[320,1600]{1,0:T(8,128)(2,1)}, bf16[320,1600]{1,0:T(8,128)(2,1)}, u32[]{:S(2)}, u32[]{:S(2)}) %collective-permute-start.31) | collective-permute-done | bytes 1024032 | tf_op jit(solution)/shard_map/ppermute | solution.py:48
  510.1 6.2 convert_reduce_fusion.4
  517.6 12.9 %convolution_convert_fusion.6 = bf16[800,1600]{1,0:T(8,128)(2,1)} fusion(bf16[2560,1600]{1,0:T(8,128)(2,1)S(1)} %bitcast.110, f32[2560,800]{0,1:T(8,128)} %fusion.72, f32[800]{0:T(1024)S(1)} %fusion.49), kind=kOutput, calls=%fused_computation.22 | convolution fusion | flops 6575360000 | bytes 18947200 | tf_op jit(solution)/shard_map/dot_general | solution.py:528
  531.0 9.6 collective-permute-done.49
  548.9 8.6 collective-permute-done.54
  564.3 6.3 convolution_convert_fusion.4
  571.9 51.4 %attend_back.1 = bf16[2560,768]{1,0:T(8,128)(2,1)} custom-call(s32[10]{0:T(128)S(1)} %fusion.57.count, s32[10,10]{1,0:T(8,128)S(1)} %select_reduce_fusion.1.listed, s32[10]{0:T(128)S(1)} %compare_convert_fusion.3.owned, bf16[4,2560,128]{2,1,0:T(8,128)(2,1)} %pad_maximum_fusion.1.qx, bf16[4,2560,128]{2,1,0:T(8,128)(2,1)} %copy.428.kx, ...), custom_call_target="tpu_custom_call" | custom-call | flops 16777216000 | bytes 20971520 | tf_op jit(solution)/shard_map/attend_back/pallas_call | solution.py:321
  629.9 8.6 convolution_convert_fusion.7
  639.8 6.9 convolution_convert_fusion.8
  650.6 14.3 %reshape.420 = bf16[12800,200]{1,0:T(8,128)(2,1)} reshape(bf16[1600,1600]{1,0:T(8,128)(2,1)} %pad_maximum_fusion) | data formatting | bytes 10240000 | tf_op jit(solution)/shard_map/reshape | solution.py:578
  666.6 9.2 convolution_convert_fusion
  683.4 54.5 %pmax.7 = f32[25]{0:T(128)S(1)} all-reduce(f32[25]{0:T(128)S(1)} %pad_maximum_fusion.21), channel_id=1, replica_groups=mesh['t'=4,'a'=2,'b'=2,'c'=2] {'t','a','b','c'}, use_global_device_ids=true, to_apply=%region_42.43 | all-reduce | flops 25 | bytes 200 | tf_op jit(solution)/shard_map/pmax | solution.py:500
  748.1 19.1 %collective-permute-done.62 = bf16[160,1600]{1,0:T(8,128)(2,1)S(1)} collective-permute-done((bf16[160,1600]{1,0:T(8,128)(2,1)S(1)}, bf16[160,1600]{1,0:T(8,128)(2,1)S(1)}, u32[]{:S(2)}, u32[]{:S(2)}) %collective-permute-start.62) | collective-permute-done | bytes 512032 | tf_op jit(solution)/shard_map/ppermute | solution.py:48
  777.1 4.2 all-to-all-start.3
  789.6 45.0 %all-to-all-done.3 = bf16[8,50,800]{2,1,0:T(8,128)(2,1)} async-done(((bf16[8,50,800]{2,1,0:T(8,128)(2,1)}), bf16[8,50,800]{2,1,0:T(8,128)(2,1)}, u32[]{:S(2)}, u32[]{:S(2)}) %all-to-all-start.3) | async-done | bytes 640032 | tf_op jit(solution)/shard_map/all_to_all | solution.py:392
  839.1 4.3 fusion.19
  845.6 4.5 all-to-all-start.2
  850.1 3.7 fusion.18
  853.8 7.9 all-to-all-done.2
  869.3 3.3 reshape_reshape.11
  876.9 101.4 %all-reduce.6.cloned.1.call-done = (f32[1600]{0:T(1024)}, f32[1600]{0:T(1024)}, f32[1600]{0:T(1024)}, f32[1600]{0:T(1024)}, f32[1600]{0:T(1024)}, /*index=5*/f32...) async-done(((f32[1600]{0:T(1024)}, f32[1600]{0:T(1024)}, f32[1600]{0:T(1024)}, f32[1600]{0:T(1024)}, f32[1600]{0:T(1024)}, /*index=5*/f32[1600]{0:T(1024)}, ...) | async-done | bytes 76816 | tf_op jit(solution)/shard_map/psum | solution.py:604
  (495 shorter events, 248.3 us)
Async XLA Ops:
  7.2 85.1 %all-gather.5.cloned.1.call-start = ((), (), s32[]{:S(2)}) async-start(), calls=%async_computation.8 | async-start | bytes 3072000 | tf_op jit(solution)/shard_map/all_gather | solution.py:403
  31.0 156.5 %all-gather.7.cloned.1.call-start = ((), (), s32[]{:S(2)}) async-start(), calls=%async_computation.9 | async-start | bytes 6758400 | tf_op jit(solution)/shard_map/all_gather | solution.py:468
  34.4 36.5 %collective-permute-start.3 = (bf16[320,1600]{1,0:T(8,128)(2,1)}, bf16[320,1600]{1,0:T(8,128)(2,1)}, u32[]{:S(2)}, u32[]{:S(2)}) collective-permute-start(bf16[320,1600]{1,0:T(8,128)(2,1)} %get-tuple-element.173), channel_id=1, source_target_pairs={{0,4},{4,0},{1,5},{5,1},{2,6},{6,2},{3,7},{7,3},{8,12},{12,8},{9,1... | collective-permute-start | bytes 3072008 | tf_op jit(solution)/shard_map/ppermute | solution.py:48
  35.0 26.8 %collective-permute-start.1 = (bf16[320,1600]{1,0:T(8,128)(2,1)}, bf16[320,1600]{1,0:T(8,128)(2,1)}, u32[]{:S(2)}, u32[]{:S(2)}) collective-permute-start(bf16[320,1600]{1,0:T(8,128)(2,1)} %get-tuple-element.173), channel_id=1, source_target_pairs={{0,2},{2,0},{1,3},{3,1},{4,6},{6,4},{5,7},{7,5},{8,10},{10,8},{9,1... | collective-permute-start | bytes 3072008 | tf_op jit(solution)/shard_map/ppermute | solution.py:48
  35.5 39.1 %collective-permute-start = (bf16[320,1600]{1,0:T(8,128)(2,1)}, bf16[320,1600]{1,0:T(8,128)(2,1)}, u32[]{:S(2)}, u32[]{:S(2)}) collective-permute-start(bf16[320,1600]{1,0:T(8,128)(2,1)} %get-tuple-element.173), channel_id=1, source_target_pairs={{0,1},{1,0},{2,3},{3,2},{4,5},{5,4},{6,7},{7,6},{8,9},{9,8},{10,11... | collective-permute-start | bytes 3072008 | tf_op jit(solution)/shard_map/ppermute | solution.py:48
  38.1 31.4 %all-to-all-start.1 = ((bf16[8,50,800]{2,1,0:T(8,128)(2,1)}), bf16[8,50,800]{2,1,0:T(8,128)(2,1)S(1)}, u32[]{:S(2)}, u32[]{:S(2)}) async-start(bf16[8,50,800]{2,1,0:T(8,128)(2,1)} %reshape.434), calls=%async_computation.1 | async-start | bytes 1605632 | tf_op jit(solution)/shard_map/all_to_all | solution.py:392
  41.8 302.5 %all-gather.9.cloned.1.call-start = ((), (), s32[]{:S(2)}) async-start(), calls=%async_computation.10 | async-start | bytes 3584000 | tf_op jit(solution)/shard_map/all_gather | solution.py:403
  61.7 23.3 %collective-permute-start.2 = (bf16[320,1600]{1,0:T(8,128)(2,1)}, bf16[320,1600]{1,0:T(8,128)(2,1)S(1)}, u32[]{:S(2)}, u32[]{:S(2)}) collective-permute-start(bf16[320,1600]{1,0:T(8,128)(2,1)} %collective-permute-done.1), channel_id=1, source_target_pairs={{0,1},{1,0},{2,3},{3,2},{4,5},{5,4},{6,7},{7,6},{8,9},{9,8},{10,11... | collective-permute-start | bytes 3072008 | tf_op jit(solution)/shard_map/ppermute | solution.py:48
  70.7 287.0 %all-gather.11.cloned.1.call-start = ((), (), s32[]{:S(2)}) async-start(), calls=%async_computation.11 | async-start | bytes 3328000 | tf_op jit(solution)/shard_map/all_gather | solution.py:475
  216.1 39.3 %collective-permute-start.33 = (bf16[320,1600]{1,0:T(8,128)(2,1)}, bf16[320,1600]{1,0:T(8,128)(2,1)}, u32[]{:S(2)}, u32[]{:S(2)}) collective-permute-start(bf16[320,1600]{1,0:T(8,128)(2,1)} %param.18), channel_id=1, source_target_pairs={{0,2},{2,0},{1,3},{3,1},{4,6},{6,4},{5,7},{7,5},{8,10},{10,8},{9,1... | collective-permute-start | bytes 3072008 | tf_op jit(solution)/shard_map/ppermute | solution.py:48
  217.1 44.4 %collective-permute-start.32 = (bf16[320,1600]{1,0:T(8,128)(2,1)}, bf16[320,1600]{1,0:T(8,128)(2,1)}, u32[]{:S(2)}, u32[]{:S(2)}) collective-permute-start(bf16[320,1600]{1,0:T(8,128)(2,1)} %param.18), channel_id=1, source_target_pairs={{0,1},{1,0},{2,3},{3,2},{4,5},{5,4},{6,7},{7,6},{8,9},{9,8},{10,11... | collective-permute-start | bytes 3072008 | tf_op jit(solution)/shard_map/ppermute | solution.py:48
  217.2 41.8 %collective-permute-start.35 = (bf16[320,1600]{1,0:T(8,128)(2,1)}, bf16[320,1600]{1,0:T(8,128)(2,1)}, u32[]{:S(2)}, u32[]{:S(2)}) collective-permute-start(bf16[320,1600]{1,0:T(8,128)(2,1)} %param.18), channel_id=1, source_target_pairs={{0,4},{4,0},{1,5},{5,1},{2,6},{6,2},{3,7},{7,3},{8,12},{12,8},{9,1... | collective-permute-start | bytes 3072008 | tf_op jit(solution)/shard_map/ppermute | solution.py:48
  222.6 552.3 %reduce-scatter.11.cloned.1.call-start = ((), (), s32[]{:S(2)}) async-start(), calls=%async_computation.14 | async-start | bytes 3584000 | tf_op jit(solution)/shard_map/reduce_scatter | solution.py:411
  225.7 66.2 %collective-permute-start.8 = (bf16[320,1600]{1,0:T(8,128)(2,1)}, bf16[320,1600]{1,0:T(8,128)(2,1)S(1)}, u32[]{:S(2)}, u32[]{:S(2)}) collective-permute-start(bf16[320,1600]{1,0:T(8,128)(2,1)} %get-tuple-element.195), channel_id=1, source_target_pairs={{0,1},{1,0},{2,3},{3,2},{4,5},{5,4},{6,7},{7,6},{8,9},{9,8},{10,11... | collective-permute-start | bytes 3072008 | tf_op jit(solution)/shard_map/ppermute | solution.py:48
  230.4 24.3 %collective-permute-start.11 = (bf16[160,1600]{1,0:T(8,128)(2,1)}, bf16[160,1600]{1,0:T(8,128)(2,1)S(1)}, u32[]{:S(2)}, u32[]{:S(2)}) collective-permute-start(bf16[160,1600]{1,0:T(8,128)(2,1)} %get-tuple-element.215), channel_id=1, source_target_pairs={{0,4},{4,0},{1,5},{5,1},{2,6},{6,2},{3,7},{7,3},{8,12},{12,8},{9,1... | collective-permute-start | bytes 1536008 | tf_op jit(solution)/shard_map/ppermute | solution.py:48
  254.7 37.8 %collective-permute-start.15 = (bf16[320,1600]{1,0:T(8,128)(2,1)S(1)}, bf16[320,1600]{1,0:T(8,128)(2,1)S(1)}, u32[]{:S(2)}, u32[]{:S(2)}) collective-permute-start(bf16[320,1600]{1,0:T(8,128)(2,1)S(1)} %pad_maximum_fusion.6), channel_id=1, source_target_pairs={{0,4},{4,0},{1,5},{5,1},{2,6},{6,2},{3,7},{7,3},{8,12},{12,8},{9,1... | collective-permute-start | bytes 3072008 | tf_op jit(solution)/shard_map/ppermute | solution.py:48
  255.4 37.1 %collective-permute-start.12 = (bf16[320,1600]{1,0:T(8,128)(2,1)S(1)}, bf16[320,1600]{1,0:T(8,128)(2,1)S(1)}, u32[]{:S(2)}, u32[]{:S(2)}) collective-permute-start(bf16[320,1600]{1,0:T(8,128)(2,1)S(1)} %pad_maximum_fusion.5), channel_id=1, source_target_pairs={{0,2},{2,0},{1,3},{3,1},{4,6},{6,4},{5,7},{7,5},{8,10},{10,8},{9,1... | collective-permute-start | bytes 3072008 | tf_op jit(solution)/shard_map/ppermute | solution.py:48
  259.0 32.4 %collective-permute-start.37 = (bf16[160,1600]{1,0:T(8,128)(2,1)S(1)}, bf16[160,1600]{1,0:T(8,128)(2,1)S(1)}, u32[]{:S(2)}, u32[]{:S(2)}) collective-permute-start(bf16[160,1600]{1,0:T(8,128)(2,1)S(1)} %slice.384), channel_id=1, source_target_pairs={{0,4},{4,0},{1,5},{5,1},{2,6},{6,2},{3,7},{7,3},{8,12},{12,8},{9,1... | collective-permute-start | bytes 1536008 | tf_op jit(solution)/shard_map/ppermute | solution.py:48
  261.6 30.3 %collective-permute-start.38 = (bf16[160,1600]{1,0:T(8,128)(2,1)S(1)}, bf16[160,1600]{1,0:T(8,128)(2,1)S(1)}, u32[]{:S(2)}, u32[]{:S(2)}) collective-permute-start(bf16[160,1600]{1,0:T(8,128)(2,1)S(1)} %slice.385), channel_id=1, source_target_pairs={{0,2},{2,0},{1,3},{3,1},{4,6},{6,4},{5,7},{7,5},{8,10},{10,8},{9,1... | collective-permute-start | bytes 1536008 | tf_op jit(solution)/shard_map/ppermute | solution.py:48
  292.0 30.3 %collective-permute-start.39 = (bf16[320,1600]{1,0:T(8,128)(2,1)S(1)}, bf16[320,1600]{1,0:T(8,128)(2,1)S(1)}, u32[]{:S(2)}, u32[]{:S(2)}) collective-permute-start(bf16[320,1600]{1,0:T(8,128)(2,1)S(1)} %pad_maximum_fusion.10), channel_id=1, source_target_pairs={{0,1},{1,0},{2,3},{3,2},{4,5},{5,4},{6,7},{7,6},{8,9},{9,8},{10,11... | collective-permute-start | bytes 3072008 | tf_op jit(solution)/shard_map/ppermute | solution.py:48
  296.8 25.4 %collective-permute-start.17 = (bf16[320,1600]{1,0:T(8,128)(2,1)S(1)}, bf16[320,1600]{1,0:T(8,128)(2,1)S(1)}, u32[]{:S(2)}, u32[]{:S(2)}) collective-permute-start(bf16[320,1600]{1,0:T(8,128)(2,1)S(1)} %get-tuple-element.169), channel_id=1, source_target_pairs={{0,2},{2,0},{1,3},{3,1},{4,6},{6,4},{5,7},{7,5},{8,10},{10,8},{9,1... | collective-permute-start | bytes 3072008 | tf_op jit(solution)/shard_map/ppermute | solution.py:48
  298.1 25.2 %collective-permute-start.19 = (bf16[320,1600]{1,0:T(8,128)(2,1)S(1)}, bf16[320,1600]{1,0:T(8,128)(2,1)S(1)}, u32[]{:S(2)}, u32[]{:S(2)}) collective-permute-start(bf16[320,1600]{1,0:T(8,128)(2,1)S(1)} %get-tuple-element.169), channel_id=1, source_target_pairs={{0,4},{4,0},{1,5},{5,1},{2,6},{6,2},{3,7},{7,3},{8,12},{12,8},{9,1... | collective-permute-start | bytes 3072008 | tf_op jit(solution)/shard_map/ppermute | solution.py:48
  299.6 26.4 %collective-permute-start.16 = (bf16[320,1600]{1,0:T(8,128)(2,1)S(1)}, bf16[320,1600]{1,0:T(8,128)(2,1)S(1)}, u32[]{:S(2)}, u32[]{:S(2)}) collective-permute-start(bf16[320,1600]{1,0:T(8,128)(2,1)S(1)} %get-tuple-element.169), channel_id=1, source_target_pairs={{0,1},{1,0},{2,3},{3,2},{4,5},{5,4},{6,7},{7,6},{8,9},{9,8},{10,11... | collective-permute-start | bytes 3072008 | tf_op jit(solution)/shard_map/ppermute | solution.py:48
  389.3 392.1 %reduce-scatter.13.cloned.1.call-start = ((), (), s32[]{:S(2)}) async-start(), calls=%async_computation.15 | async-start | bytes 3328000
  404.2 19.5 %collective-permute-start.41 = (bf16[320,1600]{1,0:T(8,128)(2,1)S(1)}, bf16[320,1600]{1,0:T(8,128)(2,1)S(1)}, u32[]{:S(2)}, u32[]{:S(2)}) collective-permute-start(bf16[320,1600]{1,0:T(8,128)(2,1)S(1)} %get-tuple-element.184), channel_id=1, source_target_pairs={{0,1},{1,0},{2,3},{3,2},{4,5},{5,4},{6,7},{7,6},{8,9},{9,8},{10,11... | collective-permute-start | bytes 3072008 | tf_op jit(solution)/shard_map/ppermute | solution.py:48
  422.6 70.8 %collective-permute-start.24 = (bf16[320,1600]{1,0:T(8,128)(2,1)}, bf16[320,1600]{1,0:T(8,128)(2,1)}, u32[]{:S(2)}, u32[]{:S(2)}) collective-permute-start(bf16[320,1600]{1,0:T(8,128)(2,1)} %get-tuple-element.188), channel_id=1, source_target_pairs={{0,1},{1,0},{2,3},{3,2},{4,5},{5,4},{6,7},{7,6},{8,9},{9,8},{10,11... | collective-permute-start | bytes 3072008 | tf_op jit(solution)/shard_map/ppermute | solution.py:48
  425.1 40.8 %collective-permute-start.40 = (bf16[320,1600]{1,0:T(8,128)(2,1)}, bf16[320,1600]{1,0:T(8,128)(2,1)}, u32[]{:S(2)}, u32[]{:S(2)}) collective-permute-start(bf16[320,1600]{1,0:T(8,128)(2,1)} %get-tuple-element.181), channel_id=1, source_target_pairs={{0,1},{1,0},{2,3},{3,2},{4,5},{5,4},{6,7},{7,6},{8,9},{9,8},{10,11... | collective-permute-start | bytes 3072008 | tf_op jit(solution)/shard_map/ppermute | solution.py:48
  433.9 30.6 %collective-permute-start.27 = (bf16[160,1600]{1,0:T(8,128)(2,1)S(1)}, bf16[160,1600]{1,0:T(8,128)(2,1)S(1)}, u32[]{:S(2)}, u32[]{:S(2)}) collective-permute-start(bf16[160,1600]{1,0:T(8,128)(2,1)S(1)} %get-tuple-element.213), channel_id=1, source_target_pairs={{0,4},{4,0},{1,5},{5,1},{2,6},{6,2},{3,7},{7,3},{8,12},{12,8},{9,1... | collective-permute-start | bytes 1536008 | tf_op jit(solution)/shard_map/ppermute | solution.py:48
  435.3 26.9 %collective-permute-start.30 = (bf16[160,1600]{1,0:T(8,128)(2,1)S(1)}, bf16[160,1600]{1,0:T(8,128)(2,1)S(1)}, u32[]{:S(2)}, u32[]{:S(2)}) collective-permute-start(bf16[160,1600]{1,0:T(8,128)(2,1)S(1)} %get-tuple-element.214), channel_id=1, source_target_pairs={{0,2},{2,0},{1,3},{3,1},{4,6},{6,4},{5,7},{7,5},{8,10},{10,8},{9,1... | collective-permute-start | bytes 1536008 | tf_op jit(solution)/shard_map/ppermute | solution.py:48
  459.7 26.8 %collective-permute-start.47 = (bf16[320,1600]{1,0:T(8,128)(2,1)}, bf16[320,1600]{1,0:T(8,128)(2,1)}, u32[]{:S(2)}, u32[]{:S(2)}) collective-permute-start(bf16[320,1600]{1,0:T(8,128)(2,1)} %pad_maximum_fusion.12), channel_id=1, source_target_pairs={{0,4},{4,0},{1,5},{5,1},{2,6},{6,2},{3,7},{7,3},{8,12},{12,8},{9,1... | collective-permute-start | bytes 3072008 | tf_op jit(solution)/shard_map/ppermute | solution.py:48
  462.3 26.8 %collective-permute-start.44 = (bf16[320,1600]{1,0:T(8,128)(2,1)}, bf16[320,1600]{1,0:T(8,128)(2,1)}, u32[]{:S(2)}, u32[]{:S(2)}) collective-permute-start(bf16[320,1600]{1,0:T(8,128)(2,1)} %pad_maximum_fusion.11), channel_id=1, source_target_pairs={{0,2},{2,0},{1,3},{3,1},{4,6},{6,4},{5,7},{7,5},{8,10},{10,8},{9,1... | collective-permute-start | bytes 3072008 | tf_op jit(solution)/shard_map/ppermute | solution.py:48
  464.4 43.4 %collective-permute-start.31 = (bf16[320,1600]{1,0:T(8,128)(2,1)}, bf16[320,1600]{1,0:T(8,128)(2,1)}, u32[]{:S(2)}, u32[]{:S(2)}) collective-permute-start(bf16[320,1600]{1,0:T(8,128)(2,1)} %pad_maximum_fusion.9), channel_id=1, source_target_pairs={{0,4},{4,0},{1,5},{5,1},{2,6},{6,2},{3,7},{7,3},{8,12},{12,8},{9,1... | collective-permute-start | bytes 3072008 | tf_op jit(solution)/shard_map/ppermute | solution.py:48
  465.9 44.2 %collective-permute-start.28 = (bf16[320,1600]{1,0:T(8,128)(2,1)}, bf16[320,1600]{1,0:T(8,128)(2,1)}, u32[]{:S(2)}, u32[]{:S(2)}) collective-permute-start(bf16[320,1600]{1,0:T(8,128)(2,1)} %pad_maximum_fusion.8), channel_id=1, source_target_pairs={{0,2},{2,0},{1,3},{3,1},{4,6},{6,4},{5,7},{7,5},{8,10},{10,8},{9,1... | collective-permute-start | bytes 3072008 | tf_op jit(solution)/shard_map/ppermute | solution.py:48
  516.3 26.7 %collective-permute-start.51 = (bf16[320,1600]{1,0:T(8,128)(2,1)}, bf16[320,1600]{1,0:T(8,128)(2,1)S(1)}, u32[]{:S(2)}, u32[]{:S(2)}) collective-permute-start(bf16[320,1600]{1,0:T(8,128)(2,1)} %get-tuple-element.164), channel_id=1, source_target_pairs={{0,4},{4,0},{1,5},{5,1},{2,6},{6,2},{3,7},{7,3},{8,12},{12,8},{9,1... | collective-permute-start | bytes 3072008 | tf_op jit(solution)/shard_map/ppermute | solution.py:48
  516.9 23.7 %collective-permute-start.49 = (bf16[320,1600]{1,0:T(8,128)(2,1)}, bf16[320,1600]{1,0:T(8,128)(2,1)S(1)}, u32[]{:S(2)}, u32[]{:S(2)}) collective-permute-start(bf16[320,1600]{1,0:T(8,128)(2,1)} %get-tuple-element.164), channel_id=1, source_target_pairs={{0,2},{2,0},{1,3},{3,1},{4,6},{6,4},{5,7},{7,5},{8,10},{10,8},{9,1... | collective-permute-start | bytes 3072008 | tf_op jit(solution)/shard_map/ppermute | solution.py:48
  517.5 28.0 %collective-permute-start.48 = (bf16[320,1600]{1,0:T(8,128)(2,1)}, bf16[320,1600]{1,0:T(8,128)(2,1)}, u32[]{:S(2)}, u32[]{:S(2)}) collective-permute-start(bf16[320,1600]{1,0:T(8,128)(2,1)} %get-tuple-element.164), channel_id=1, source_target_pairs={{0,1},{1,0},{2,3},{3,2},{4,5},{5,4},{6,7},{7,6},{8,9},{9,8},{10,11... | collective-permute-start | bytes 3072008 | tf_op jit(solution)/shard_map/ppermute | solution.py:48
  530.5 313.0 %reduce-scatter.7.cloned.1.call-start = ((), (), s32[]{:S(2)}) async-start(), calls=%async_computation.12 | async-start | bytes 3072000 | tf_op jit(solution)/shard_map/reduce_scatter | solution.py:411
  638.5 236.7 %reduce-scatter.9.cloned.1.call-start = ((), (), s32[]{:S(2)}) async-start(), calls=%async_computation.13 | async-start | bytes 6758400 | tf_op jit(solution)/shard_map/reduce_scatter | solution.py:577
  680.4 57.4 %collective-permute-start.61 = (bf16[320,1600]{1,0:T(8,128)(2,1)}, bf16[320,1600]{1,0:T(8,128)(2,1)S(1)}, u32[]{:S(2)}, u32[]{:S(2)}) collective-permute-start(bf16[320,1600]{1,0:T(8,128)(2,1)} %get-tuple-element.175), channel_id=1, source_target_pairs={{0,1},{1,0},{2,3},{3,2},{4,5},{5,4},{6,7},{7,6},{8,9},{9,8},{10,11... | collective-permute-start | bytes 3072008 | tf_op jit(solution)/shard_map/ppermute | solution.py:48
  680.4 57.4 %collective-permute-start.58 = (bf16[320,1600]{1,0:T(8,128)(2,1)}, bf16[320,1600]{1,0:T(8,128)(2,1)S(1)}, u32[]{:S(2)}, u32[]{:S(2)}) collective-permute-start(bf16[320,1600]{1,0:T(8,128)(2,1)} %get-tuple-element.176), channel_id=1, source_target_pairs={{0,1},{1,0},{2,3},{3,2},{4,5},{5,4},{6,7},{7,6},{8,9},{9,8},{10,11... | collective-permute-start | bytes 3072008 | tf_op jit(solution)/shard_map/ppermute | solution.py:48
  681.0 56.9 %collective-permute-start.57 = (bf16[320,1600]{1,0:T(8,128)(2,1)}, bf16[320,1600]{1,0:T(8,128)(2,1)}, u32[]{:S(2)}, u32[]{:S(2)}) collective-permute-start(bf16[320,1600]{1,0:T(8,128)(2,1)} %get-tuple-element.177), channel_id=1, source_target_pairs={{0,1},{1,0},{2,3},{3,2},{4,5},{5,4},{6,7},{7,6},{8,9},{9,8},{10,11... | collective-permute-start | bytes 3072008 | tf_op jit(solution)/shard_map/ppermute | solution.py:48
  740.8 26.3 %collective-permute-start.62 = (bf16[160,1600]{1,0:T(8,128)(2,1)S(1)}, bf16[160,1600]{1,0:T(8,128)(2,1)S(1)}, u32[]{:S(2)}, u32[]{:S(2)}) collective-permute-start(bf16[160,1600]{1,0:T(8,128)(2,1)S(1)} %get-tuple-element.210), channel_id=1, source_target_pairs={{0,2},{2,0},{1,3},{3,1},{4,6},{6,4},{5,7},{7,5},{8,10},{10,8},{9,1... | collective-permute-start | bytes 1536008 | tf_op jit(solution)/shard_map/ppermute | solution.py:48
  746.0 93.1 %collective-permute-start.56 = (bf16[320,1600]{1,0:T(8,128)(2,1)}, bf16[320,1600]{1,0:T(8,128)(2,1)}, u32[]{:S(2)}, u32[]{:S(2)}) collective-permute-start(bf16[320,1600]{1,0:T(8,128)(2,1)} %get-tuple-element.174), channel_id=1, source_target_pairs={{0,1},{1,0},{2,3},{3,2},{4,5},{5,4},{6,7},{7,6},{8,9},{9,8},{10,11... | collective-permute-start | bytes 3072008 | tf_op jit(solution)/shard_map/ppermute | solution.py:48
  746.2 22.2 %collective-permute-start.59 = (bf16[160,1600]{1,0:T(8,128)(2,1)S(1)}, bf16[160,1600]{1,0:T(8,128)(2,1)S(1)}, u32[]{:S(2)}, u32[]{:S(2)}) collective-permute-start(bf16[160,1600]{1,0:T(8,128)(2,1)S(1)} %get-tuple-element.209), channel_id=1, source_target_pairs={{0,4},{4,0},{1,5},{5,1},{2,6},{6,2},{3,7},{7,3},{8,12},{12,8},{9,1... | collective-permute-start | bytes 1536008 | tf_op jit(solution)/shard_map/ppermute | solution.py:48
  768.4 70.7 %collective-permute-start.63 = (bf16[320,1600]{1,0:T(8,128)(2,1)}, bf16[320,1600]{1,0:T(8,128)(2,1)}, u32[]{:S(2)}, u32[]{:S(2)}) collective-permute-start(bf16[320,1600]{1,0:T(8,128)(2,1)} %pad_maximum_fusion.15), channel_id=1, source_target_pairs={{0,4},{4,0},{1,5},{5,1},{2,6},{6,2},{3,7},{7,3},{8,12},{12,8},{9,1... | collective-permute-start | bytes 3072008 | tf_op jit(solution)/shard_map/ppermute | solution.py:48
  769.6 69.5 %collective-permute-start.60 = (bf16[320,1600]{1,0:T(8,128)(2,1)}, bf16[320,1600]{1,0:T(8,128)(2,1)}, u32[]{:S(2)}, u32[]{:S(2)}) collective-permute-start(bf16[320,1600]{1,0:T(8,128)(2,1)} %pad_maximum_fusion.14), channel_id=1, source_target_pairs={{0,2},{2,0},{1,3},{3,1},{4,6},{6,4},{5,7},{7,5},{8,10},{10,8},{9,1... | collective-permute-start | bytes 3072008 | tf_op jit(solution)/shard_map/ppermute | solution.py:48
  777.1 57.4 %all-to-all-start.3 = ((bf16[8,50,800]{2,1,0:T(8,128)(2,1)}), bf16[8,50,800]{2,1,0:T(8,128)(2,1)}, u32[]{:S(2)}, u32[]{:S(2)}) async-start(bf16[8,50,800]{2,1,0:T(8,128)(2,1)} %reshape.421), calls=%async_computation.6 | async-start | bytes 1605632 | tf_op jit(solution)/shard_map/all_to_all | solution.py:392
  781.3 196.9 %all-reduce.6.cloned.1.call-start = ((), (), s32[]{:S(2)}) async-start(), calls=%async_computation.16 | async-start | bytes 188416 | tf_op jit(solution)/shard_map/psum | solution.py:604
  (76 other events, 870.0 us)
Sparse Core Ops, SparseCore 0:
  31.2 51.4 all-gather.4
  85.5 69.4 all-gather.6
  156.6 57.5 all-gather.8
  222.7 63.2 all-gather.10
  389.4 64.3 reduce-scatter.10
  530.7 58.8 reduce-scatter.12
  638.6 61.9 reduce-scatter.6
  702.9 146.1 reduce-scatter.8
  856.7 121.5 all-reduce.5

commit v2 on v1

v2 whole, which is shorter than its diff:
```python
from functools import partial

import jax
import jax.numpy as jnp
from jax import lax
from jax.experimental import pallas as pl
from jax.experimental.layout import Layout, with_layout_constraint
from jax.experimental.pallas import tpu as pltpu
from jax.sharding import Mesh, PartitionSpec as P

HEAD_DIM = 64
TREE_TOK = 2560
GROUP = 8

EPS = 1e-05
TAU = 7.0
NEGATIVE = -1e30

BQ = 256
BK = 256
LANES = 128

TREE = "t"
PLANE = ("a", "b", "c")
EVERY = ("t", "a", "b", "c")
BF = jnp.bfloat16
F32 = jnp.float32


def norm_forward(values, norm_gain, norm_shift):
    row_mean = jnp.mean(values, axis=-1, keepdims=True)
    centered = values - row_mean
    inv_std = lax.rsqrt(jnp.mean(centered * centered, axis=-1, keepdims=True) + EPS)
    normed = centered * inv_std
    return (normed * norm_gain + norm_shift, normed, inv_std)


def norm_backward(upstream, normed, inv_std, norm_gain):
    scaled = upstream * norm_gain
    inner = (
        scaled
        - jnp.mean(scaled, axis=-1, keepdims=True)
        - normed * jnp.mean(scaled * normed, axis=-1, keepdims=True)
    )
    return (inner * inv_std, jnp.sum(upstream * normed, axis=0), jnp.sum(upstream, axis=0))


def swap(value, axis):
    return lax.ppermute(value, axis, [(0, 1), (1, 0)])


def after(value, *others):
    return lax.optimization_barrier((value, *others))[0] if others else value


def rows_major(array):
    return with_layout_constraint(array, Layout(major_to_minor=tuple(range(array.ndim))))


def plane_write(blocks, other, place, base):
    rows = blocks[0].shape[0]
    full = base
    if full is None:
        full = jnp.zeros((GROUP * rows,) + blocks[0].shape[1:], blocks[0].dtype)
    for r, block in enumerate(blocks):
        for q, piece in ((2 * r, block), (2 * r + 1, other[r])):
            full = lax.dynamic_update_slice_in_dim(full, piece, (place ^ q) * rows, 0)
    return rows_major(full)


def plane_gather(own, place, base=None):
    half = own.shape[0] // 2
    from_b, from_a = swap(own, "b"), swap(own, "a")
    diag = jnp.concatenate([swap(from_b[:half], "a"), swap(from_a[half:], "b")], axis=0)
    blocks = (own, from_b, from_a, diag)
    full = plane_write(blocks, [swap(block, "c") for block in blocks], place, base)
    return full, (from_b, from_a)


def plane_fetch(own):
    across = lax.ppermute(own, ("a", "b"), [(i, i ^ 3) for i in range(4)])
    return (swap(own, "b"), swap(own, "a"), across)


def plane_scatter(array, place, hold=lambda sent: ()):
    rows = array.shape[0] // GROUP
    array = rows_major(array)
    sent = [block_of(array, place ^ r, rows) for r in range(GROUP)]
    sent = list(lax.optimization_barrier(tuple(sent)))
    came = tuple(swap(sent[r + 1], "c") for r in (6, 2, 4, 0))
    came = after(came, *hold(sent))
    diag, for_b, for_a, mine = (
        sent[r].astype(F32) + block.astype(F32) for r, block in zip((6, 2, 4, 0), came)
    )
    half = diag.shape[0] // 2
    top, bottom = lax.optimization_barrier((diag[:half].astype(BF), diag[half:].astype(BF)))
    top, bottom = swap(top, "b"), swap(bottom, "a")
    for_a = jnp.concatenate([for_a[:half] + top.astype(F32), for_a[half:]], axis=0).astype(BF)
    for_b = jnp.concatenate([for_b[:half], for_b[half:] + bottom.astype(F32)], axis=0).astype(BF)
    for_a, for_b = lax.optimization_barrier((for_a, for_b))
    total = mine + swap(for_b, "b").astype(F32) + swap(for_a, "a").astype(F32)
    return total, (for_a, for_b)


def block_of(array, index, rows):
    return lax.dynamic_slice_in_dim(array, index * rows, rows, 0)


def tree_parts(grad):
    count, me = lax.axis_size(TREE), lax.axis_index(TREE)
    rows = grad.shape[0] // count
    parts = [block_of(grad, me, rows)]
    for hop in range(1, count):
        sent = block_of(grad, (me + hop) % count, rows)
        pairs = [(i, (i + hop) % count) for i in range(count)]
        parts.append(lax.ppermute(sent, TREE, pairs))
    return tuple(parts)


def pairwise(values, combines, axis, pairs):
    others = [lax.ppermute(value, axis, pairs) for value in values]
    return [combine(*both) for combine, *both in zip(combines, values, others)]


def over_plane(values, combines):
    for axis in ("c", "b", "a"):
        values = pairwise(values, combines, axis, [(0, 1), (1, 0)])
    return values


def over_trees(values, combines):
    count = lax.axis_size(TREE)
    hop = 1
    while hop < count:
        values = pairwise(values, combines, TREE, [(i, i ^ hop) for i in range(count)])
        hop *= 2
    return values


def tree_tables(lengths, parent_row):
    count = lengths.shape[0]
    numbers = jnp.arange(count, dtype=jnp.int32)
    ends = jnp.sum(jnp.where(numbers[None, :] <= numbers[:, None], lengths[None, :], 0), axis=1)
    starts = ends - lengths
    reach = (
        (numbers[:, None] == numbers[None, :]) | (parent_row[:, None] == numbers[None, :])
    ).astype(F32)
    hops = 1
    while hops < count:
        reach = (
            jnp.sum(reach[:, :, None] * reach[None, :, :], axis=1) > 0.5
        ).astype(F32)
        hops *= 2
    return starts, ends, reach


def block_lists(hot, path, q_blocks, k_blocks):
    q_has = jnp.max(path.reshape(q_blocks, -1, path.shape[1]), axis=1)
    k_has = jnp.max(hot.reshape(k_blocks, -1, hot.shape[1]), axis=1)
    live = jnp.sum(q_has[:, None, :] * k_has[None, :, :], axis=2) > 0.5
    q_first = jnp.arange(q_blocks, dtype=jnp.int32) * (BQ // BK)
    keys = jnp.arange(k_blocks, dtype=jnp.int32)
    live = (live & (keys[None, :] < q_first[:, None])).astype(jnp.int32)
    rank = jnp.sum(
        jnp.where(keys[None, :, None] > keys[None, None, :], live[:, None, :], 0), axis=2
    )
    listed = jnp.sum(
        jnp.where(
            (rank[:, :, None] == keys[None, None, :]) & (live[:, :, None] > 0),
            keys[None, :, None],
            0,
        ),
        axis=1,
    )
    return jnp.sum(live, axis=1).astype(jnp.int32), listed.astype(jnp.int32)


def score_block(kx, qx):
    return lax.dot_general(kx, qx, (((1,), (1,)), ((), ())), preferred_element_type=F32)


def causal(key_first, query_first):
    keys = key_first + lax.broadcasted_iota(jnp.int32, (BK, BQ), 0)
    queries = query_first + lax.broadcasted_iota(jnp.int32, (BK, BQ), 1)
    return keys <= queries


def in_blocks(count, listed, step, group, some):
    others = count[step]

    @pl.when(others % 2 == 0)
    def _():
        for h in group:
            some(h, (step,), True)

    @pl.when(others % 2 == 1)
    def _():
        for h in group:
            some(h, (step, listed[step, others - 1]), True)

    def body(i, carry):
        for h in group:
            some(h, (listed[step, 2 * i], listed[step, 2 * i + 1]), False)
        return carry

    lax.fori_loop(0, others // 2, body, 0)


def head_cols(part, h, local):
    at = (part * local + h) * HEAD_DIM
    return slice(at, at + HEAD_DIM)


def attend_kernel(
    count, listed, owned, proj, q_mark, k_mark, out, out_wide, lse, top, kx, vt, qx, m_s, l_s, acc_s
):
    step = pl.program_id(0)
    q_first = step * BQ
    local = acc_s.shape[0]
    here = pl.ds(pl.multiple_of(q_first, BQ), BQ)

    @pl.when(step == 0)
    def _():
        top[...] = jnp.full(top.shape, NEGATIVE, F32)

    for h in range(local):
        kx[h, here, :] = jnp.concatenate([proj[:, head_cols(1, h, local)], k_mark[...]], axis=1)
        query = proj[:, head_cols(0, h, local)] * jnp.asarray(HEAD_DIM ** (-0.5), BF)
        qx[h] = jnp.concatenate([query, q_mark[...]], axis=1)
    vt[:, here] = proj[:, 2 * local * HEAD_DIM :].T

    def some(h, blocks, diagonal):
        rows = [pl.ds(pl.multiple_of(kb * BK, BK), BK) for kb in blocks]
        scores = [score_block(kx[h, r, :], qx[h]) for r in rows]
        if diagonal:
            scores[0] = jnp.where(causal(blocks[0] * BK, q_first), scores[0], NEGATIVE)
        old = m_s[h : h + 1, :]
        new = old
        for score in scores:
            new = jnp.maximum(new, jnp.max(score, axis=0, keepdims=True))
        weights = [jnp.exp(score - new) for score in scores]
        shrink = jnp.exp(old - new)
        m_s[h : h + 1, :] = new
        l_s[h : h + 1, :] = l_s[h : h + 1, :] * shrink + sum(
            jnp.sum(weight, axis=0, keepdims=True) for weight in weights
        )
        acc_s[h] = acc_s[h] * shrink + sum(
            jnp.dot(
                vt[h * HEAD_DIM : (h + 1) * HEAD_DIM, r],
                weight.astype(BF),
                preferred_element_type=F32,
            )
            for r, weight in zip(rows, weights)
        )

    def heads(group):
        for h in group:
            m_s[h : h + 1, :] = jnp.full((1, BQ), NEGATIVE, F32)
            l_s[h : h + 1, :] = jnp.zeros((1, BQ), F32)
            acc_s[h] = jnp.zeros((HEAD_DIM, BQ), F32)
        in_blocks(count, listed, step, group, some)
        for h in group:
            total = l_s[h : h + 1, :]
            out_wide[h] = acc_s[h] / total
            lse[h : h + 1, :] = m_s[h : h + 1, :] + jnp.log(total)
            top[h : h + 1, :] = jnp.maximum(top[h : h + 1, :], m_s[h : h + 1, :])

    last = local - 1
    heads(range(last))

    @pl.when(owned[step] > 0)
    def _():
        heads([last])

    @pl.when(owned[step] == 0)
    def _():
        out_wide[last] = jnp.zeros((HEAD_DIM, BQ), F32)
        lse[last : last + 1, :] = jnp.zeros((1, BQ), F32)

    for h in range(local):
        out[:, h * HEAD_DIM : (h + 1) * HEAD_DIM] = out_wide[h].T.astype(BF)


def whole_block(shape):
    return pl.BlockSpec(shape, lambda i, *_: (0,) * len(shape), pipeline_mode=pl.Buffered(1))


def attend(count, listed, owned, proj, q_mark, k_mark):
    tokens, width = proj.shape
    heads = width // (3 * HEAD_DIM)
    return pl.pallas_call(
        attend_kernel,
        grid_spec=pltpu.PrefetchScalarGridSpec(
            num_scalar_prefetch=3,
            grid=(tokens // BQ,),
            in_specs=[
                pl.BlockSpec((BQ, width), lambda i, *_: (i, 0)),
                pl.BlockSpec((BQ, q_mark.shape[1]), lambda i, *_: (i, 0)),
                pl.BlockSpec((BQ, k_mark.shape[1]), lambda i, *_: (i, 0)),
            ],
            out_specs=[
                pl.BlockSpec((BQ, heads * HEAD_DIM), lambda i, *_: (i, 0)),
                pl.BlockSpec((heads, HEAD_DIM, BQ), lambda i, *_: (0, 0, i)),
                pl.BlockSpec((heads, BQ), lambda i, *_: (0, i)),
                pl.BlockSpec((heads, BQ), lambda i, *_: (0, 0)),
            ],
            scratch_shapes=[
                pltpu.VMEM((heads, tokens, LANES), BF),
                pltpu.VMEM((heads * HEAD_DIM, tokens), BF),
                pltpu.VMEM((heads, BQ, LANES), BF),
                pltpu.VMEM((heads, BQ), F32),
                pltpu.VMEM((heads, BQ), F32),
                pltpu.VMEM((heads, HEAD_DIM, BQ), F32),
            ],
        ),
        out_shape=[
            jax.ShapeDtypeStruct((tokens, heads * HEAD_DIM), BF),
            jax.ShapeDtypeStruct((heads, HEAD_DIM, tokens), F32),
            jax.ShapeDtypeStruct((heads, tokens), F32),
            jax.ShapeDtypeStruct((heads, BQ), F32),
        ],
        compiler_params=pltpu.CompilerParams(
            dimension_semantics=("arbitrary",), vmem_limit_bytes=32 << 20
        ),
        cost_estimate=pl.CostEstimate(
            flops=heads * tokens * tokens * HEAD_DIM * 4,
            bytes_accessed=heads * tokens * 1024,
            transcendentals=heads * tokens * tokens // 2,
        ),
        name="attend",
    )(count, listed, owned, proj, q_mark, k_mark)


def attend_back_kernel(
    count, listed, owned, proj, q_mark, k_mark, up, out_wide, lse, grads, kx, kt, vs, qx, dk_s, dv_s, dq_s
):
    step = pl.program_id(0)
    q_first = step * BQ
    local = dq_s.shape[0]
    last = local - 1
    width = local * HEAD_DIM
    here = pl.ds(pl.multiple_of(q_first, BQ), BQ)

    for h in range(local):
        kx[h, here, :] = jnp.concatenate([proj[:, head_cols(1, h, local)], k_mark[...]], axis=1)
        query = proj[:, head_cols(0, h, local)] * jnp.asarray(HEAD_DIM ** (-0.5), BF)
        qx[h] = jnp.concatenate([query, q_mark[...]], axis=1)
        vs[h, here, :] = proj[:, head_cols(2, h, local)]
        dk_s[h, here, :] = jnp.zeros((BQ, HEAD_DIM), F32)
        dv_s[h, here, :] = jnp.zeros((BQ, HEAD_DIM), F32)
    kt[:, here] = proj[:, width : 2 * width].T

    def heads(group):
        parts = {}
        for h in group:
            rows_up = up[:, h * HEAD_DIM : (h + 1) * HEAD_DIM]
            cols_up = rows_up.astype(F32).T
            delta = jnp.sum(out_wide[h] * cols_up, axis=0, keepdims=True)
            parts[h] = (rows_up, cols_up.astype(BF), delta, lse[h : h + 1, :])
            dq_s[h] = jnp.zeros((HEAD_DIM, BQ), F32)

        def some(h, blocks, diagonal):
            rows_up, cols_up, delta, norm = parts[h]
            rows = [pl.ds(pl.multiple_of(kb * BK, BK), BK) for kb in blocks]
            probs = [jnp.exp(score_block(kx[h, r, :], qx[h]) - norm) for r in rows]
            if diagonal:
                probs[0] = jnp.where(causal(blocks[0] * BK, q_first), probs[0], 0.0)
            dprobs = [jnp.dot(vs[h, r, :], cols_up, preferred_element_type=F32) for r in rows]
            dscores = [(p * (d - delta)).astype(BF) for p, d in zip(probs, dprobs)]
            for r, p, d in zip(rows, probs, dscores):
                dv_s[h, r, :] += jnp.dot(p.astype(BF), rows_up, preferred_element_type=F32)
                dk_s[h, r, :] += jnp.dot(d, qx[h][:, :HEAD_DIM], preferred_element_type=F32)
            dq_s[h] += sum(
                jnp.dot(
                    kt[h * HEAD_DIM : (h + 1) * HEAD_DIM, r], d, preferred_element_type=F32
                )
                for r, d in zip(rows, dscores)
            )

        in_blocks(count, listed, step, group, some)

    heads(range(last))

    @pl.when(owned[step] > 0)
    def _():
        heads([last])

    @pl.when(owned[step] == 0)
    def _():
        dq_s[last] = jnp.zeros((HEAD_DIM, BQ), F32)

    for h in range(local):
        grads[here, h * HEAD_DIM : (h + 1) * HEAD_DIM] = (
            dq_s[h] * (HEAD_DIM ** (-0.5))
        ).T.astype(BF)

    @pl.when(step == pl.num_programs(0) - 1)
    def _():
        for h in range(local):
            at = width + h * HEAD_DIM
            grads[:, at : at + HEAD_DIM] = dk_s[h].astype(BF)
            at = 2 * width + h * HEAD_DIM
            grads[:, at : at + HEAD_DIM] = dv_s[h].astype(BF)


def attend_back(count, listed, owned, proj, q_mark, k_mark, up, out_wide, lse):
    tokens, width = proj.shape
    heads = width // (3 * HEAD_DIM)
    return pl.pallas_call(
        attend_back_kernel,
        grid_spec=pltpu.PrefetchScalarGridSpec(
            num_scalar_prefetch=3,
            grid=(tokens // BQ,),
            in_specs=[
                pl.BlockSpec((BQ, width), lambda i, *_: (i, 0)),
                pl.BlockSpec((BQ, q_mark.shape[1]), lambda i, *_: (i, 0)),
                pl.BlockSpec((BQ, k_mark.shape[1]), lambda i, *_: (i, 0)),
                pl.BlockSpec((BQ, heads * HEAD_DIM), lambda i, *_: (i, 0)),
                pl.BlockSpec((heads, HEAD_DIM, BQ), lambda i, *_: (0, 0, i)),
                pl.BlockSpec((heads, BQ), lambda i, *_: (0, i)),
            ],
            out_specs=whole_block((tokens, width)),
            scratch_shapes=[
                pltpu.VMEM((heads, tokens, LANES), BF),
                pltpu.VMEM((heads * HEAD_DIM, tokens), BF),
                pltpu.VMEM((heads, tokens, HEAD_DIM), BF),
                pltpu.VMEM((heads, BQ, LANES), BF),
                pltpu.VMEM((heads, tokens, HEAD_DIM), F32),
                pltpu.VMEM((heads, tokens, HEAD_DIM), F32),
                pltpu.VMEM((heads, HEAD_DIM, BQ), F32),
            ],
        ),
        out_shape=jax.ShapeDtypeStruct((tokens, width), BF),
        compiler_params=pltpu.CompilerParams(
            dimension_semantics=("arbitrary",), vmem_limit_bytes=44 << 20
        ),
        cost_estimate=pl.CostEstimate(
            flops=heads * tokens * tokens * HEAD_DIM * 10,
            bytes_accessed=heads * tokens * 2048,
            transcendentals=heads * tokens * tokens // 2,
        ),
        name="attend_back",
    )(count, listed, owned, proj, q_mark, k_mark, up, out_wide, lse)


def head_split(matrix, parts):
    rows, cols = matrix.shape
    heads = cols // (parts * HEAD_DIM)
    each = heads // GROUP
    cube = matrix.reshape(rows, parts, heads, HEAD_DIM)
    own = cube[:, :, : each * GROUP].reshape(rows, parts, GROUP, each, HEAD_DIM)
    rest = jnp.broadcast_to(
        cube[:, :, None, each * GROUP :], (rows, parts, GROUP, heads - each * GROUP, HEAD_DIM)
    )
    joined = jnp.concatenate([own, rest], axis=3)
    return jnp.transpose(joined, (2, 0, 1, 3, 4)).reshape(GROUP, rows, -1)


def head_join(shares, parts, heads):
    group, rows, _ = shares.shape
    each = heads // GROUP
    cube = shares.astype(F32).reshape(group, rows, parts, -1, HEAD_DIM)
    own = jnp.transpose(cube[:, :, :, :each], (1, 2, 0, 3, 4)).reshape(
        rows, parts, each * GROUP, HEAD_DIM
    )
    rest = jnp.sum(cube[:, :, :, each:], axis=0)
    return jnp.concatenate([own, rest], axis=2).reshape(rows, -1)


def hidden_split(matrix, unit):
    rows = matrix.shape[0]
    cube = matrix.reshape(rows, -1, GROUP, unit)
    return jnp.transpose(cube, (2, 0, 1, 3)).reshape(GROUP, rows, -1)


def hidden_join(shares, unit):
    group, rows, _ = shares.shape
    cube = shares.reshape(group, rows, -1, unit)
    return jnp.transpose(cube, (1, 2, 0, 3)).reshape(rows, -1)


def exchange(shares):
    return lax.all_to_all(shares, PLANE, split_axis=0, concat_axis=0, tiled=True)


def take(stack, place):
    return lax.dynamic_index_in_dim(stack, place, 0, keepdims=False)


def columns_start(shard, width, split):
    if shard.size % width == 0:
        mine = exchange(split(shard.reshape(-1, width)))
        return mine.reshape(-1, mine.shape[-1])
    return shard


def columns_end(rows, size, width, split, place):
    if size % width == 0:
        return lax.all_gather(rows, TREE, axis=0, tiled=True)
    full = lax.all_gather(rows, EVERY, axis=0, tiled=True).reshape(-1, width)
    return take(split(full), place)


def columns_first(grad, size, width):
    if size % width == 0:
        rows = lax.psum_scatter(grad, TREE, scatter_dimension=0, tiled=True)
        return rows.reshape(GROUP, -1, rows.shape[-1])
    return grad


def columns_second(slots, join, shard_shape, width, place):
    if shard_shape[0] * shard_shape[1] % width == 0:
        return join(slots).astype(F32).reshape(shard_shape)
    spots = jnp.arange(GROUP, dtype=jnp.int32)[:, None, None] == place
    shares = jnp.where(spots, slots[None], jnp.zeros((), BF))
    full = join(shares).astype(BF).reshape(-1, shard_shape[1])
    return lax.psum_scatter(full, EVERY, scatter_dimension=0, tiled=True).astype(F32)


def owner_rows(share, trees):
    t, p, i = (
        lax.broadcasted_iota(jnp.int32, (trees, GROUP, share), dim) for dim in range(3)
    )
    return (t * GROUP + p) * share + i


def slots_out(columns, own, share, place):
    rows = owner_rows(share, lax.axis_size(TREE)) - place * own
    numbers = jnp.arange(own, dtype=jnp.int32)
    pick = jnp.any(rows[..., None] == numbers, axis=0).reshape(-1, own).astype(BF)
    slots = lax.dot_general(
        pick, columns[:, :own], (((1,), (1,)), ((), ())), preferred_element_type=F32
    )
    return slots.astype(BF).reshape(GROUP, share, -1)


def slots_in(slots, own, share, place, padded):
    trees = lax.axis_size(TREE)
    rows = take(jnp.swapaxes(owner_rows(share, trees), 0, 1), place)
    total = jnp.zeros((trees,) + slots.shape[1:], slots.dtype)
    for source in range(GROUP):
        held = (rows >= source * own) & (rows < (source + 1) * own)
        total = jnp.where(held[:, :, None], slots[source][None], total)
    return jnp.pad(total, ((0, 0), (0, padded - share), (0, 0))).reshape(trees * padded, -1)


def on_device(
    tokens,
    cotangent,
    w_qkv,
    w_out,
    w_fc,
    w_proj,
    ln1_gain,
    ln1_bias,
    q_bias,
    v_bias,
    out_bias,
    ln2_gain,
    ln2_bias,
    fc_bias,
    proj_bias,
    seg_lengths,
    parents,
):
    tok_dev, model_width = tokens.shape
    hidden = fc_bias.shape[0]
    flat_cols = w_qkv.shape[1]
    heads = model_width // HEAD_DIM
    each = heads // GROUP
    rest = heads - each * GROUP
    local = each + rest
    tree = lax.axis_index(TREE)
    place = (lax.axis_index("a") * 2 + lax.axis_index("b")) * 2 + lax.axis_index("c")
    device = tree * GROUP + place
    unit = max(1, hidden // lax.axis_size(EVERY))

    starts, ends, reach = tree_tables(take(seg_lengths, tree), take(parents, tree))
    position = jnp.arange(TREE_TOK, dtype=jnp.int32)
    hot = (
        (position[:, None] >= starts[None, :]) & (position[:, None] < ends[None, :])
    ).astype(F32)
    path = jnp.dot(hot, reach, preferred_element_type=F32)
    q_blocks, k_blocks = TREE_TOK // BQ, TREE_TOK // BK
    count, listed = block_lists(hot, path, q_blocks, k_blocks)
    block_numbers = jnp.arange(q_blocks, dtype=jnp.int32)
    turn = q_blocks - 1 - block_numbers
    owner = jnp.where(turn < GROUP, turn, 2 * GROUP - 2 - turn)
    owned = (owner == place).astype(jnp.int32)
    pad = LANES - HEAD_DIM - hot.shape[1]
    k_mark = jnp.pad(hot, ((0, 0), (0, pad))).astype(BF)
    q_mark = jnp.pad((1.0 - path) * NEGATIVE, ((0, 0), (0, pad))).astype(BF)

    residual_in = tokens.astype(F32)
    first_norm, normed_one, inv_one = norm_forward(residual_in, ln1_gain, ln1_bias)
    first_own = first_norm.astype(BF)
    qkv_split, fc_split = partial(head_split, parts=3), partial(hidden_split, unit=unit)
    qkv_rows = columns_start(after(w_qkv, first_own), 3 * model_width, qkv_split)
    w_qkv_l = columns_end(qkv_rows, w_qkv.size, 3 * model_width, qkv_split, place)
    qkv_bias = jnp.concatenate([q_bias, jnp.zeros_like(q_bias), v_bias])
    qkv_bias_l = take(head_split(qkv_bias[None], 3), place)[0]
    first_low, _ = plane_gather(first_own, place)

    two_far = plane_fetch(after(cotangent, first_low))
    whole_rows = w_out.size % model_width == 0
    ratio = model_width // flat_cols
    w_out_full = lax.all_gather(after(w_out, first_low), EVERY, axis=0, tiled=True)
    w_out_l = jnp.concatenate(
        [
            block_of(w_out_full, place, each * HEAD_DIM * ratio),
            w_out_full[each * GROUP * HEAD_DIM * ratio :],
        ],
        axis=0,
    ).reshape(-1, model_width)
    proj_whole = w_proj.size % model_width == 0
    if proj_whole:
        w_proj_l = lax.all_gather(
            after(w_proj.reshape(-1, model_width), first_low), TREE, axis=0, tiled=True
        )
    else:
        proj_full = lax.all_gather(w_proj, EVERY, axis=0, tiled=True).reshape(hidden, model_width)
        w_proj_l = take(
            jnp.transpose(proj_full.reshape(-1, GROUP, unit, model_width), (1, 0, 2, 3)), place
        ).reshape(-1, model_width)
    fc_bias_l = take(hidden_split(fc_bias[None], unit), place)[0]
    projected = (jnp.dot(first_low, w_qkv_l, preferred_element_type=F32) + qkv_bias_l).astype(BF)

    fc_rows = columns_start(after(w_fc, projected), hidden, fc_split)
    attended, out_wide, lse, tops = attend(count, listed, owned, projected, q_mark, k_mark)
    attended, two_far, fc_rows = lax.optimization_barrier((attended, two_far, fc_rows))
    w_fc_l = columns_end(fc_rows, w_fc.size, hidden, fc_split, place)
    branch = jnp.dot(attended, w_out_l, preferred_element_type=F32).astype(BF)
    mid_sum, mid_last = plane_scatter(branch, place)
    two_blocks = after((cotangent,) + two_far, *mid_last)
    grad_two = plane_write(two_blocks, [swap(block, "c") for block in two_blocks], place, None)
    middle = residual_in + mid_sum + out_bias

    second_norm, normed_two, inv_two = norm_forward(middle, ln2_gain, ln2_bias)
    second_own = second_norm.astype(BF)
    second_low, _ = plane_gather(second_own, place, branch)
    own_slots = ()
    if whole_rows:
        share = w_out.size // model_width
        own_slots = slots_out(after(attended, second_own), each * HEAD_DIM, share, place)
        own_slots = exchange(after(own_slots, second_low))
    pre_act = jnp.dot(second_low, w_fc_l, preferred_element_type=F32) + fc_bias_l
    activated, gelu_pull = jax.vjp(partial(jax.nn.gelu, approximate=True), pre_act)
    act_low = activated.astype(BF)
    over_cols = lambda left, right: lax.dot_general(
        left, right, (((1,), (1,)), ((), ())), preferred_element_type=F32
    )
    over_rows = lambda left, right: lax.dot_general(
        left, right, (((0,), (0,)), ((), ())), preferred_element_type=F32
    )
    pre_low = gelu_pull(over_cols(grad_two, w_proj_l))[0].astype(BF)
    norm_back = over_cols(pre_low, w_fc_l).astype(BF)
    norm_back, own_slots = lax.optimization_barrier((norm_back, own_slots))
    back_sum, back_last = plane_scatter(norm_back, place)

    grad_out = cotangent.astype(F32)
    proj_bias_grad = jnp.sum(grad_out, axis=0)
    mid_part, ln2_gain_grad, ln2_bias_grad = norm_backward(back_sum, normed_two, inv_two, ln2_gain)
    middle_grad = grad_out + mid_part
    branch_own = middle_grad.astype(BF)
    out_bias_grad = jnp.sum(branch_own.astype(F32), axis=0)

    branch_low, _ = plane_gather(branch_own, place, norm_back)

    fc_low = over_rows(second_low, after(pre_low, branch_own)).astype(BF)
    proj_low = over_rows(after(act_low, branch_own), grad_two).astype(BF)
    branch_two = jnp.dot(
        after(act_low, proj_low), w_proj_l, preferred_element_type=F32
    ).astype(BF)
    attn_back = over_cols(branch_low, w_out_l).astype(BF)
    attn_back = after(attn_back, branch_two)

    two_sum = lax.psum_scatter(
        after(branch_two, branch_low), PLANE, scatter_dimension=0, tiled=True
    )
    fc_rows = columns_first(fc_low, w_fc.size, hidden)
    proj_parts = tree_parts(proj_low) if proj_whole else ()
    qkv_low = attend_back(
        count, listed, owned, projected, q_mark, k_mark, attn_back, out_wide, lse
    )
    qkv_low, fc_rows, proj_parts = lax.optimization_barrier((qkv_low, fc_rows, proj_parts))
    if w_fc.size % hidden == 0:
        fc_rows = exchange(fc_rows)
    first_back = over_cols(qkv_low, w_qkv_l).astype(BF)
    made = []

    def beside(sent):
        made.append(over_rows(first_low, after(qkv_low, two_sum, *sent)).astype(BF))
        return made + [fc_rows]

    in_sum, in_last = plane_scatter(first_back, place, beside)
    qkv_rows = columns_first(made[0], w_qkv.size, 3 * model_width)
    branch_late = after(branch_low, *in_last)
    if whole_rows:
        padded = -(-share // 16) * 16
        out_rows = jnp.dot(
            slots_in(own_slots, each * HEAD_DIM, share, place, padded),
            branch_late,
            preferred_element_type=F32,
        ).astype(BF)
        out_rows = lax.psum_scatter(
            after(out_rows, qkv_rows), TREE, scatter_dimension=0, tiled=True
        )
        common = over_rows(attended[:, each * HEAD_DIM :], branch_late).astype(BF)
    else:
        out_low = over_rows(attended, branch_late).astype(BF)
        common = jnp.zeros((8, LANES), BF)
    in_part, ln1_gain_grad, ln1_bias_grad = norm_backward(in_sum, normed_one, inv_one, ln1_gain)

    fc_bias_part = jnp.sum(after(pre_low, *in_last).astype(F32), axis=0)
    fc_parts = jnp.zeros((GROUP, hidden // GROUP), F32)
    fc_parts = lax.dynamic_update_slice(fc_parts, fc_bias_part[None], (place, 0))
    fc_parts = hidden_join(fc_parts[:, None], unit)[0]
    column_sums = jnp.sum(after(qkv_low, *in_last).astype(F32), axis=0)
    column_sums = column_sums.reshape(3, local, HEAD_DIM)
    bias_parts = jnp.zeros((3, GROUP, each, HEAD_DIM), F32)
    bias_parts = lax.dynamic_update_slice(
        bias_parts, column_sums[:, None, :each], (0, place, 0, 0)
    )
    bias_parts = jnp.concatenate(
        [bias_parts.reshape(3, each * GROUP, HEAD_DIM), column_sums[:, each:]], axis=1
    ).reshape(3, model_width)
    sums = jnp.concatenate(
        [
            ln1_gain_grad,
            ln1_bias_grad,
            bias_parts[0],
            bias_parts[2],
            out_bias_grad,
            ln2_gain_grad,
            ln2_bias_grad,
            proj_bias_grad,
            fc_parts,
        ]
    )
    top_heads = jnp.max(tops, axis=1)
    spread = jnp.full((GROUP, each), NEGATIVE, F32)
    spread = lax.dynamic_update_slice(spread, top_heads[None, :each], (place, 0))
    spread = jnp.concatenate([spread.reshape(-1), top_heads[each:]])
    is_sum = jnp.arange(sums.shape[0] + heads, dtype=jnp.int32) < sums.shape[0]
    combine = lambda left, right: jnp.where(is_sum, left + right, jnp.maximum(left, right))
    sums = jnp.concatenate([sums, spread])

    whole_qkv = w_qkv.size % (3 * model_width) == 0
    combines = [combine, lambda left, right: left + right]
    sums, common = over_plane(lax.optimization_barrier((sums, common)), combines)
    if whole_qkv:
        qkv_rows = exchange(after(qkv_rows, in_sum))
    sums, common, qkv_rows = lax.optimization_barrier((sums, common, qkv_rows))
    sums, common = over_trees([sums, common], combines)
    logit_max = sums[-heads:]
    qkv_shard = columns_second(
        qkv_rows, partial(head_join, parts=3, heads=heads), w_qkv.shape, 3 * model_width, place
    )
    fc_shard = columns_second(
        after(fc_rows, sums), partial(hidden_join, unit=unit), w_fc.shape, hidden, place
    )
    if whole_rows:
        rows = device * share + jnp.arange(share, dtype=jnp.int32) - GROUP * each * HEAD_DIM
        numbers = jnp.arange(common.shape[0], dtype=jnp.int32)
        pick = (rows[:, None] == numbers[None, :]).astype(BF)
        out_shard = out_rows[:share].astype(F32) + jnp.dot(
            pick, common, preferred_element_type=F32
        )
        out_shard = out_shard.reshape(w_out.shape)
    else:
        out_zero = jnp.zeros((each * GROUP * HEAD_DIM, model_width), BF)
        out_rows = jnp.concatenate(
            [
                lax.dynamic_update_slice(
                    out_zero, out_low[: each * HEAD_DIM], (place * each * HEAD_DIM, 0)
                ),
                out_low[each * HEAD_DIM :],
            ],
            axis=0,
        ).reshape(-1, flat_cols)
        out_shard = lax.psum_scatter(out_rows, EVERY, scatter_dimension=0, tiled=True).astype(F32)
    if proj_whole:
        proj_shard = sum(part.astype(F32) for part in after(proj_parts, in_sum))
        proj_shard = proj_shard.reshape(w_proj.shape)
    else:
        spots = jnp.arange(GROUP, dtype=jnp.int32)[None, :, None, None] == place
        proj_rows = jnp.where(
            spots, proj_low.reshape(-1, 1, unit, model_width), jnp.zeros((), BF)
        ).reshape(-1, flat_cols)
        proj_shard = lax.psum_scatter(proj_rows, EVERY, scatter_dimension=0, tiled=True).astype(F32)
    input_grad = middle_grad + in_part
    output = (middle + after(two_sum, sums).astype(F32) + proj_bias).astype(BF)

    cut = lambda array, i: array[i * model_width : (i + 1) * model_width]
    small = (
        *(cut(sums, i) for i in range(7)),
        sums[8 * model_width : -heads],
        cut(sums, 7),
    )

    clip_gain = jnp.sqrt(TAU / jnp.maximum(logit_max, TAU))
    rows_dev = w_qkv.shape[0]
    flat_index = (after(device, in_sum) * rows_dev + jnp.arange(rows_dev, dtype=jnp.int32)[:, None]) * flat_cols
    flat_index = flat_index + jnp.arange(flat_cols, dtype=jnp.int32)[None, :]
    column = flat_index % (3 * model_width)
    head_of = column % model_width // HEAD_DIM
    head_numbers = jnp.arange(heads, dtype=jnp.int32)
    head_gain = jnp.sum(
        jnp.where(
            head_of[:, :, None] == head_numbers[None, None, :], clip_gain[None, None, :], 0.0
        ),
        axis=2,
    )
    factor = jnp.where(column < 2 * model_width, head_gain, 1.0)
    clipped = (w_qkv.astype(F32) * factor).astype(BF)
    return (
        output,
        input_grad,
        qkv_shard,
        out_shard,
        fc_shard,
        proj_shard,
        *small,
        logit_max,
        clipped,
    )


def solution(mesh):
    split = Mesh(mesh.devices.reshape(-1, 2, 2, 2), EVERY)
    rows = P(EVERY, None)
    return jax.shard_map(
        on_device,
        mesh=split,
        in_specs=(rows,) * 6 + (P(),) * 11,
        out_specs=(rows,) * 6 + (P(),) * 10 + (rows,),
        check_vma=False,
    )
```

time: 1000 us -> 719 us (0.72)
  waiting for transfers between devices: 369 us -> 181 us
  blocking collectives: 71.1 us -> 16.5 us
  local copies, waits for them, and re-layouts: 186 us -> 137 us
  starting transfers between devices: 53.3 us -> 74 us
  Pallas kernels: 102 us -> 84.6 us
    psum x1 -> x0, waiting for transfers between devices: 101 us -> none  [on_device(): lax.psum((ln1_gain_grad, ln1_bias_grad, bias_parts[0], bias_parts[2], out...]
    ppermute x64 -> x54, waiting for transfers between devices: 207 us -> 136 us  [swap(): return lax.ppermute(value, axis, [(0, 1), (1, 0)])]
    unnamed x173 -> x143, local copies, waits for them, and re-layouts: 87.1 us -> 25.6 us
    pmax x1 -> x0, blocking collectives: 54.5 us -> none  [on_device(): lax.pmax(jnp.concatenate([spread.reshape(-1), top_heads[each:]]), EVERY)]
    all_to_all x3 -> x4, waiting for transfers between devices: 59.8 us -> 8.58 us  [exchange(): lax.all_to_all(shares, PLANE, split_axis=0, concat_axis=0, tiled=True)]
    dynamic_update_slice x1 -> x30, local copies, waits for them, and re-layouts: 0.08 us -> 46.2 us  [plane_write(): full = lax.dynamic_update_slice_in_dim(full, piece, (place ^ q) * rows, 0)]
    all_gather x4, waiting for transfers between devices: 0.03 us -> 26.1 us  [the longest x1 26.1 us: on_device(): lax.all_gather(after(w_out, first_low), EVERY, axis=0, tiled=True)]
    ppermute x0 -> x14, starting transfers between devices: none -> 21.6 us  [the longest x10 15.2 us: pairwise(): others = [lax.ppermute(value, axis, pairs) for value in values]]
  transfers between devices with their start and end apart: 76 -> 80, of which waited for: 31 -> 28; matrix products, arithmetic and copies ran while one was open for 33% -> 40% of each run, Pallas kernels for 10% -> 12%
where the time goes in v2:
time: 719 us; the launch traced here: 709 us
  waiting for transfers between devices  181 us (25%)
  local copies, waits for them, and re-layouts  137 us (19%)
  matrix products  137 us (19%)
  Pallas kernels  84.6 us (12%)
  starting transfers between devices  74 us (10%)
  other arithmetic  62.9 us (9%)
  blocking collectives  16.5 us (2%)
  between operations  16 us (2%)
    ppermute x54, waiting for transfers between devices, swap(): return lax.ppermute(value, axis, [(0, 1), (1, 0)])  136 us
    dynamic_update_slice x30, local copies, waits for them, and re-layouts, plane_write(): full = lax.dynamic_update_slice_in_dim(full, piece, (place ^ q) * rows, 0)  46.2 us
    pallas_call x1, Pallas kernels, attend_back(): pl.pallas_call(attend_back_kernel, grid_spec=pltpu.PrefetchScalarGridSpec...  44.6 us
    dot_general x4, matrix products, on_device(): lax.dot_general(left, right, (((1,), (1,)), ((), ())), preferred_element_...  43.2 us
    dot_general x4, matrix products, on_device(): lax.dot_general(left, right, (((0,), (0,)), ((), ())), preferred_element_...  42.8 us
    pallas_call x1, Pallas kernels, attend(): pl.pallas_call(attend_kernel, grid_spec=pltpu.PrefetchScalarGridSpec(num_...  40.1 us
    ppermute x54, starting transfers between devices, swap(): return lax.ppermute(value, axis, [(0, 1), (1, 0)])  34.9 us
    all_gather x1, waiting for transfers between devices, on_device(): lax.all_gather(after(w_out, first_low), EVERY, axis=0, tiled=True)  26.1 us
  transfers between devices with their start and end apart: 80, of which 28 were waited for; matrix products, arithmetic and copies ran while one was open for 40% of the time, Pallas kernels for 12%

profile of v2, /device:TPU:0, one launch (start us, length us, event | category | flops | bytes accessed | tf_op | source)
XLA Modules:
  0.0 708.6 jit_solution(100393119949491647)
XLA Ops:
  13.2 3.4 copy-done.16
  21.7 16.5 %all_to_all.25 = bf16[8,50,768]{2,1,0:T(8,128)(2,1)S(1)} all-to-all(bf16[8,50,768]{2,1,0:T(8,128)(2,1)S(1)} %reshape.574), channel_id=1, replica_groups=mesh['t'=4,'a'=2,'b'=2,'c'=2] {'a','b','c'}, dimensions={0} | all-to-all | bytes 1228800 | tf_op jit(solution)/shard_map/all_to_all | solution.py:483
  40.6 24.1 %collective-permute-done.1 = bf16[320,1600]{1,0:T(8,128)(2,1)S(1)} collective-permute-done((bf16[320,1600]{1,0:T(8,128)(2,1)}, bf16[320,1600]{1,0:T(8,128)(2,1)S(1)}, u32[]{:S(2)}, u32[]{:S(2)}) %collective-permute-start.1) | collective-permute-done | bytes 1024032 | tf_op jit(solution)/shard_map/ppermute | solution.py:49
  70.0 9.4 %collective-permute-done.5 = bf16[160,1600]{1,0:T(8,128)(2,1)S(1)} collective-permute-done((bf16[160,1600]{1,0:T(8,128)(2,1)S(1)}, bf16[160,1600]{1,0:T(8,128)(2,1)S(1)}, u32[]{:S(2)}, u32[]{:S(2)}) %collective-permute-start.5) | collective-permute-done | bytes 512032 | tf_op jit(solution)/shard_map/ppermute | solution.py:49
  93.7 11.8 %add_convert_fusion.proj = bf16[2560,768]{1,0:T(8,128)(2,1)} fusion(bf16[2560,1600]{1,0:T(8,128)(2,1)} %constant_dynamic-update-slice_fusion.25, bf16[1600,768]{1,0:T(8,128)(2,1)} %all-gather.5.cloned.1.call-done, f32[768]{0:T(1024)S(1)} %fusion.53), kind=kOutput, calls=%fused_computation.18 | convolution fusion | flops 6295388160 | bytes 14584832 | tf_op jit(solution)/shard_map/dot_general | solution.py:626
  108.0 3.5 all-to-all-start.1
  113.9 40.1 %attend.1 = (bf16[2560,256]{1,0:T(8,128)(2,1)S(1)}, f32[4,64,2560]{2,1,0:T(8,128)S(1)}, f32[4,2560]{1,0:T(4,128)S(1)}, f32[4,256]{1,0:T(4,128)S(1)}) custom-call(s32[10]{0:T(128)S(1)} %fusion.58.count, s32[10,10]{1,0:T(8,128)S(1)} %select_reduce_fusion.1.listed, s32[10]{0:T(128)S(1)} %compare_convert_fusion.3.owned, bf16[2560,768]{1,0:T(8,128)(2,1)S(1)} %copy-done.4, ...), custom_call_target="tpu_custom_call" | custom-call | flops 6710886400 | bytes 10485760 | tf_op jit(solution)/shard_map/attend/pallas_call | solution.py:291
  157.1 26.1 %all-gather.7.cloned.1.call-done = bf16[12800,200]{1,0:T(8,128)(2,1)} async-done(((bf16[400,200]{1,0:T(8,128)(2,1)}), bf16[12800,200]{1,0:T(8,128)(2,1)}) %all-gather.7.cloned.1.call-update) | async-done | bytes 5120016 | tf_op jit(solution)/shard_map/all_gather | solution.py:607
  190.3 3.5 constant_dynamic-slice_fusion.22
  204.3 11.4 %collective-permute-done.16 = bf16[160,1600]{1,0:T(8,128)(2,1)S(1)} collective-permute-done((bf16[160,1600]{1,0:T(8,128)(2,1)S(1)}, bf16[160,1600]{1,0:T(8,128)(2,1)S(1)}, u32[]{:S(2)}, u32[]{:S(2)}) %collective-permute-start.16) | collective-permute-done | bytes 512032 | tf_op jit(solution)/shard_map/ppermute | solution.py:49
  226.1 3.9 broadcast.461
  232.5 10.9 %collective-permute-done.17 = bf16[320,1600]{1,0:T(8,128)(2,1)} collective-permute-done((bf16[320,1600]{1,0:T(8,128)(2,1)}, bf16[320,1600]{1,0:T(8,128)(2,1)}, u32[]{:S(2)}, u32[]{:S(2)}) %collective-permute-start.17) | collective-permute-done | bytes 1024032 | tf_op jit(solution)/shard_map/ppermute | solution.py:49
  244.4 2.9 fusion.60
  264.5 10.6 %collective-permute-done.20 = bf16[320,1600]{1,0:T(8,128)(2,1)} collective-permute-done((bf16[320,1600]{1,0:T(8,128)(2,1)}, bf16[320,1600]{1,0:T(8,128)(2,1)}, u32[]{:S(2)}, u32[]{:S(2)}) %collective-permute-start.20) | collective-permute-done | bytes 1024032 | tf_op jit(solution)/shard_map/ppermute | solution.py:49
  286.9 6.7 collective-permute-done.24
  304.2 4.4 all-to-all-start.2
  308.8 13.0 %fusion.67 = f32[2560,800]{0,1:T(8,128)} fusion(bf16[2560,1600]{1,0:T(8,128)(2,1)} %constant_dynamic-update-slice_fusion.17, bf16[1600,800]{1,0:T(8,128)(2,1)} %all-gather.9.cloned.1.call-done), kind=kOutput, calls=%fused_computation.289 | convolution fusion | flops 6553600000 | bytes 18944000 | tf_op jit(solution)/shard_map/dot_general | solution.py:646
  321.8 17.9 %fusion.6 = (bf16[2560,800]{0,1:T(8,128)(2,1)S(1)}, bf16[2560,800]{0,1:T(8,128)(2,1)}) fusion(f32[2560,800]{0,1:T(8,128)} %fusion.67, f32[800]{0:T(1024)S(1)} %fusion.52, bf16[2560,1600]{1,0:T(8,128)(2,1)} %constant_dynamic-update-slice_fusion.9, bf16[800,1600]{1,0:T(8,128)(2,1)} %all-gather.11.cloned.1.call-done), kind=kOutput, calls=%fused_computation.14 | convolution fusion | flops 6600704000 | bytes 27139200 | tf_op jit(solution)/shard_map/dot_general | solution.py:649
  341.7 12.1 %convolution_convert_fusion.2 = bf16[2560,1600]{1,0:T(8,128)(2,1)} fusion(bf16[2560,800]{0,1:T(8,128)(2,1)S(1)} %get-tuple-element.177, bf16[1600,800]{1,0:T(8,128)(2,1)S(1)} %copy-done.61), kind=kOutput, calls=%fused_computation.6 | convolution fusion | flops 6557696000 | bytes 14848000 | tf_op jit(solution)/shard_map/dot_general | solution.py:649
  353.7 4.1 constant_dynamic-slice_fusion.13
  365.0 10.4 %collective-permute-done.36 = bf16[160,1600]{1,0:T(8,128)(2,1)S(1)} collective-permute-done((bf16[160,1600]{1,0:T(8,128)(2,1)S(1)}, bf16[160,1600]{1,0:T(8,128)(2,1)S(1)}, u32[]{:S(2)}, u32[]{:S(2)}) %collective-permute-start.36) | collective-permute-done | bytes 512032 | tf_op jit(solution)/shard_map/ppermute | solution.py:49
  380.2 21.5 %collective-permute-done.37 = bf16[320,1600]{1,0:T(8,128)(2,1)S(1)} collective-permute-done((bf16[320,1600]{1,0:T(8,128)(2,1)S(1)}, bf16[320,1600]{1,0:T(8,128)(2,1)S(1)}, u32[]{:S(2)}, u32[]{:S(2)}) %collective-permute-start.37) | collective-permute-done | bytes 1024032 | tf_op jit(solution)/shard_map/ppermute | solution.py:49
  404.4 4.5 convert_reduce_fusion.4
  411.2 10.9 %convolution_convert_fusion.6 = bf16[1600,800]{1,0:T(8,128)(2,1)} fusion(bf16[2560,1600]{1,0:T(8,128)(2,1)S(1)} %bitcast.115, bf16[2560,800]{0,1:T(8,128)(2,1)S(1)} %copy-done.22), kind=kOutput, calls=%fused_computation.21 | convolution fusion | flops 6554880000 | bytes 14848000 | tf_op jit(solution)/shard_map/dot_general | solution.py:652
  422.2 13.5 %convolution_convert_fusion.7 = bf16[800,1600]{1,0:T(8,128)(2,1)} fusion(bf16[2560,800]{0,1:T(8,128)(2,1)} %get-tuple-element.151, bf16[2560,1600]{1,0:T(8,128)(2,1)} %constant_dynamic-update-slice_fusion.9), kind=kOutput, calls=%fused_computation.22 | convolution fusion | flops 6554880000 | bytes 14848000 | tf_op jit(solution)/shard_map/dot_general | solution.py:652
  435.7 11.8 %convolution_convert_fusion.1 = bf16[2560,1600]{1,0:T(8,128)(2,1)} fusion(bf16[2560,800]{0,1:T(8,128)(2,1)S(1)} %copy-done.63, bf16[800,1600]{1,0:T(8,128)(2,1)S(1)} %copy-done.62), kind=kOutput, calls=%fused_computation.5 | convolution fusion | flops 6557696000 | bytes 14848000 | tf_op jit(solution)/shard_map/dot_general | solution.py:671
  456.8 7.5 %collective-permute-done.44 = bf16[160,1600]{1,0:T(8,128)(2,1)S(1)} collective-permute-done((bf16[160,1600]{1,0:T(8,128)(2,1)S(1)}, bf16[160,1600]{1,0:T(8,128)(2,1)S(1)}, u32[]{:S(2)}, u32[]{:S(2)}) %collective-permute-start.44) | collective-permute-done | bytes 512032 | tf_op jit(solution)/shard_map/ppermute | solution.py:49
  485.7 44.6 %attend_back.1 = bf16[2560,768]{1,0:T(8,128)(2,1)S(1)} custom-call(s32[10]{0:T(128)S(1)} %fusion.58.count, s32[10,10]{1,0:T(8,128)S(1)} %select_reduce_fusion.1.listed, s32[10]{0:T(128)S(1)} %compare_convert_fusion.3.owned, bf16[2560,768]{1,0:T(8,128)(2,1)} %add_convert_fusion.proj, bf16[2560,64]{1,0:T(8,128)(2,1)S(1)} %pad.15.q_mark, ...), custom_call_target="tpu_custom_call" | custom-call | flops 16777216000 | bytes 20971520 | tf_op jit(solution)/shard_map/attend_back/pallas_call | solution.py:409
  535.7 10.5 %convolution_convert_fusion = bf16[2560,1600]{1,0:T(8,128)(2,1)S(1)} fusion(bf16[2560,768]{1,0:T(8,128)(2,1)} %copy-done.2, bf16[1600,768]{1,0:T(8,128)(2,1)} %all-gather.5.cloned.1.call-done), kind=kOutput, calls=%fused_computation.4 | convolution fusion | flops 6295552000 | bytes 14581760 | tf_op jit(solution)/shard_map/dot_general | solution.py:649
  549.8 4.2 all-to-all-start.3
  554.3 12.6 %convolution_convert_fusion.8 = bf16[1600,768]{1,0:T(8,128)(2,1)} fusion(bf16[2560,1600]{1,0:T(8,128)(2,1)} %constant_dynamic-update-slice_fusion.25, bf16[2560,768]{1,0:T(8,128)(2,1)} %copy-done.2), kind=kOutput, calls=%fused_computation.23 | convolution fusion | flops 6292684800 | bytes 14581760 | tf_op jit(solution)/shard_map/dot_general | solution.py:652
  575.0 9.4 %collective-permute-done.55 = bf16[160,1600]{1,0:T(8,128)(2,1)S(1)} collective-permute-done((bf16[160,1600]{1,0:T(8,128)(2,1)S(1)}, bf16[160,1600]{1,0:T(8,128)(2,1)S(1)}, u32[]{:S(2)}, u32[]{:S(2)}) %collective-permute-start.55) | collective-permute-done | bytes 512032 | tf_op jit(solution)/shard_map/ppermute | solution.py:49
  589.9 5.8 convolution_convert_fusion.10
  596.5 2.9 convert_reduce_fusion
  600.4 7.9 %convolution_convert_fusion.9 = bf16[256,1600]{0,1:T(8,128)(2,1)} fusion(bf16[256,2560]{1,0:T(8,128)(2,1)S(1)} %bitcast.121, bf16[2560,1600]{1,0:T(8,128)(2,1)} %constant_dynamic-update-slice_fusion.1), kind=kOutput, calls=%fused_computation.29 | convolution fusion | flops 2097561600 | bytes 10321920 | tf_op jit(solution)/shard_map/dot_general | solution.py:700
  608.3 3.7 collective-permute-done.56
  613.3 3.9 fusion.16
  619.8 3.9 fusion.19
  626.3 3.2 collective-permute-done.59
  640.4 3.5 all-to-all-start.4
  647.2 8.2 %all-to-all-done.4 = bf16[8,50,768]{2,1,0:T(8,128)(2,1)S(1)} async-done(((bf16[8,50,768]{2,1,0:T(8,128)(2,1)}), bf16[8,50,768]{2,1,0:T(8,128)(2,1)S(1)}, u32[]{:S(2)}, u32[]{:S(2)}) %all-to-all-start.4) | async-done | bytes 614432 | tf_op jit(solution)/shard_map/all_to_all | solution.py:483
  655.3 5.4 collective-permute-start.64
  669.0 3.2 reshape_reshape.11
  672.3 2.8 copy.186
  675.1 3.3 collective-permute-done.65
  685.9 2.9 reshape.576
  692.0 3.4 collective-permute-start.67
  696.1 3.1 collective-permute-done.67
  (507 shorter events, 227.8 us)
Async XLA Ops:
  7.2 86.5 %all-gather.5.cloned.1.call-start = ((), (), s32[]{:S(2)}) async-start(), calls=%async_computation.9 | async-start | bytes 3072000 | tf_op jit(solution)/shard_map/all_gather | solution.py:499
  39.2 144.0 %all-gather.7.cloned.1.call-start = ((), (), s32[]{:S(2)}) async-start(), calls=%async_computation.10 | async-start | bytes 6758400 | tf_op jit(solution)/shard_map/all_gather | solution.py:607
  39.4 25.3 %collective-permute-start.1 = (bf16[320,1600]{1,0:T(8,128)(2,1)}, bf16[320,1600]{1,0:T(8,128)(2,1)S(1)}, u32[]{:S(2)}, u32[]{:S(2)}) collective-permute-start(bf16[320,1600]{1,0:T(8,128)(2,1)} %get-tuple-element.321), channel_id=1, source_target_pairs={{0,2},{2,0},{1,3},{3,1},{4,6},{6,4},{5,7},{7,5},{8,10},{10,8},{9,1... | collective-permute-start | bytes 3072008 | tf_op jit(solution)/shard_map/ppermute | solution.py:49
  40.1 25.4 %collective-permute-start.3 = (bf16[320,1600]{1,0:T(8,128)(2,1)}, bf16[320,1600]{1,0:T(8,128)(2,1)S(1)}, u32[]{:S(2)}, u32[]{:S(2)}) collective-permute-start(bf16[320,1600]{1,0:T(8,128)(2,1)} %get-tuple-element.321), channel_id=1, source_target_pairs={{0,4},{4,0},{1,5},{5,1},{2,6},{6,2},{3,7},{7,3},{8,12},{12,8},{9,1... | collective-permute-start | bytes 3072008 | tf_op jit(solution)/shard_map/ppermute | solution.py:49
  40.6 26.0 %collective-permute-start = (bf16[320,1600]{1,0:T(8,128)(2,1)}, bf16[320,1600]{1,0:T(8,128)(2,1)}, u32[]{:S(2)}, u32[]{:S(2)}) collective-permute-start(bf16[320,1600]{1,0:T(8,128)(2,1)} %get-tuple-element.321), channel_id=1, source_target_pairs={{0,1},{1,0},{2,3},{3,2},{4,5},{5,4},{6,7},{7,6},{8,9},{9,8},{10,11... | collective-permute-start | bytes 3072008 | tf_op jit(solution)/shard_map/ppermute | solution.py:49
  64.8 15.2 %collective-permute-start.2 = (bf16[320,1600]{1,0:T(8,128)(2,1)S(1)}, bf16[320,1600]{1,0:T(8,128)(2,1)S(1)}, u32[]{:S(2)}, u32[]{:S(2)}) collective-permute-start(bf16[320,1600]{1,0:T(8,128)(2,1)S(1)} %collective-permute-done.1), channel_id=1, source_target_pairs={{0,1},{1,0},{2,3},{3,2},{4,5},{5,4},{6,7},{7,6},{8,9},{9,8},{10,11... | collective-permute-start | bytes 3072008 | tf_op jit(solution)/shard_map/ppermute | solution.py:49
  66.6 15.5 %collective-permute-start.4 = (bf16[320,1600]{1,0:T(8,128)(2,1)S(1)}, bf16[320,1600]{1,0:T(8,128)(2,1)S(1)}, u32[]{:S(2)}, u32[]{:S(2)}) collective-permute-start(bf16[320,1600]{1,0:T(8,128)(2,1)S(1)} %collective-permute-done.3), channel_id=1, source_target_pairs={{0,1},{1,0},{2,3},{3,2},{4,5},{5,4},{6,7},{7,6},{8,9},{9,8},{10,11... | collective-permute-start | bytes 3072008 | tf_op jit(solution)/shard_map/ppermute | solution.py:49
  90.1 67.0 %collective-permute-start.10 = (bf16[320,1600]{1,0:T(8,128)(2,1)}, bf16[320,1600]{1,0:T(8,128)(2,1)}, u32[]{:S(2)}, u32[]{:S(2)}) collective-permute-start(bf16[320,1600]{1,0:T(8,128)(2,1)} %param.18), channel_id=1, source_target_pairs={{0,6},{2,4},{4,2},{6,0},{1,7},{3,5},{5,3},{7,1},{8,14},{10,12},{12... | collective-permute-start | bytes 3072008 | tf_op jit(solution)/shard_map/ppermute | solution.py:81
  91.8 65.3 %collective-permute-start.8 = (bf16[320,1600]{1,0:T(8,128)(2,1)}, bf16[320,1600]{1,0:T(8,128)(2,1)}, u32[]{:S(2)}, u32[]{:S(2)}) collective-permute-start(bf16[320,1600]{1,0:T(8,128)(2,1)} %param.18), channel_id=1, source_target_pairs={{0,2},{2,0},{1,3},{3,1},{4,6},{6,4},{5,7},{7,5},{8,10},{10,8},{9,1... | collective-permute-start | bytes 3072008 | tf_op jit(solution)/shard_map/ppermute | solution.py:49
  93.0 64.1 %collective-permute-start.9 = (bf16[320,1600]{1,0:T(8,128)(2,1)}, bf16[320,1600]{1,0:T(8,128)(2,1)}, u32[]{:S(2)}, u32[]{:S(2)}) collective-permute-start(bf16[320,1600]{1,0:T(8,128)(2,1)} %param.18), channel_id=1, source_target_pairs={{0,4},{4,0},{1,5},{5,1},{2,6},{6,2},{3,7},{7,3},{8,12},{12,8},{9,1... | collective-permute-start | bytes 3072008 | tf_op jit(solution)/shard_map/ppermute | solution.py:49
  108.0 47.9 %all-to-all-start.1 = ((bf16[8,50,800]{2,1,0:T(8,128)(2,1)}), bf16[8,50,800]{2,1,0:T(8,128)(2,1)S(1)}, u32[]{:S(2)}, u32[]{:S(2)}) async-start(bf16[8,50,800]{2,1,0:T(8,128)(2,1)} %reshape.575), calls=%async_computation.1 | async-start | bytes 1605632 | tf_op jit(solution)/shard_map/all_to_all | solution.py:483
  111.5 197.3 %all-gather.9.cloned.1.call-start = ((), (), s32[]{:S(2)}) async-start(), calls=%async_computation.11 | async-start | bytes 3584000 | tf_op jit(solution)/shard_map/all_gather | solution.py:499
  196.7 125.1 %all-gather.11.cloned.1.call-start = ((), (), s32[]{:S(2)}) async-start(), calls=%async_computation.12 | async-start | bytes 3328000 | tf_op jit(solution)/shard_map/all_gather | solution.py:617
  197.8 34.6 %collective-permute-start.11 = (bf16[320,1600]{1,0:T(8,128)(2,1)}, bf16[320,1600]{1,0:T(8,128)(2,1)}, u32[]{:S(2)}, u32[]{:S(2)}) collective-permute-start(bf16[320,1600]{1,0:T(8,128)(2,1)} %get-tuple-element.115), channel_id=1, source_target_pairs={{0,1},{1,0},{2,3},{3,2},{4,5},{5,4},{6,7},{7,6},{8,9},{9,8},{10,11... | collective-permute-start | bytes 3072008 | tf_op jit(solution)/shard_map/ppermute | solution.py:49
  218.4 25.0 %collective-permute-start.17 = (bf16[320,1600]{1,0:T(8,128)(2,1)}, bf16[320,1600]{1,0:T(8,128)(2,1)}, u32[]{:S(2)}, u32[]{:S(2)}) collective-permute-start(bf16[320,1600]{1,0:T(8,128)(2,1)} %pad_maximum_fusion.2), channel_id=1, source_target_pairs={{0,2},{2,0},{1,3},{3,1},{4,6},{6,4},{5,7},{7,5},{8,10},{10,8},{9,1... | collective-permute-start | bytes 3072008 | tf_op jit(solution)/shard_map/ppermute | solution.py:49
  219.4 25.0 %collective-permute-start.18 = (bf16[320,1600]{1,0:T(8,128)(2,1)}, bf16[320,1600]{1,0:T(8,128)(2,1)}, u32[]{:S(2)}, u32[]{:S(2)}) collective-permute-start(bf16[320,1600]{1,0:T(8,128)(2,1)} %pad_maximum_fusion.1), channel_id=1, source_target_pairs={{0,4},{4,0},{1,5},{5,1},{2,6},{6,2},{3,7},{7,3},{8,12},{12,8},{9,1... | collective-permute-start | bytes 3072008 | tf_op jit(solution)/shard_map/ppermute | solution.py:49
  225.5 25.1 %collective-permute-start.27 = (bf16[320,1600]{1,0:T(8,128)(2,1)}, bf16[320,1600]{1,0:T(8,128)(2,1)S(1)}, u32[]{:S(2)}, u32[]{:S(2)}) collective-permute-start(bf16[320,1600]{1,0:T(8,128)(2,1)} %param.18), channel_id=1, source_target_pairs={{0,1},{1,0},{2,3},{3,2},{4,5},{5,4},{6,7},{7,6},{8,9},{9,8},{10,11... | collective-permute-start | bytes 3072008 | tf_op jit(solution)/shard_map/ppermute | solution.py:49
  225.6 30.0 %collective-permute-start.28 = (bf16[320,1600]{1,0:T(8,128)(2,1)}, bf16[320,1600]{1,0:T(8,128)(2,1)S(1)}, u32[]{:S(2)}, u32[]{:S(2)}) collective-permute-start(bf16[320,1600]{1,0:T(8,128)(2,1)} %collective-permute-done.8), channel_id=1, source_target_pairs={{0,1},{1,0},{2,3},{3,2},{4,5},{5,4},{6,7},{7,6},{8,9},{9,8},{10,11... | collective-permute-start | bytes 3072008 | tf_op jit(solution)/shard_map/ppermute | solution.py:49
  232.4 26.5 %collective-permute-start.29 = (bf16[320,1600]{1,0:T(8,128)(2,1)}, bf16[320,1600]{1,0:T(8,128)(2,1)S(1)}, u32[]{:S(2)}, u32[]{:S(2)}) collective-permute-start(bf16[320,1600]{1,0:T(8,128)(2,1)} %collective-permute-done.9), channel_id=1, source_target_pairs={{0,1},{1,0},{2,3},{3,2},{4,5},{5,4},{6,7},{7,6},{8,9},{9,8},{10,11... | collective-permute-start | bytes 3072008 | tf_op jit(solution)/shard_map/ppermute | solution.py:49
  243.3 31.7 %collective-permute-start.30 = (bf16[320,1600]{1,0:T(8,128)(2,1)}, bf16[320,1600]{1,0:T(8,128)(2,1)S(1)}, u32[]{:S(2)}, u32[]{:S(2)}) collective-permute-start(bf16[320,1600]{1,0:T(8,128)(2,1)} %collective-permute-done.10), channel_id=1, source_target_pairs={{0,1},{1,0},{2,3},{3,2},{4,5},{5,4},{6,7},{7,6},{8,9},{9,8},{10,11... | collective-permute-start | bytes 3072008 | tf_op jit(solution)/shard_map/ppermute | solution.py:49
  249.9 25.2 %collective-permute-start.20 = (bf16[320,1600]{1,0:T(8,128)(2,1)}, bf16[320,1600]{1,0:T(8,128)(2,1)}, u32[]{:S(2)}, u32[]{:S(2)}) collective-permute-start(bf16[320,1600]{1,0:T(8,128)(2,1)} %get-tuple-element.317), channel_id=1, source_target_pairs={{0,2},{2,0},{1,3},{3,1},{4,6},{6,4},{5,7},{7,5},{8,10},{10,8},{9,1... | collective-permute-start | bytes 3072008 | tf_op jit(solution)/shard_map/ppermute | solution.py:49
  250.6 30.0 %collective-permute-start.22 = (bf16[320,1600]{1,0:T(8,128)(2,1)}, bf16[320,1600]{1,0:T(8,128)(2,1)}, u32[]{:S(2)}, u32[]{:S(2)}) collective-permute-start(bf16[320,1600]{1,0:T(8,128)(2,1)} %get-tuple-element.317), channel_id=1, source_target_pairs={{0,4},{4,0},{1,5},{5,1},{2,6},{6,2},{3,7},{7,3},{8,12},{12,8},{9,1... | collective-permute-start | bytes 3072008 | tf_op jit(solution)/shard_map/ppermute | solution.py:49
  255.6 26.7 %collective-permute-start.19 = (bf16[320,1600]{1,0:T(8,128)(2,1)}, bf16[320,1600]{1,0:T(8,128)(2,1)}, u32[]{:S(2)}, u32[]{:S(2)}) collective-permute-start(bf16[320,1600]{1,0:T(8,128)(2,1)} %get-tuple-element.317), channel_id=1, source_target_pairs={{0,1},{1,0},{2,3},{3,2},{4,5},{5,4},{6,7},{7,6},{8,9},{9,8},{10,11... | collective-permute-start | bytes 3072008 | tf_op jit(solution)/shard_map/ppermute | solution.py:49
  275.1 21.1 %collective-permute-start.21 = (bf16[320,1600]{1,0:T(8,128)(2,1)}, bf16[320,1600]{1,0:T(8,128)(2,1)}, u32[]{:S(2)}, u32[]{:S(2)}) collective-permute-start(bf16[320,1600]{1,0:T(8,128)(2,1)} %collective-permute-done.20), channel_id=1, source_target_pairs={{0,1},{1,0},{2,3},{3,2},{4,5},{5,4},{6,7},{7,6},{8,9},{9,8},{10,11... | collective-permute-start | bytes 3072008 | tf_op jit(solution)/shard_map/ppermute | solution.py:49
  282.3 18.5 %collective-permute-start.23 = (bf16[320,1600]{1,0:T(8,128)(2,1)}, bf16[320,1600]{1,0:T(8,128)(2,1)S(1)}, u32[]{:S(2)}, u32[]{:S(2)}) collective-permute-start(bf16[320,1600]{1,0:T(8,128)(2,1)} %collective-permute-done.22), channel_id=1, source_target_pairs={{0,1},{1,0},{2,3},{3,2},{4,5},{5,4},{6,7},{7,6},{8,9},{9,8},{10,11... | collective-permute-start | bytes 3072008 | tf_op jit(solution)/shard_map/ppermute | solution.py:49
  304.2 49.6 %all-to-all-start.2 = ((bf16[8,50,2560]{2,1,0:T(8,128)(2,1)}), bf16[8,50,2560]{2,1,0:T(8,128)(2,1)}, u32[]{:S(2)}, u32[]{:S(2)}) async-start(bf16[8,50,2560]{2,1,0:T(8,128)(2,1)} %reshape.558), calls=%async_computation.2 | async-start | bytes 4587520 | tf_op jit(solution)/shard_map/all_to_all | solution.py:483
  308.5 223.7 %reduce-scatter.9.cloned.1.call-start = ((), (), s32[]{:S(2)}) async-start(), calls=%async_computation.14 | async-start | bytes 3584000 | tf_op jit(solution)/shard_map/reduce_scatter | solution.py:506
  358.8 21.4 %collective-permute-start.31 = (bf16[320,1600]{1,0:T(8,128)(2,1)S(1)}, bf16[320,1600]{1,0:T(8,128)(2,1)S(1)}, u32[]{:S(2)}, u32[]{:S(2)}) collective-permute-start(bf16[320,1600]{1,0:T(8,128)(2,1)S(1)} %get-tuple-element.139), channel_id=1, source_target_pairs={{0,1},{1,0},{2,3},{3,2},{4,5},{5,4},{6,7},{7,6},{8,9},{9,8},{10,11... | collective-permute-start | bytes 3072008 | tf_op jit(solution)/shard_map/ppermute | solution.py:49
  377.3 24.5 %collective-permute-start.37 = (bf16[320,1600]{1,0:T(8,128)(2,1)S(1)}, bf16[320,1600]{1,0:T(8,128)(2,1)S(1)}, u32[]{:S(2)}, u32[]{:S(2)}) collective-permute-start(bf16[320,1600]{1,0:T(8,128)(2,1)S(1)} %pad_maximum_fusion.4), channel_id=1, source_target_pairs={{0,2},{2,0},{1,3},{3,1},{4,6},{6,4},{5,7},{7,5},{8,10},{10,8},{9,1... | collective-permute-start | bytes 3072008 | tf_op jit(solution)/shard_map/ppermute | solution.py:49
  378.8 24.1 %collective-permute-start.38 = (bf16[320,1600]{1,0:T(8,128)(2,1)S(1)}, bf16[320,1600]{1,0:T(8,128)(2,1)S(1)}, u32[]{:S(2)}, u32[]{:S(2)}) collective-permute-start(bf16[320,1600]{1,0:T(8,128)(2,1)S(1)} %pad_maximum_fusion.3), channel_id=1, source_target_pairs={{0,4},{4,0},{1,5},{5,1},{2,6},{6,2},{3,7},{7,3},{8,12},{12,8},{9,1... | collective-permute-start | bytes 3072008 | tf_op jit(solution)/shard_map/ppermute | solution.py:49
  408.9 38.5 %collective-permute-start.40 = (bf16[320,1600]{1,0:T(8,128)(2,1)S(1)}, bf16[320,1600]{1,0:T(8,128)(2,1)}, u32[]{:S(2)}, u32[]{:S(2)}) collective-permute-start(bf16[320,1600]{1,0:T(8,128)(2,1)S(1)} %get-tuple-element.312), channel_id=1, source_target_pairs={{0,2},{2,0},{1,3},{3,1},{4,6},{6,4},{5,7},{7,5},{8,10},{10,8},{9,1... | collective-permute-start | bytes 3072008 | tf_op jit(solution)/shard_map/ppermute | solution.py:49
  409.5 41.1 %collective-permute-start.42 = (bf16[320,1600]{1,0:T(8,128)(2,1)S(1)}, bf16[320,1600]{1,0:T(8,128)(2,1)S(1)}, u32[]{:S(2)}, u32[]{:S(2)}) collective-permute-start(bf16[320,1600]{1,0:T(8,128)(2,1)S(1)} %get-tuple-element.312), channel_id=1, source_target_pairs={{0,4},{4,0},{1,5},{5,1},{2,6},{6,2},{3,7},{7,3},{8,12},{12,8},{9,1... | collective-permute-start | bytes 3072008 | tf_op jit(solution)/shard_map/ppermute | solution.py:49
  411.2 40.9 %collective-permute-start.39 = (bf16[320,1600]{1,0:T(8,128)(2,1)S(1)}, bf16[320,1600]{1,0:T(8,128)(2,1)}, u32[]{:S(2)}, u32[]{:S(2)}) collective-permute-start(bf16[320,1600]{1,0:T(8,128)(2,1)S(1)} %get-tuple-element.312), channel_id=1, source_target_pairs={{0,1},{1,0},{2,3},{3,2},{4,5},{5,4},{6,7},{7,6},{8,9},{9,8},{10,11... | collective-permute-start | bytes 3072008 | tf_op jit(solution)/shard_map/ppermute | solution.py:49
  422.2 132.1 %reduce-scatter.7.cloned.1.call-start = ((), (), s32[]{:S(2)}) async-start(), calls=%async_computation.13 | async-start | bytes 9584640 | tf_op jit(solution)/shard_map/reduce_scatter | solution.py:677
  447.5 17.1 %collective-permute-start.41 = (bf16[320,1600]{1,0:T(8,128)(2,1)}, bf16[320,1600]{1,0:T(8,128)(2,1)S(1)}, u32[]{:S(2)}, u32[]{:S(2)}) collective-permute-start(bf16[320,1600]{1,0:T(8,128)(2,1)} %collective-permute-done.40), channel_id=1, source_target_pairs={{0,1},{1,0},{2,3},{3,2},{4,5},{5,4},{6,7},{7,6},{8,9},{9,8},{10,11... | collective-permute-start | bytes 3072008 | tf_op jit(solution)/shard_map/ppermute | solution.py:49
  478.3 56.2 %collective-permute-start.47 = (bf16[200,1600]{1,0:T(8,128)(2,1)}, bf16[200,1600]{1,0:T(8,128)(2,1)S(1)}, u32[]{:S(2)}, u32[]{:S(2)}) collective-permute-start(bf16[200,1600]{1,0:T(8,128)(2,1)} %get-tuple-element.350), channel_id=1, source_target_pairs={{0,8},{8,16},{16,24},{24,0},{1,9},{9,17},{17,25},{25,1},{2,10},{10... | collective-permute-start | bytes 1920008 | tf_op jit(solution)/shard_map/ppermute | solution.py:116
  479.8 54.7 %collective-permute-start.48 = (bf16[200,1600]{1,0:T(8,128)(2,1)}, bf16[200,1600]{1,0:T(8,128)(2,1)S(1)}, u32[]{:S(2)}, u32[]{:S(2)}) collective-permute-start(bf16[200,1600]{1,0:T(8,128)(2,1)} %get-tuple-element.349), channel_id=1, source_target_pairs={{0,16},{8,24},{16,0},{24,8},{1,17},{9,25},{17,1},{25,9},{2,18},{10... | collective-permute-start | bytes 1920008 | tf_op jit(solution)/shard_map/ppermute | solution.py:116
  480.7 53.8 %collective-permute-start.49 = (bf16[200,1600]{1,0:T(8,128)(2,1)}, bf16[200,1600]{1,0:T(8,128)(2,1)S(1)}, u32[]{:S(2)}, u32[]{:S(2)}) collective-permute-start(bf16[200,1600]{1,0:T(8,128)(2,1)} %get-tuple-element.348), channel_id=1, source_target_pairs={{0,24},{8,0},{16,8},{24,16},{1,25},{9,1},{17,9},{25,17},{2,26},{10... | collective-permute-start | bytes 1920008 | tf_op jit(solution)/shard_map/ppermute | solution.py:116
  548.7 18.2 %collective-permute-start.50 = (bf16[320,1600]{1,0:T(8,128)(2,1)}, bf16[320,1600]{1,0:T(8,128)(2,1)}, u32[]{:S(2)}, u32[]{:S(2)}) collective-permute-start(bf16[320,1600]{1,0:T(8,128)(2,1)} %get-tuple-element.159), channel_id=1, source_target_pairs={{0,1},{1,0},{2,3},{3,2},{4,5},{5,4},{6,7},{7,6},{8,9},{9,8},{10,11... | collective-permute-start | bytes 3072008 | tf_op jit(solution)/shard_map/ppermute | solution.py:49
  548.7 18.2 %collective-permute-start.51 = (bf16[320,1600]{1,0:T(8,128)(2,1)}, bf16[320,1600]{1,0:T(8,128)(2,1)}, u32[]{:S(2)}, u32[]{:S(2)}) collective-permute-start(bf16[320,1600]{1,0:T(8,128)(2,1)} %get-tuple-element.160), channel_id=1, source_target_pairs={{0,1},{1,0},{2,3},{3,2},{4,5},{5,4},{6,7},{7,6},{8,9},{9,8},{10,11... | collective-permute-start | bytes 3072008 | tf_op jit(solution)/shard_map/ppermute | solution.py:49
  549.2 17.7 %collective-permute-start.52 = (bf16[320,1600]{1,0:T(8,128)(2,1)}, bf16[320,1600]{1,0:T(8,128)(2,1)}, u32[]{:S(2)}, u32[]{:S(2)}) collective-permute-start(bf16[320,1600]{1,0:T(8,128)(2,1)} %get-tuple-element.161), channel_id=1, source_target_pairs={{0,1},{1,0},{2,3},{3,2},{4,5},{5,4},{6,7},{7,6},{8,9},{9,8},{10,11... | collective-permute-start | bytes 3072008 | tf_op jit(solution)/shard_map/ppermute | solution.py:49
  549.2 17.7 %collective-permute-start.53 = (bf16[320,1600]{1,0:T(8,128)(2,1)}, bf16[320,1600]{1,0:T(8,128)(2,1)}, u32[]{:S(2)}, u32[]{:S(2)}) collective-permute-start(bf16[320,1600]{1,0:T(8,128)(2,1)} %get-tuple-element.162), channel_id=1, source_target_pairs={{0,1},{1,0},{2,3},{3,2},{4,5},{5,4},{6,7},{7,6},{8,9},{9,8},{10,11... | collective-permute-start | bytes 3072008 | tf_op jit(solution)/shard_map/ppermute | solution.py:49
  549.8 17.1 %all-to-all-start.3 = ((bf16[8,50,800]{2,1,0:T(8,128)(2,1)}), bf16[8,50,800]{2,1,0:T(8,128)(2,1)}, u32[]{:S(2)}, u32[]{:S(2)}) async-start(bf16[8,50,800]{2,1,0:T(8,128)(2,1)} %reshape.559), calls=%async_computation.5 | async-start | bytes 1605632 | tf_op jit(solution)/shard_map/all_to_all | solution.py:483
  554.0 84.3 %reduce-scatter.11.cloned.1.call-start = ((), (), s32[]{:S(2)}) async-start(), calls=%async_computation.15 | async-start | bytes 3072000 | tf_op jit(solution)/shard_map/reduce_scatter | solution.py:506
  587.1 24.9 %collective-permute-start.56 = (bf16[320,1600]{1,0:T(8,128)(2,1)}, bf16[320,1600]{1,0:T(8,128)(2,1)S(1)}, u32[]{:S(2)}, u32[]{:S(2)}) collective-permute-start(bf16[320,1600]{1,0:T(8,128)(2,1)} %pad_maximum_fusion.6), channel_id=1, source_target_pairs={{0,2},{2,0},{1,3},{3,1},{4,6},{6,4},{5,7},{7,5},{8,10},{10,8},{9,1... | collective-permute-start | bytes 3072008 | tf_op jit(solution)/shard_map/ppermute | solution.py:49
  588.5 24.7 %collective-permute-start.57 = (bf16[320,1600]{1,0:T(8,128)(2,1)}, bf16[320,1600]{1,0:T(8,128)(2,1)}, u32[]{:S(2)}, u32[]{:S(2)}) collective-permute-start(bf16[320,1600]{1,0:T(8,128)(2,1)} %pad_maximum_fusion.5), channel_id=1, source_target_pairs={{0,4},{4,0},{1,5},{5,1},{2,6},{6,2},{3,7},{7,3},{8,12},{12,8},{9,1... | collective-permute-start | bytes 3072008 | tf_op jit(solution)/shard_map/ppermute | solution.py:49
  643.9 55.4 %reduce-scatter.13.cloned.1.call-start = ((), (), s32[]{:S(2)}) async-start(), calls=%async_computation.16 | async-start | bytes 1064960 | tf_op jit(solution)/shard_map/reduce_scatter | solution.py:705
  665.5 25.4 %collective-permute-start.66 = (bf16[64,1600]{1,0:T(8,128)(2,1)}, bf16[64,1600]{1,0:T(8,128)(2,1)}, u32[]{:S(2)}, u32[]{:S(2)}) collective-permute-start(bf16[64,1600]{1,0:T(8,128)(2,1)} %add.507), channel_id=1, source_target_pairs={{0,8},{8,0},{16,24},{24,16},{1,9},{9,1},{17,25},{25,17},{2,10},{10... | collective-permute-start | bytes 614408 | tf_op jit(solution)/shard_map/ppermute | solution.py:121
  (100 other events, 863.5 us)
Sparse Core Ops, SparseCore 0:
  39.3 51.4 all-gather.4
  93.6 89.4 all-gather.6
  196.8 57.3 all-gather.8
  255.7 54.1 all-gather.10
  422.3 54.7 reduce-scatter.8
  480.5 71.8 reduce-scatter.6
  567.0 53.4 reduce-scatter.10
  647.3 34.9 reduce-scatter.12

commit v3 on v2

--- a/solution.py
+++ b/solution.py
@@ -77,9 +77,13 @@
     return full, (from_b, from_a)
 
 
-def plane_fetch(own):
-    across = lax.ppermute(own, ("a", "b"), [(i, i ^ 3) for i in range(4)])
-    return (swap(own, "b"), swap(own, "a"), across)
+def plane_near(own):
+    return swap(own, "b"), swap(own, "a")
+
+
+def plane_far(from_b, from_a):
+    half = from_b.shape[0] // 2
+    return jnp.concatenate([swap(from_b[:half], "a"), swap(from_a[half:], "b")], axis=0)
 
 
 def plane_scatter(array, place, hold=lambda sent: ()):
@@ -198,12 +202,19 @@
         for h in group:
             some(h, (step, listed[step, others - 1]), True)
 
+    pairs = others // 2
+
+    @pl.when(pairs % 2 == 1)
+    def _():
+        for h in group:
+            some(h, (listed[step, 2 * pairs - 2], listed[step, 2 * pairs - 1]), False)
+
     def body(i, carry):
         for h in group:
-            some(h, (listed[step, 2 * i], listed[step, 2 * i + 1]), False)
+            some(h, tuple(listed[step, 4 * i + k] for k in range(4)), False)
         return carry
 
-    lax.fori_loop(0, others // 2, body, 0)
+    lax.fori_loop(0, pairs // 2, body, 0)
 
 
 def head_cols(part, h, local):
@@ -595,13 +606,13 @@
     first_norm, normed_one, inv_one = norm_forward(residual_in, ln1_gain, ln1_bias)
     first_own = first_norm.astype(BF)
     qkv_split, fc_split = partial(head_split, parts=3), partial(hidden_split, unit=unit)
-    qkv_rows = columns_start(after(w_qkv, first_own), 3 * model_width, qkv_split)
+    qkv_rows = columns_start(w_qkv, 3 * model_width, qkv_split)
     w_qkv_l = columns_end(qkv_rows, w_qkv.size, 3 * model_width, qkv_split, place)
     qkv_bias = jnp.concatenate([q_bias, jnp.zeros_like(q_bias), v_bias])
     qkv_bias_l = take(head_split(qkv_bias[None], 3), place)[0]
     first_low, _ = plane_gather(first_own, place)
 
-    two_far = plane_fetch(after(cotangent, first_low))
+    two_near = plane_near(after(cotangent, first_low))
     whole_rows = w_out.size % model_width == 0
     ratio = model_width // flat_cols
     w_out_full = lax.all_gather(after(w_out, first_low), EVERY, axis=0, tiled=True)
@@ -627,11 +638,13 @@
 
     fc_rows = columns_start(after(w_fc, projected), hidden, fc_split)
     attended, out_wide, lse, tops = attend(count, listed, owned, projected, q_mark, k_mark)
-    attended, two_far, fc_rows = lax.optimization_barrier((attended, two_far, fc_rows))
+    attended, two_near, fc_rows = lax.optimization_barrier((attended, two_near, fc_rows))
+    two_far = plane_far(*two_near)
+    attended = after(attended, two_far)
     w_fc_l = columns_end(fc_rows, w_fc.size, hidden, fc_split, place)
     branch = jnp.dot(attended, w_out_l, preferred_element_type=F32).astype(BF)
     mid_sum, mid_last = plane_scatter(branch, place)
-    two_blocks = after((cotangent,) + two_far, *mid_last)
+    two_blocks = after((cotangent, *two_near, two_far), *mid_last)
     grad_two = plane_write(two_blocks, [swap(block, "c") for block in two_blocks], place, None)
     middle = residual_in + mid_sum + out_bias
 
@@ -698,7 +711,7 @@
     if whole_rows:
         padded = -(-share // 16) * 16
         out_rows = jnp.dot(
-            slots_in(own_slots, each * HEAD_DIM, share, place, padded),
+            slots_in(after(own_slots, *in_last), each * HEAD_DIM, share, place, padded),
             branch_late,
             preferred_element_type=F32,
         ).astype(BF)
@@ -746,12 +759,14 @@
     sums = jnp.concatenate([sums, spread])
 
     whole_qkv = w_qkv.size % (3 * model_width) == 0
-    combines = [combine, lambda left, right: left + right]
+    add = lambda left, right: left + right
+    combines = [combine, add]
+    (common,) = over_trees([common], [add])
     sums, common = over_plane(lax.optimization_barrier((sums, common)), combines)
     if whole_qkv:
         qkv_rows = exchange(after(qkv_rows, in_sum))
     sums, common, qkv_rows = lax.optimization_barrier((sums, common, qkv_rows))
-    sums, common = over_trees([sums, common], combines)
+    (sums,) = over_trees([sums], [combine])
     logit_max = sums[-heads:]
     qkv_shard = columns_second(
         qkv_rows, partial(head_join, parts=3, heads=heads), w_qkv.shape, 3 * model_width, place

time: 719 us -> 709 us (0.986)
  blocking collectives: 16.5 us -> 0 us
  local copies, waits for them, and re-layouts: 137 us -> 145 us
  waiting for transfers between devices: 181 us -> 189 us
    all_gather x1, waiting for transfers between devices: 26.1 us -> 0.01 us  [on_device(): lax.all_gather(after(w_out, first_low), EVERY, axis=0, tiled=True)]
    ppermute x10, waiting for transfers between devices: 9.63 us -> 26.2 us  [pairwise(): others = [lax.ppermute(value, axis, pairs) for value in values]]
    all_to_all x1 -> x0, blocking collectives: 16.5 us -> none  [exchange(): lax.all_to_all(shares, PLANE, split_axis=0, concat_axis=0, tiled=True)]
    all_to_all x4 -> x5, waiting for transfers between devices: 8.58 us -> 19.6 us  [exchange(): lax.all_to_all(shares, PLANE, split_axis=0, concat_axis=0, tiled=True)]
    ppermute x10, starting transfers between devices: 15.2 us -> 7.75 us  [pairwise(): others = [lax.ppermute(value, axis, pairs) for value in values]]
    ppermute x54 -> x56, waiting for transfers between devices: 136 us -> 143 us  [swap(): return lax.ppermute(value, axis, [(0, 1), (1, 0)])]
    all_to_all x4 -> x5, starting transfers between devices: 15.7 us -> 20.8 us  [exchange(): lax.all_to_all(shares, PLANE, split_axis=0, concat_axis=0, tiled=True)]
    unnamed x143 -> x135, local copies, waits for them, and re-layouts: 25.6 us -> 27.7 us
  transfers between devices with their start and end apart: 80 -> 82, of which waited for: 28 -> 31; matrix products, arithmetic and copies ran while one was open for 40% -> 42% of each run, Pallas kernels for 12% -> 12%
where the time goes in v3:
time: 709 us; the launch traced here: 701 us
  waiting for transfers between devices  189 us (27%)
  local copies, waits for them, and re-layouts  145 us (20%)
  matrix products  132 us (19%)
  Pallas kernels  85.6 us (12%)
  starting transfers between devices  70.9 us (10%)
  other arithmetic  61.9 us (9%)
  between operations  16 us (2%)
    ppermute x56, waiting for transfers between devices, swap(): return lax.ppermute(value, axis, [(0, 1), (1, 0)])  143 us
    dynamic_update_slice x30, local copies, waits for them, and re-layouts, plane_write(): full = lax.dynamic_update_slice_in_dim(full, piece, (place ^ q) * rows, 0)  46.2 us
    dot_general x4, matrix products, on_device(): lax.dot_general(left, right, (((1,), (1,)), ((), ())), preferred_element_...  45.9 us
    pallas_call x1, Pallas kernels, attend_back(): pl.pallas_call(attend_back_kernel, grid_spec=pltpu.PrefetchScalarGridSpec...  45.6 us
    pallas_call x1, Pallas kernels, attend(): pl.pallas_call(attend_kernel, grid_spec=pltpu.PrefetchScalarGridSpec(num_...  40 us
    dot_general x4, matrix products, on_device(): lax.dot_general(left, right, (((0,), (0,)), ((), ())), preferred_element_...  39 us
    ppermute x56, starting transfers between devices, swap(): return lax.ppermute(value, axis, [(0, 1), (1, 0)])  36.7 us
    unnamed x135, local copies, waits for them, and re-layouts  27.7 us
  transfers between devices with their start and end apart: 82, of which 31 were waited for; matrix products, arithmetic and copies ran while one was open for 42% of the time, Pallas kernels for 12%

profile of v3, /device:TPU:0, one launch (start us, length us, event | category | flops | bytes accessed | tf_op | source)
XLA Modules:
  0.0 701.5 jit_solution(16159534039986735534)
XLA Ops:
  8.5 2.8 reshape_reshape.9
  14.2 5.2 all-to-all-start
  20.2 10.7 %all-to-all-done = bf16[8,50,768]{2,1,0:T(8,128)(2,1)S(1)} async-done(((bf16[8,50,768]{2,1,0:T(8,128)(2,1)}), bf16[8,50,768]{2,1,0:T(8,128)(2,1)S(1)}, u32[]{:S(2)}, u32[]{:S(2)}) %all-to-all-start) | async-done | bytes 614432 | tf_op jit(solution)/shard_map/all_to_all | solution.py:494
  34.4 3.4 copy-done.15
  38.9 23.4 %collective-permute-done.1 = bf16[320,1600]{1,0:T(8,128)(2,1)S(1)} collective-permute-done((bf16[320,1600]{1,0:T(8,128)(2,1)}, bf16[320,1600]{1,0:T(8,128)(2,1)S(1)}, u32[]{:S(2)}, u32[]{:S(2)}) %collective-permute-start.1) | collective-permute-done | bytes 1024032 | tf_op jit(solution)/shard_map/ppermute | solution.py:49
  67.9 8.9 %collective-permute-done.5 = bf16[160,1600]{1,0:T(8,128)(2,1)S(1)} collective-permute-done((bf16[160,1600]{1,0:T(8,128)(2,1)S(1)}, bf16[160,1600]{1,0:T(8,128)(2,1)S(1)}, u32[]{:S(2)}, u32[]{:S(2)}) %collective-permute-start.5) | collective-permute-done | bytes 512032 | tf_op jit(solution)/shard_map/ppermute | solution.py:49
  90.7 11.8 %add_convert_fusion.proj = bf16[2560,768]{1,0:T(8,128)(2,1)} fusion(bf16[2560,1600]{1,0:T(8,128)(2,1)} %constant_dynamic-update-slice_fusion.33, bf16[1600,768]{1,0:T(8,128)(2,1)} %all-gather.5.cloned.1.call-done, f32[768]{0:T(1024)S(1)} %fusion.52), kind=kOutput, calls=%fused_computation.18 | convolution fusion | flops 6295388160 | bytes 14584832 | tf_op jit(solution)/shard_map/dot_general | solution.py:637
  105.0 3.5 all-to-all-start.1
  111.0 40.0 %attend.1 = (bf16[2560,256]{1,0:T(8,128)(2,1)S(1)}, f32[4,64,2560]{2,1,0:T(8,128)S(1)}, f32[4,2560]{1,0:T(4,128)S(1)}, f32[4,256]{1,0:T(4,128)S(1)}) custom-call(s32[10]{0:T(128)S(1)} %fusion.57.count, s32[10,10]{1,0:T(8,128)S(1)} %select_reduce_fusion.1.listed, s32[10]{0:T(128)S(1)} %compare_convert_fusion.3.owned, bf16[2560,768]{1,0:T(8,128)(2,1)S(1)} %copy-done.4, ...), custom_call_target="tpu_custom_call" | custom-call | flops 6710886400 | bytes 10485760 | tf_op jit(solution)/shard_map/attend/pallas_call | solution.py:302
  160.3 10.0 %collective-permute-done.10 = bf16[160,1600]{1,0:T(8,128)(2,1)} collective-permute-done((bf16[160,1600]{1,0:T(8,128)(2,1)}, bf16[160,1600]{1,0:T(8,128)(2,1)}, u32[]{:S(2)}, u32[]{:S(2)}) %collective-permute-start.10) | collective-permute-done | bytes 512032 | tf_op jit(solution)/shard_map/ppermute | solution.py:49
  181.1 3.5 constant_dynamic-slice_fusion.22
  194.8 11.5 %collective-permute-done.17 = bf16[160,1600]{1,0:T(8,128)(2,1)S(1)} collective-permute-done((bf16[160,1600]{1,0:T(8,128)(2,1)S(1)}, bf16[160,1600]{1,0:T(8,128)(2,1)S(1)}, u32[]{:S(2)}, u32[]{:S(2)}) %collective-permute-start.17) | collective-permute-done | bytes 512032 | tf_op jit(solution)/shard_map/ppermute | solution.py:49
  216.6 3.9 broadcast.461
  223.1 10.7 %collective-permute-done.18 = bf16[320,1600]{1,0:T(8,128)(2,1)} collective-permute-done((bf16[320,1600]{1,0:T(8,128)(2,1)}, bf16[320,1600]{1,0:T(8,128)(2,1)}, u32[]{:S(2)}, u32[]{:S(2)}) %collective-permute-start.18) | collective-permute-done | bytes 1024032 | tf_op jit(solution)/shard_map/ppermute | solution.py:49
  234.0 2.9 fusion.59
  253.8 11.7 %collective-permute-done.21 = bf16[320,1600]{1,0:T(8,128)(2,1)} collective-permute-done((bf16[320,1600]{1,0:T(8,128)(2,1)}, bf16[320,1600]{1,0:T(8,128)(2,1)}, u32[]{:S(2)}, u32[]{:S(2)}) %collective-permute-start.21) | collective-permute-done | bytes 1024032 | tf_op jit(solution)/shard_map/ppermute | solution.py:49
  277.3 6.7 collective-permute-done.25
  293.4 4.4 all-to-all-start.2
  298.0 12.9 %fusion.66 = f32[2560,800]{0,1:T(8,128)} fusion(bf16[2560,1600]{1,0:T(8,128)(2,1)} %constant_dynamic-update-slice_fusion.25, bf16[1600,800]{1,0:T(8,128)(2,1)} %all-gather.9.cloned.1.call-done), kind=kOutput, calls=%fused_computation.290 | convolution fusion | flops 6553600000 | bytes 18944000 | tf_op jit(solution)/shard_map/dot_general | solution.py:659
  311.0 17.9 %fusion.6 = (bf16[2560,800]{0,1:T(8,128)(2,1)S(1)}, bf16[2560,800]{0,1:T(8,128)(2,1)}) fusion(f32[2560,800]{0,1:T(8,128)} %fusion.66, f32[800]{0:T(1024)S(1)} %fusion.51, bf16[2560,1600]{1,0:T(8,128)(2,1)} %constant_dynamic-update-slice_fusion.17, bf16[800,1600]{1,0:T(8,128)(2,1)} %all-gather.11.cloned.1.call-done), kind=kOutput, calls=%fused_computation.14 | convolution fusion | flops 6600704000 | bytes 27139200 | tf_op jit(solution)/shard_map/dot_general | solution.py:662
  330.9 12.1 %convolution_convert_fusion.2 = bf16[2560,1600]{1,0:T(8,128)(2,1)} fusion(bf16[2560,800]{0,1:T(8,128)(2,1)S(1)} %get-tuple-element.176, bf16[1600,800]{1,0:T(8,128)(2,1)S(1)} %copy-done.53), kind=kOutput, calls=%fused_computation.6 | convolution fusion | flops 6557696000 | bytes 14848000 | tf_op jit(solution)/shard_map/dot_general | solution.py:662
  343.0 4.1 constant_dynamic-slice_fusion.13
  354.2 10.4 %collective-permute-done.37 = bf16[160,1600]{1,0:T(8,128)(2,1)S(1)} collective-permute-done((bf16[160,1600]{1,0:T(8,128)(2,1)S(1)}, bf16[160,1600]{1,0:T(8,128)(2,1)S(1)}, u32[]{:S(2)}, u32[]{:S(2)}) %collective-permute-start.37) | collective-permute-done | bytes 512032 | tf_op jit(solution)/shard_map/ppermute | solution.py:49
  369.5 21.5 %collective-permute-done.38 = bf16[320,1600]{1,0:T(8,128)(2,1)S(1)} collective-permute-done((bf16[320,1600]{1,0:T(8,128)(2,1)S(1)}, bf16[320,1600]{1,0:T(8,128)(2,1)S(1)}, u32[]{:S(2)}, u32[]{:S(2)}) %collective-permute-start.38) | collective-permute-done | bytes 1024032 | tf_op jit(solution)/shard_map/ppermute | solution.py:49
  394.2 5.0 convert_reduce_fusion.4
  401.4 10.9 %convolution_convert_fusion.6 = bf16[1600,800]{1,0:T(8,128)(2,1)} fusion(bf16[2560,1600]{1,0:T(8,128)(2,1)S(1)} %bitcast.118, bf16[2560,800]{0,1:T(8,128)(2,1)S(1)} %copy-done.20), kind=kOutput, calls=%fused_computation.21 | convolution fusion | flops 6554880000 | bytes 14848000 | tf_op jit(solution)/shard_map/dot_general | solution.py:665
  412.4 14.0 %convolution_convert_fusion.7 = bf16[800,1600]{1,0:T(8,128)(2,1)} fusion(bf16[2560,800]{0,1:T(8,128)(2,1)} %get-tuple-element.150, bf16[2560,1600]{1,0:T(8,128)(2,1)} %constant_dynamic-update-slice_fusion.17), kind=kOutput, calls=%fused_computation.22 | convolution fusion | flops 6554880000 | bytes 14848000 | tf_op jit(solution)/shard_map/dot_general | solution.py:665
  426.5 11.7 %convolution_convert_fusion.1 = bf16[2560,1600]{1,0:T(8,128)(2,1)} fusion(bf16[2560,800]{0,1:T(8,128)(2,1)S(1)} %copy-done.55, bf16[800,1600]{1,0:T(8,128)(2,1)S(1)} %copy-done.54), kind=kOutput, calls=%fused_computation.5 | convolution fusion | flops 6557696000 | bytes 14848000 | tf_op jit(solution)/shard_map/dot_general | solution.py:684
  447.1 7.8 %collective-permute-done.45 = bf16[160,1600]{1,0:T(8,128)(2,1)S(1)} collective-permute-done((bf16[160,1600]{1,0:T(8,128)(2,1)S(1)}, bf16[160,1600]{1,0:T(8,128)(2,1)S(1)}, u32[]{:S(2)}, u32[]{:S(2)}) %collective-permute-start.45) | collective-permute-done | bytes 512032 | tf_op jit(solution)/shard_map/ppermute | solution.py:49
  463.2 3.3 constant_dynamic-slice_fusion.9
  466.8 3.6 collective-permute-start.50
  470.4 6.0 convolution_convert_fusion.5.up
  476.4 45.6 %attend_back.1 = bf16[2560,768]{1,0:T(8,128)(2,1)S(1)} custom-call(s32[10]{0:T(128)S(1)} %fusion.57.count, s32[10,10]{1,0:T(8,128)S(1)} %select_reduce_fusion.1.listed, s32[10]{0:T(128)S(1)} %compare_convert_fusion.3.owned, bf16[2560,768]{1,0:T(8,128)(2,1)} %add_convert_fusion.proj, bf16[2560,64]{1,0:T(8,128)(2,1)S(1)} %pad.15.q_mark, ...), custom_call_target="tpu_custom_call" | custom-call | flops 16777216000 | bytes 20971520 | tf_op jit(solution)/shard_map/attend_back/pallas_call | solution.py:420
  527.4 9.8 %convolution_convert_fusion = bf16[2560,1600]{1,0:T(8,128)(2,1)S(1)} fusion(bf16[2560,768]{1,0:T(8,128)(2,1)} %copy-done.2, bf16[1600,768]{1,0:T(8,128)(2,1)} %all-gather.5.cloned.1.call-done), kind=kOutput, calls=%fused_computation.4 | convolution fusion | flops 6295552000 | bytes 14581760 | tf_op jit(solution)/shard_map/dot_general | solution.py:662
  540.8 4.2 all-to-all-start.3
  545.3 12.6 %convolution_convert_fusion.8 = bf16[1600,768]{1,0:T(8,128)(2,1)} fusion(bf16[2560,1600]{1,0:T(8,128)(2,1)} %constant_dynamic-update-slice_fusion.33, bf16[2560,768]{1,0:T(8,128)(2,1)} %copy-done.2), kind=kOutput, calls=%fused_computation.23 | convolution fusion | flops 6292684800 | bytes 14581760 | tf_op jit(solution)/shard_map/dot_general | solution.py:665
  566.2 9.3 %collective-permute-done.56 = bf16[160,1600]{1,0:T(8,128)(2,1)S(1)} collective-permute-done((bf16[160,1600]{1,0:T(8,128)(2,1)S(1)}, bf16[160,1600]{1,0:T(8,128)(2,1)S(1)}, u32[]{:S(2)}, u32[]{:S(2)}) %collective-permute-start.56) | collective-permute-done | bytes 512032 | tf_op jit(solution)/shard_map/ppermute | solution.py:49
  586.6 4.8 convolution_convert_fusion.9
  592.1 2.9 convert_reduce_fusion
  594.9 3.7 collective-permute-done.59
  601.4 15.0 %collective-permute-done.60 = bf16[64,1600]{1,0:T(8,128)(2,1)} collective-permute-done((bf16[64,1600]{1,0:T(8,128)(2,1)}, bf16[64,1600]{1,0:T(8,128)(2,1)}, u32[]{:S(2)}, u32[]{:S(2)}) %collective-permute-start.60) | collective-permute-done | bytes 204832 | tf_op jit(solution)/shard_map/ppermute | solution.py:125
  618.5 4.1 fusion.16
  626.1 3.9 fusion.19
  632.8 2.9 collective-permute-done.62
  647.7 3.5 all-to-all-start.4
  653.8 8.8 %all-to-all-done.4 = bf16[8,50,768]{2,1,0:T(8,128)(2,1)S(1)} async-done(((bf16[8,50,768]{2,1,0:T(8,128)(2,1)}), bf16[8,50,768]{2,1,0:T(8,128)(2,1)S(1)}, u32[]{:S(2)}, u32[]{:S(2)}) %all-to-all-start.4) | async-done | bytes 614432 | tf_op jit(solution)/shard_map/all_to_all | solution.py:494
  672.0 3.2 reshape_reshape.11
  681.6 2.9 reshape.576
  (506 shorter events, 231.8 us)
Async XLA Ops:
  14.2 16.7 %all-to-all-start = ((bf16[8,50,768]{2,1,0:T(8,128)(2,1)}), bf16[8,50,768]{2,1,0:T(8,128)(2,1)S(1)}, u32[]{:S(2)}, u32[]{:S(2)}) async-start(bf16[8,50,768]{2,1,0:T(8,128)(2,1)} %reshape.574), calls=%async_computation | async-start | bytes 1376256 | tf_op jit(solution)/shard_map/all_to_all | solution.py:494
  19.4 71.3 %all-gather.5.cloned.1.call-start = ((), (), s32[]{:S(2)}) async-start(), calls=%async_computation.9 | async-start | bytes 3072000 | tf_op jit(solution)/shard_map/all_gather | solution.py:510
  31.9 142.1 %all-gather.7.cloned.1.call-start = ((), (), s32[]{:S(2)}) async-start(), calls=%async_computation.10 | async-start | bytes 6758400 | tf_op jit(solution)/shard_map/all_gather | solution.py:618
  37.7 24.5 %collective-permute-start.1 = (bf16[320,1600]{1,0:T(8,128)(2,1)}, bf16[320,1600]{1,0:T(8,128)(2,1)S(1)}, u32[]{:S(2)}, u32[]{:S(2)}) collective-permute-start(bf16[320,1600]{1,0:T(8,128)(2,1)} %get-tuple-element.321), channel_id=1, source_target_pairs={{0,2},{2,0},{1,3},{3,1},{4,6},{6,4},{5,7},{7,5},{8,10},{10,8},{9,1... | collective-permute-start | bytes 3072008 | tf_op jit(solution)/shard_map/ppermute | solution.py:49
  38.3 25.4 %collective-permute-start.3 = (bf16[320,1600]{1,0:T(8,128)(2,1)}, bf16[320,1600]{1,0:T(8,128)(2,1)S(1)}, u32[]{:S(2)}, u32[]{:S(2)}) collective-permute-start(bf16[320,1600]{1,0:T(8,128)(2,1)} %get-tuple-element.321), channel_id=1, source_target_pairs={{0,4},{4,0},{1,5},{5,1},{2,6},{6,2},{3,7},{7,3},{8,12},{12,8},{9,1... | collective-permute-start | bytes 3072008 | tf_op jit(solution)/shard_map/ppermute | solution.py:49
  38.9 25.7 %collective-permute-start = (bf16[320,1600]{1,0:T(8,128)(2,1)}, bf16[320,1600]{1,0:T(8,128)(2,1)}, u32[]{:S(2)}, u32[]{:S(2)}) collective-permute-start(bf16[320,1600]{1,0:T(8,128)(2,1)} %get-tuple-element.321), channel_id=1, source_target_pairs={{0,1},{1,0},{2,3},{3,2},{4,5},{5,4},{6,7},{7,6},{8,9},{9,8},{10,11... | collective-permute-start | bytes 3072008 | tf_op jit(solution)/shard_map/ppermute | solution.py:49
  87.4 66.4 %collective-permute-start.8 = (bf16[320,1600]{1,0:T(8,128)(2,1)}, bf16[320,1600]{1,0:T(8,128)(2,1)}, u32[]{:S(2)}, u32[]{:S(2)}) collective-permute-start(bf16[320,1600]{1,0:T(8,128)(2,1)} %param.18), channel_id=1, source_target_pairs={{0,2},{2,0},{1,3},{3,1},{4,6},{6,4},{5,7},{7,5},{8,10},{10,8},{9,1... | collective-permute-start | bytes 3072008 | tf_op jit(solution)/shard_map/ppermute | solution.py:49
  89.2 64.6 %collective-permute-start.9 = (bf16[320,1600]{1,0:T(8,128)(2,1)}, bf16[320,1600]{1,0:T(8,128)(2,1)}, u32[]{:S(2)}, u32[]{:S(2)}) collective-permute-start(bf16[320,1600]{1,0:T(8,128)(2,1)} %param.18), channel_id=1, source_target_pairs={{0,4},{4,0},{1,5},{5,1},{2,6},{6,2},{3,7},{7,3},{8,12},{12,8},{9,1... | collective-permute-start | bytes 3072008 | tf_op jit(solution)/shard_map/ppermute | solution.py:49
  105.0 47.4 %all-to-all-start.1 = ((bf16[8,50,800]{2,1,0:T(8,128)(2,1)}), bf16[8,50,800]{2,1,0:T(8,128)(2,1)S(1)}, u32[]{:S(2)}, u32[]{:S(2)}) async-start(bf16[8,50,800]{2,1,0:T(8,128)(2,1)} %reshape.575), calls=%async_computation.1 | async-start | bytes 1605632 | tf_op jit(solution)/shard_map/all_to_all | solution.py:494
  108.6 189.5 %all-gather.9.cloned.1.call-start = ((), (), s32[]{:S(2)}) async-start(), calls=%async_computation.11 | async-start | bytes 3584000 | tf_op jit(solution)/shard_map/all_gather | solution.py:510
  187.1 123.9 %all-gather.11.cloned.1.call-start = ((), (), s32[]{:S(2)}) async-start(), calls=%async_computation.12 | async-start | bytes 3328000 | tf_op jit(solution)/shard_map/all_gather | solution.py:628
  188.2 34.7 %collective-permute-start.12 = (bf16[320,1600]{1,0:T(8,128)(2,1)}, bf16[320,1600]{1,0:T(8,128)(2,1)}, u32[]{:S(2)}, u32[]{:S(2)}) collective-permute-start(bf16[320,1600]{1,0:T(8,128)(2,1)} %get-tuple-element.117), channel_id=1, source_target_pairs={{0,1},{1,0},{2,3},{3,2},{4,5},{5,4},{6,7},{7,6},{8,9},{9,8},{10,11... | collective-permute-start | bytes 3072008 | tf_op jit(solution)/shard_map/ppermute | solution.py:49
  208.6 25.1 %collective-permute-start.18 = (bf16[320,1600]{1,0:T(8,128)(2,1)}, bf16[320,1600]{1,0:T(8,128)(2,1)}, u32[]{:S(2)}, u32[]{:S(2)}) collective-permute-start(bf16[320,1600]{1,0:T(8,128)(2,1)} %pad_maximum_fusion.2), channel_id=1, source_target_pairs={{0,2},{2,0},{1,3},{3,1},{4,6},{6,4},{5,7},{7,5},{8,10},{10,8},{9,1... | collective-permute-start | bytes 3072008 | tf_op jit(solution)/shard_map/ppermute | solution.py:49
  209.4 24.6 %collective-permute-start.19 = (bf16[320,1600]{1,0:T(8,128)(2,1)}, bf16[320,1600]{1,0:T(8,128)(2,1)}, u32[]{:S(2)}, u32[]{:S(2)}) collective-permute-start(bf16[320,1600]{1,0:T(8,128)(2,1)} %pad_maximum_fusion.1), channel_id=1, source_target_pairs={{0,4},{4,0},{1,5},{5,1},{2,6},{6,2},{3,7},{7,3},{8,12},{12,8},{9,1... | collective-permute-start | bytes 3072008 | tf_op jit(solution)/shard_map/ppermute | solution.py:49
  216.0 25.0 %collective-permute-start.28 = (bf16[320,1600]{1,0:T(8,128)(2,1)}, bf16[320,1600]{1,0:T(8,128)(2,1)S(1)}, u32[]{:S(2)}, u32[]{:S(2)}) collective-permute-start(bf16[320,1600]{1,0:T(8,128)(2,1)} %param.18), channel_id=1, source_target_pairs={{0,1},{1,0},{2,3},{3,2},{4,5},{5,4},{6,7},{7,6},{8,9},{9,8},{10,11... | collective-permute-start | bytes 3072008 | tf_op jit(solution)/shard_map/ppermute | solution.py:49
  216.1 28.9 %collective-permute-start.29 = (bf16[320,1600]{1,0:T(8,128)(2,1)}, bf16[320,1600]{1,0:T(8,128)(2,1)S(1)}, u32[]{:S(2)}, u32[]{:S(2)}) collective-permute-start(bf16[320,1600]{1,0:T(8,128)(2,1)} %collective-permute-done.8), channel_id=1, source_target_pairs={{0,1},{1,0},{2,3},{3,2},{4,5},{5,4},{6,7},{7,6},{8,9},{9,8},{10,11... | collective-permute-start | bytes 3072008 | tf_op jit(solution)/shard_map/ppermute | solution.py:49
  222.9 25.4 %collective-permute-start.30 = (bf16[320,1600]{1,0:T(8,128)(2,1)}, bf16[320,1600]{1,0:T(8,128)(2,1)S(1)}, u32[]{:S(2)}, u32[]{:S(2)}) collective-permute-start(bf16[320,1600]{1,0:T(8,128)(2,1)} %collective-permute-done.9), channel_id=1, source_target_pairs={{0,1},{1,0},{2,3},{3,2},{4,5},{5,4},{6,7},{7,6},{8,9},{9,8},{10,11... | collective-permute-start | bytes 3072008 | tf_op jit(solution)/shard_map/ppermute | solution.py:49
  233.8 31.8 %collective-permute-start.31 = (bf16[320,1600]{1,0:T(8,128)(2,1)}, bf16[320,1600]{1,0:T(8,128)(2,1)S(1)}, u32[]{:S(2)}, u32[]{:S(2)}) collective-permute-start(bf16[320,1600]{1,0:T(8,128)(2,1)} %constant_dynamic-update-slice_fusion.2), channel_id=1, source_target_pairs={{0,1},{1,0},{2,3},{3,2},{4,5},{5,4},{6,7},{7,6},{8,9},{9,8},{10,11... | collective-permute-start | bytes 3072008 | tf_op jit(solution)/shard_map/ppermute | solution.py:49
  239.5 26.0 %collective-permute-start.21 = (bf16[320,1600]{1,0:T(8,128)(2,1)}, bf16[320,1600]{1,0:T(8,128)(2,1)}, u32[]{:S(2)}, u32[]{:S(2)}) collective-permute-start(bf16[320,1600]{1,0:T(8,128)(2,1)} %get-tuple-element.317), channel_id=1, source_target_pairs={{0,2},{2,0},{1,3},{3,1},{4,6},{6,4},{5,7},{7,5},{8,10},{10,8},{9,1... | collective-permute-start | bytes 3072008 | tf_op jit(solution)/shard_map/ppermute | solution.py:49
  241.0 29.0 %collective-permute-start.23 = (bf16[320,1600]{1,0:T(8,128)(2,1)}, bf16[320,1600]{1,0:T(8,128)(2,1)}, u32[]{:S(2)}, u32[]{:S(2)}) collective-permute-start(bf16[320,1600]{1,0:T(8,128)(2,1)} %get-tuple-element.317), channel_id=1, source_target_pairs={{0,4},{4,0},{1,5},{5,1},{2,6},{6,2},{3,7},{7,3},{8,12},{12,8},{9,1... | collective-permute-start | bytes 3072008 | tf_op jit(solution)/shard_map/ppermute | solution.py:49
  245.0 27.7 %collective-permute-start.20 = (bf16[320,1600]{1,0:T(8,128)(2,1)}, bf16[320,1600]{1,0:T(8,128)(2,1)}, u32[]{:S(2)}, u32[]{:S(2)}) collective-permute-start(bf16[320,1600]{1,0:T(8,128)(2,1)} %get-tuple-element.317), channel_id=1, source_target_pairs={{0,1},{1,0},{2,3},{3,2},{4,5},{5,4},{6,7},{7,6},{8,9},{9,8},{10,11... | collective-permute-start | bytes 3072008 | tf_op jit(solution)/shard_map/ppermute | solution.py:49
  265.6 19.9 %collective-permute-start.22 = (bf16[320,1600]{1,0:T(8,128)(2,1)}, bf16[320,1600]{1,0:T(8,128)(2,1)}, u32[]{:S(2)}, u32[]{:S(2)}) collective-permute-start(bf16[320,1600]{1,0:T(8,128)(2,1)} %collective-permute-done.21), channel_id=1, source_target_pairs={{0,1},{1,0},{2,3},{3,2},{4,5},{5,4},{6,7},{7,6},{8,9},{9,8},{10,11... | collective-permute-start | bytes 3072008 | tf_op jit(solution)/shard_map/ppermute | solution.py:49
  272.7 17.5 %collective-permute-start.24 = (bf16[320,1600]{1,0:T(8,128)(2,1)}, bf16[320,1600]{1,0:T(8,128)(2,1)S(1)}, u32[]{:S(2)}, u32[]{:S(2)}) collective-permute-start(bf16[320,1600]{1,0:T(8,128)(2,1)} %collective-permute-done.23), channel_id=1, source_target_pairs={{0,1},{1,0},{2,3},{3,2},{4,5},{5,4},{6,7},{7,6},{8,9},{9,8},{10,11... | collective-permute-start | bytes 3072008 | tf_op jit(solution)/shard_map/ppermute | solution.py:49
  293.4 49.6 %all-to-all-start.2 = ((bf16[8,50,2560]{2,1,0:T(8,128)(2,1)}), bf16[8,50,2560]{2,1,0:T(8,128)(2,1)}, u32[]{:S(2)}, u32[]{:S(2)}) async-start(bf16[8,50,2560]{2,1,0:T(8,128)(2,1)} %reshape.558), calls=%async_computation.2 | async-start | bytes 4587520 | tf_op jit(solution)/shard_map/all_to_all | solution.py:494
  297.8 226.1 %reduce-scatter.9.cloned.1.call-start = ((), (), s32[]{:S(2)}) async-start(), calls=%async_computation.14 | async-start | bytes 3584000 | tf_op jit(solution)/shard_map/reduce_scatter | solution.py:517
  348.1 21.4 %collective-permute-start.32 = (bf16[320,1600]{1,0:T(8,128)(2,1)S(1)}, bf16[320,1600]{1,0:T(8,128)(2,1)S(1)}, u32[]{:S(2)}, u32[]{:S(2)}) collective-permute-start(bf16[320,1600]{1,0:T(8,128)(2,1)S(1)} %get-tuple-element.138), channel_id=1, source_target_pairs={{0,1},{1,0},{2,3},{3,2},{4,5},{5,4},{6,7},{7,6},{8,9},{9,8},{10,11... | collective-permute-start | bytes 3072008 | tf_op jit(solution)/shard_map/ppermute | solution.py:49
  366.5 24.5 %collective-permute-start.38 = (bf16[320,1600]{1,0:T(8,128)(2,1)S(1)}, bf16[320,1600]{1,0:T(8,128)(2,1)S(1)}, u32[]{:S(2)}, u32[]{:S(2)}) collective-permute-start(bf16[320,1600]{1,0:T(8,128)(2,1)S(1)} %pad_maximum_fusion.4), channel_id=1, source_target_pairs={{0,2},{2,0},{1,3},{3,1},{4,6},{6,4},{5,7},{7,5},{8,10},{10,8},{9,1... | collective-permute-start | bytes 3072008 | tf_op jit(solution)/shard_map/ppermute | solution.py:49
  368.1 24.1 %collective-permute-start.39 = (bf16[320,1600]{1,0:T(8,128)(2,1)S(1)}, bf16[320,1600]{1,0:T(8,128)(2,1)S(1)}, u32[]{:S(2)}, u32[]{:S(2)}) collective-permute-start(bf16[320,1600]{1,0:T(8,128)(2,1)S(1)} %pad_maximum_fusion.3), channel_id=1, source_target_pairs={{0,4},{4,0},{1,5},{5,1},{2,6},{6,2},{3,7},{7,3},{8,12},{12,8},{9,1... | collective-permute-start | bytes 3072008 | tf_op jit(solution)/shard_map/ppermute | solution.py:49
  399.2 39.0 %collective-permute-start.41 = (bf16[320,1600]{1,0:T(8,128)(2,1)S(1)}, bf16[320,1600]{1,0:T(8,128)(2,1)}, u32[]{:S(2)}, u32[]{:S(2)}) collective-permute-start(bf16[320,1600]{1,0:T(8,128)(2,1)S(1)} %get-tuple-element.312), channel_id=1, source_target_pairs={{0,2},{2,0},{1,3},{3,1},{4,6},{6,4},{5,7},{7,5},{8,10},{10,8},{9,1... | collective-permute-start | bytes 3072008 | tf_op jit(solution)/shard_map/ppermute | solution.py:49
  399.7 41.2 %collective-permute-start.43 = (bf16[320,1600]{1,0:T(8,128)(2,1)S(1)}, bf16[320,1600]{1,0:T(8,128)(2,1)S(1)}, u32[]{:S(2)}, u32[]{:S(2)}) collective-permute-start(bf16[320,1600]{1,0:T(8,128)(2,1)S(1)} %get-tuple-element.312), channel_id=1, source_target_pairs={{0,4},{4,0},{1,5},{5,1},{2,6},{6,2},{3,7},{7,3},{8,12},{12,8},{9,1... | collective-permute-start | bytes 3072008 | tf_op jit(solution)/shard_map/ppermute | solution.py:49
  401.4 41.1 %collective-permute-start.40 = (bf16[320,1600]{1,0:T(8,128)(2,1)S(1)}, bf16[320,1600]{1,0:T(8,128)(2,1)}, u32[]{:S(2)}, u32[]{:S(2)}) collective-permute-start(bf16[320,1600]{1,0:T(8,128)(2,1)S(1)} %get-tuple-element.312), channel_id=1, source_target_pairs={{0,1},{1,0},{2,3},{3,2},{4,5},{5,4},{6,7},{7,6},{8,9},{9,8},{10,11... | collective-permute-start | bytes 3072008 | tf_op jit(solution)/shard_map/ppermute | solution.py:49
  412.4 132.9 %reduce-scatter.7.cloned.1.call-start = ((), (), s32[]{:S(2)}) async-start(), calls=%async_computation.13 | async-start | bytes 9584640 | tf_op jit(solution)/shard_map/reduce_scatter | solution.py:690
  438.2 17.0 %collective-permute-start.42 = (bf16[320,1600]{1,0:T(8,128)(2,1)}, bf16[320,1600]{1,0:T(8,128)(2,1)S(1)}, u32[]{:S(2)}, u32[]{:S(2)}) collective-permute-start(bf16[320,1600]{1,0:T(8,128)(2,1)} %collective-permute-done.41), channel_id=1, source_target_pairs={{0,1},{1,0},{2,3},{3,2},{4,5},{5,4},{6,7},{7,6},{8,9},{9,8},{10,11... | collective-permute-start | bytes 3072008 | tf_op jit(solution)/shard_map/ppermute | solution.py:49
  466.6 59.6 %collective-permute-start.48 = (bf16[200,1600]{1,0:T(8,128)(2,1)}, bf16[200,1600]{1,0:T(8,128)(2,1)S(1)}, u32[]{:S(2)}, u32[]{:S(2)}) collective-permute-start(bf16[200,1600]{1,0:T(8,128)(2,1)} %get-tuple-element.350), channel_id=1, source_target_pairs={{0,8},{8,16},{16,24},{24,0},{1,9},{9,17},{17,25},{25,1},{2,10},{10... | collective-permute-start | bytes 1920008 | tf_op jit(solution)/shard_map/ppermute | solution.py:120
  466.6 59.6 %collective-permute-start.49 = (bf16[200,1600]{1,0:T(8,128)(2,1)}, bf16[200,1600]{1,0:T(8,128)(2,1)S(1)}, u32[]{:S(2)}, u32[]{:S(2)}) collective-permute-start(bf16[200,1600]{1,0:T(8,128)(2,1)} %get-tuple-element.349), channel_id=1, source_target_pairs={{0,16},{8,24},{16,0},{24,8},{1,17},{9,25},{17,1},{25,9},{2,18},{10... | collective-permute-start | bytes 1920008 | tf_op jit(solution)/shard_map/ppermute | solution.py:120
  466.8 59.3 %collective-permute-start.50 = (bf16[200,1600]{1,0:T(8,128)(2,1)}, bf16[200,1600]{1,0:T(8,128)(2,1)S(1)}, u32[]{:S(2)}, u32[]{:S(2)}) collective-permute-start(bf16[200,1600]{1,0:T(8,128)(2,1)} %get-tuple-element.348), channel_id=1, source_target_pairs={{0,24},{8,0},{16,8},{24,16},{1,25},{9,1},{17,9},{25,17},{2,26},{10... | collective-permute-start | bytes 1920008 | tf_op jit(solution)/shard_map/ppermute | solution.py:120
  539.8 18.1 %collective-permute-start.51 = (bf16[320,1600]{1,0:T(8,128)(2,1)}, bf16[320,1600]{1,0:T(8,128)(2,1)}, u32[]{:S(2)}, u32[]{:S(2)}) collective-permute-start(bf16[320,1600]{1,0:T(8,128)(2,1)} %get-tuple-element.158), channel_id=1, source_target_pairs={{0,1},{1,0},{2,3},{3,2},{4,5},{5,4},{6,7},{7,6},{8,9},{9,8},{10,11... | collective-permute-start | bytes 3072008 | tf_op jit(solution)/shard_map/ppermute | solution.py:49
  539.8 18.1 %collective-permute-start.52 = (bf16[320,1600]{1,0:T(8,128)(2,1)}, bf16[320,1600]{1,0:T(8,128)(2,1)}, u32[]{:S(2)}, u32[]{:S(2)}) collective-permute-start(bf16[320,1600]{1,0:T(8,128)(2,1)} %get-tuple-element.159), channel_id=1, source_target_pairs={{0,1},{1,0},{2,3},{3,2},{4,5},{5,4},{6,7},{7,6},{8,9},{9,8},{10,11... | collective-permute-start | bytes 3072008 | tf_op jit(solution)/shard_map/ppermute | solution.py:49
  540.3 17.6 %collective-permute-start.53 = (bf16[320,1600]{1,0:T(8,128)(2,1)}, bf16[320,1600]{1,0:T(8,128)(2,1)}, u32[]{:S(2)}, u32[]{:S(2)}) collective-permute-start(bf16[320,1600]{1,0:T(8,128)(2,1)} %get-tuple-element.160), channel_id=1, source_target_pairs={{0,1},{1,0},{2,3},{3,2},{4,5},{5,4},{6,7},{7,6},{8,9},{9,8},{10,11... | collective-permute-start | bytes 3072008 | tf_op jit(solution)/shard_map/ppermute | solution.py:49
  540.3 17.6 %collective-permute-start.54 = (bf16[320,1600]{1,0:T(8,128)(2,1)}, bf16[320,1600]{1,0:T(8,128)(2,1)}, u32[]{:S(2)}, u32[]{:S(2)}) collective-permute-start(bf16[320,1600]{1,0:T(8,128)(2,1)} %get-tuple-element.161), channel_id=1, source_target_pairs={{0,1},{1,0},{2,3},{3,2},{4,5},{5,4},{6,7},{7,6},{8,9},{9,8},{10,11... | collective-permute-start | bytes 3072008 | tf_op jit(solution)/shard_map/ppermute | solution.py:49
  540.8 17.1 %all-to-all-start.3 = ((bf16[8,50,800]{2,1,0:T(8,128)(2,1)}), bf16[8,50,800]{2,1,0:T(8,128)(2,1)}, u32[]{:S(2)}, u32[]{:S(2)}) async-start(bf16[8,50,800]{2,1,0:T(8,128)(2,1)} %reshape.559), calls=%async_computation.5 | async-start | bytes 1605632 | tf_op jit(solution)/shard_map/all_to_all | solution.py:494
  545.0 100.6 %reduce-scatter.11.cloned.1.call-start = ((), (), s32[]{:S(2)}) async-start(), calls=%async_computation.15 | async-start | bytes 3072000 | tf_op jit(solution)/shard_map/reduce_scatter | solution.py:517
  578.2 39.3 %collective-permute-start.57 = (bf16[320,1600]{1,0:T(8,128)(2,1)S(1)}, bf16[320,1600]{1,0:T(8,128)(2,1)S(1)}, u32[]{:S(2)}, u32[]{:S(2)}) collective-permute-start(bf16[320,1600]{1,0:T(8,128)(2,1)S(1)} %pad_maximum_fusion.6), channel_id=1, source_target_pairs={{0,2},{2,0},{1,3},{3,1},{4,6},{6,4},{5,7},{7,5},{8,10},{10,8},{9,1... | collective-permute-start | bytes 3072008 | tf_op jit(solution)/shard_map/ppermute | solution.py:49
  579.7 38.8 %collective-permute-start.58 = (bf16[320,1600]{1,0:T(8,128)(2,1)}, bf16[320,1600]{1,0:T(8,128)(2,1)}, u32[]{:S(2)}, u32[]{:S(2)}) collective-permute-start(bf16[320,1600]{1,0:T(8,128)(2,1)} %pad_maximum_fusion.5), channel_id=1, source_target_pairs={{0,4},{4,0},{1,5},{5,1},{2,6},{6,2},{3,7},{7,3},{8,12},{12,8},{9,1... | collective-permute-start | bytes 3072008 | tf_op jit(solution)/shard_map/ppermute | solution.py:49
  581.8 16.8 %collective-permute-start.59 = (bf16[64,1600]{1,0:T(8,128)(2,1)S(1)}, bf16[64,1600]{1,0:T(8,128)(2,1)}, u32[]{:S(2)}, u32[]{:S(2)}) collective-permute-start(bf16[64,1600]{1,0:T(8,128)(2,1)S(1)} %convolution_convert_fusion.10), channel_id=1, source_target_pairs={{0,8},{8,0},{16,24},{24,16},{1,9},{9,1},{17,25},{25,17},{2,10},{10... | collective-permute-start | bytes 614408 | tf_op jit(solution)/shard_map/ppermute | solution.py:125
  600.3 16.1 %collective-permute-start.60 = (bf16[64,1600]{1,0:T(8,128)(2,1)}, bf16[64,1600]{1,0:T(8,128)(2,1)}, u32[]{:S(2)}, u32[]{:S(2)}) collective-permute-start(bf16[64,1600]{1,0:T(8,128)(2,1)} %add.502), channel_id=1, source_target_pairs={{0,16},{8,24},{16,0},{24,8},{1,17},{9,25},{17,1},{25,9},{2,18},{10... | collective-permute-start | bytes 614408 | tf_op jit(solution)/shard_map/ppermute | solution.py:125
  635.7 15.8 %collective-permute-start.63 = (f32[19225]{0:T(1024)S(1)}, f32[19225]{0:T(1024)}, u32[]{:S(2)}, u32[]{:S(2)}) collective-permute-start(f32[19225]{0:T(1024)S(1)} %maximum_select_fusion.3), channel_id=1, source_target_pairs={{0,4},{4,0},{1,5},{5,1},{2,6},{6,2},{3,7},{7,3},{8,12},{12,8},{9,1... | collective-permute-start | bytes 230708 | tf_op jit(solution)/shard_map/ppermute | solution.py:125
  651.3 40.9 %reduce-scatter.13.cloned.1.call-start = ((), (), s32[]{:S(2)}) async-start(), calls=%async_computation.16 | async-start | bytes 1064960 | tf_op jit(solution)/shard_map/reduce_scatter | solution.py:718
  (97 other events, 958.3 us)
Sparse Core Ops, SparseCore 0:
  32.0 51.4 all-gather.4
  86.4 75.5 all-gather.6
  187.2 56.2 all-gather.8
  244.9 54.1 all-gather.10
  412.5 53.5 reduce-scatter.8
  469.4 71.9 reduce-scatter.6
  558.0 58.2 reduce-scatter.10
  654.4 25.1 reduce-scatter.12

commit v4 on v3

--- a/solution.py
+++ b/solution.py
@@ -640,7 +640,6 @@
     attended, out_wide, lse, tops = attend(count, listed, owned, projected, q_mark, k_mark)
     attended, two_near, fc_rows = lax.optimization_barrier((attended, two_near, fc_rows))
     two_far = plane_far(*two_near)
-    attended = after(attended, two_far)
     w_fc_l = columns_end(fc_rows, w_fc.size, hidden, fc_split, place)
     branch = jnp.dot(attended, w_out_l, preferred_element_type=F32).astype(BF)
     mid_sum, mid_last = plane_scatter(branch, place)

time: 709 us -> 708 us (level)
  Pallas kernels: 85.6 us -> 77 us
  waiting for transfers between devices: 189 us -> 197 us
    all_gather x1, waiting for transfers between devices: 0.01 us -> 12.4 us  [on_device(): lax.all_gather(after(w_out, first_low), EVERY, axis=0, tiled=True)]
    unnamed x135 -> x134, local copies, waits for them, and re-layouts: 27.7 us -> 25.8 us
  transfers between devices with their start and end apart: 82 -> 82, of which waited for: 31 -> 31; matrix products, arithmetic and copies ran while one was open for 42% -> 41% of each run, Pallas kernels for 12% -> 11%
where the time goes in v4:
time: 708 us; the launch traced here: 702 us
  waiting for transfers between devices  197 us (28%)
  local copies, waits for them, and re-layouts  141 us (20%)
  matrix products  132 us (19%)
  Pallas kernels  77 us (11%)
  starting transfers between devices  75.1 us (11%)
  other arithmetic  63.1 us (9%)
  between operations  16 us (2%)
    ppermute x56, waiting for transfers between devices, swap(): return lax.ppermute(value, axis, [(0, 1), (1, 0)])  137 us
    dot_general x4, matrix products, on_device(): lax.dot_general(left, right, (((1,), (1,)), ((), ())), preferred_element_...  45.9 us
    dynamic_update_slice x30, local copies, waits for them, and re-layouts, plane_write(): full = lax.dynamic_update_slice_in_dim(full, piece, (place ^ q) * rows, 0)  45 us
    pallas_call x1, Pallas kernels, attend_back(): pl.pallas_call(attend_back_kernel, grid_spec=pltpu.PrefetchScalarGridSpec...  41.2 us
    dot_general x4, matrix products, on_device(): lax.dot_general(left, right, (((0,), (0,)), ((), ())), preferred_element_...  38.6 us
    pallas_call x1, Pallas kernels, attend(): pl.pallas_call(attend_kernel, grid_spec=pltpu.PrefetchScalarGridSpec(num_...  35.8 us
    ppermute x56, starting transfers between devices, swap(): return lax.ppermute(value, axis, [(0, 1), (1, 0)])  35.4 us
    ppermute x10, waiting for transfers between devices, pairwise(): others = [lax.ppermute(value, axis, pairs) for value in values]  26.8 us
  transfers between devices with their start and end apart: 82, of which 31 were waited for; matrix products, arithmetic and copies ran while one was open for 41% of the time, Pallas kernels for 11%

profile of v4, /device:TPU:0, one launch (start us, length us, event | category | flops | bytes accessed | tf_op | source)
XLA Modules:
  0.0 701.7 jit_solution(2701578937013907489)
XLA Ops:
  8.5 2.8 reshape_reshape.9
  14.2 5.2 all-to-all-start
  20.2 10.7 %all-to-all-done = bf16[8,50,768]{2,1,0:T(8,128)(2,1)S(1)} async-done(((bf16[8,50,768]{2,1,0:T(8,128)(2,1)}), bf16[8,50,768]{2,1,0:T(8,128)(2,1)S(1)}, u32[]{:S(2)}, u32[]{:S(2)}) %all-to-all-start) | async-done | bytes 614432 | tf_op jit(solution)/shard_map/all_to_all | solution.py:494
  34.4 3.4 copy-done.15
  38.9 23.4 %collective-permute-done.1 = bf16[320,1600]{1,0:T(8,128)(2,1)S(1)} collective-permute-done((bf16[320,1600]{1,0:T(8,128)(2,1)}, bf16[320,1600]{1,0:T(8,128)(2,1)S(1)}, u32[]{:S(2)}, u32[]{:S(2)}) %collective-permute-start.1) | collective-permute-done | bytes 1024032 | tf_op jit(solution)/shard_map/ppermute | solution.py:49
  67.9 8.9 %collective-permute-done.5 = bf16[160,1600]{1,0:T(8,128)(2,1)S(1)} collective-permute-done((bf16[160,1600]{1,0:T(8,128)(2,1)S(1)}, bf16[160,1600]{1,0:T(8,128)(2,1)S(1)}, u32[]{:S(2)}, u32[]{:S(2)}) %collective-permute-start.5) | collective-permute-done | bytes 512032 | tf_op jit(solution)/shard_map/ppermute | solution.py:49
  90.7 11.8 %add_convert_fusion.proj = bf16[2560,768]{1,0:T(8,128)(2,1)} fusion(bf16[2560,1600]{1,0:T(8,128)(2,1)} %constant_dynamic-update-slice_fusion.25, bf16[1600,768]{1,0:T(8,128)(2,1)} %all-gather.5.cloned.1.call-done, f32[768]{0:T(1024)S(1)} %fusion.52), kind=kOutput, calls=%fused_computation.18 | convolution fusion | flops 6295388160 | bytes 14584832 | tf_op jit(solution)/shard_map/dot_general | solution.py:637
  105.0 3.5 all-to-all-start.1
  111.0 35.8 %attend.1 = (bf16[2560,256]{1,0:T(8,128)(2,1)S(1)}, f32[4,64,2560]{2,1,0:T(8,128)S(1)}, f32[4,2560]{1,0:T(4,128)S(1)}, f32[4,256]{1,0:T(4,128)S(1)}) custom-call(s32[10]{0:T(128)S(1)} %fusion.57.count, s32[10,10]{1,0:T(8,128)S(1)} %select_reduce_fusion.1.listed, s32[10]{0:T(128)S(1)} %compare_convert_fusion.3.owned, bf16[2560,768]{1,0:T(8,128)(2,1)S(1)} %copy-done.4, ...), custom_call_target="tpu_custom_call" | custom-call | flops 6710886400 | bytes 10485760 | tf_op jit(solution)/shard_map/attend/pallas_call | solution.py:302
  149.6 12.4 %all-gather.7.cloned.1.call-done = bf16[12800,200]{1,0:T(8,128)(2,1)} async-done(((bf16[400,200]{1,0:T(8,128)(2,1)}), bf16[12800,200]{1,0:T(8,128)(2,1)}) %all-gather.7.cloned.1.call-update) | async-done | bytes 5120016 | tf_op jit(solution)/shard_map/all_gather | solution.py:618
  169.1 3.5 constant_dynamic-slice_fusion.22
  189.4 13.6 %collective-permute-done.15 = bf16[160,1600]{1,0:T(8,128)(2,1)S(1)} collective-permute-done((bf16[160,1600]{1,0:T(8,128)(2,1)S(1)}, bf16[160,1600]{1,0:T(8,128)(2,1)S(1)}, u32[]{:S(2)}, u32[]{:S(2)}) %collective-permute-start.15) | collective-permute-done | bytes 512032 | tf_op jit(solution)/shard_map/ppermute | solution.py:49
  216.3 3.9 broadcast.461
  222.7 9.5 %collective-permute-done.16 = bf16[320,1600]{1,0:T(8,128)(2,1)} collective-permute-done((bf16[320,1600]{1,0:T(8,128)(2,1)}, bf16[320,1600]{1,0:T(8,128)(2,1)}, u32[]{:S(2)}, u32[]{:S(2)}) %collective-permute-start.16) | collective-permute-done | bytes 1024032 | tf_op jit(solution)/shard_map/ppermute | solution.py:49
  232.5 2.9 fusion.59
  251.0 13.0 %collective-permute-done.19 = bf16[320,1600]{1,0:T(8,128)(2,1)} collective-permute-done((bf16[320,1600]{1,0:T(8,128)(2,1)}, bf16[320,1600]{1,0:T(8,128)(2,1)}, u32[]{:S(2)}, u32[]{:S(2)}) %collective-permute-start.19) | collective-permute-done | bytes 1024032 | tf_op jit(solution)/shard_map/ppermute | solution.py:49
  275.5 6.9 collective-permute-done.23
  291.8 4.4 all-to-all-start.2
  296.4 12.9 %fusion.66 = f32[2560,800]{0,1:T(8,128)} fusion(bf16[2560,1600]{1,0:T(8,128)(2,1)} %constant_dynamic-update-slice_fusion.17, bf16[1600,800]{1,0:T(8,128)(2,1)} %all-gather.9.cloned.1.call-done), kind=kOutput, calls=%fused_computation.289 | convolution fusion | flops 6553600000 | bytes 18944000 | tf_op jit(solution)/shard_map/dot_general | solution.py:658
  309.4 17.9 %fusion.6 = (bf16[2560,800]{0,1:T(8,128)(2,1)S(1)}, bf16[2560,800]{0,1:T(8,128)(2,1)}) fusion(f32[2560,800]{0,1:T(8,128)} %fusion.66, f32[800]{0:T(1024)S(1)} %fusion.51, bf16[2560,1600]{1,0:T(8,128)(2,1)} %constant_dynamic-update-slice_fusion.9, bf16[800,1600]{1,0:T(8,128)(2,1)} %all-gather.11.cloned.1.call-done), kind=kOutput, calls=%fused_computation.14 | convolution fusion | flops 6600704000 | bytes 27139200 | tf_op jit(solution)/shard_map/dot_general | solution.py:661
  329.2 12.1 %convolution_convert_fusion.2 = bf16[2560,1600]{1,0:T(8,128)(2,1)} fusion(bf16[2560,800]{0,1:T(8,128)(2,1)S(1)} %get-tuple-element.174, bf16[1600,800]{1,0:T(8,128)(2,1)S(1)} %copy-done.53), kind=kOutput, calls=%fused_computation.6 | convolution fusion | flops 6557696000 | bytes 14848000 | tf_op jit(solution)/shard_map/dot_general | solution.py:661
  341.4 4.1 constant_dynamic-slice_fusion.13
  352.6 10.4 %collective-permute-done.37 = bf16[160,1600]{1,0:T(8,128)(2,1)S(1)} collective-permute-done((bf16[160,1600]{1,0:T(8,128)(2,1)S(1)}, bf16[160,1600]{1,0:T(8,128)(2,1)S(1)}, u32[]{:S(2)}, u32[]{:S(2)}) %collective-permute-start.37) | collective-permute-done | bytes 512032 | tf_op jit(solution)/shard_map/ppermute | solution.py:49
  367.9 21.6 %collective-permute-done.38 = bf16[320,1600]{1,0:T(8,128)(2,1)S(1)} collective-permute-done((bf16[320,1600]{1,0:T(8,128)(2,1)S(1)}, bf16[320,1600]{1,0:T(8,128)(2,1)S(1)}, u32[]{:S(2)}, u32[]{:S(2)}) %collective-permute-start.38) | collective-permute-done | bytes 1024032 | tf_op jit(solution)/shard_map/ppermute | solution.py:49
  392.6 5.0 convert_reduce_fusion.4
  399.9 10.9 %convolution_convert_fusion.6 = bf16[1600,800]{1,0:T(8,128)(2,1)} fusion(bf16[2560,1600]{1,0:T(8,128)(2,1)S(1)} %bitcast.118, bf16[2560,800]{0,1:T(8,128)(2,1)S(1)} %copy-done.20), kind=kOutput, calls=%fused_computation.21 | convolution fusion | flops 6554880000 | bytes 14848000 | tf_op jit(solution)/shard_map/dot_general | solution.py:664
  410.9 13.5 %convolution_convert_fusion.7 = bf16[800,1600]{1,0:T(8,128)(2,1)} fusion(bf16[2560,800]{0,1:T(8,128)(2,1)} %get-tuple-element.148, bf16[2560,1600]{1,0:T(8,128)(2,1)} %constant_dynamic-update-slice_fusion.9), kind=kOutput, calls=%fused_computation.22 | convolution fusion | flops 6554880000 | bytes 14848000 | tf_op jit(solution)/shard_map/dot_general | solution.py:664
  424.4 11.7 %convolution_convert_fusion.1 = bf16[2560,1600]{1,0:T(8,128)(2,1)} fusion(bf16[2560,800]{0,1:T(8,128)(2,1)S(1)} %copy-done.55, bf16[800,1600]{1,0:T(8,128)(2,1)S(1)} %copy-done.54), kind=kOutput, calls=%fused_computation.5 | convolution fusion | flops 6557696000 | bytes 14848000 | tf_op jit(solution)/shard_map/dot_general | solution.py:683
  445.2 7.7 %collective-permute-done.45 = bf16[160,1600]{1,0:T(8,128)(2,1)S(1)} collective-permute-done((bf16[160,1600]{1,0:T(8,128)(2,1)S(1)}, bf16[160,1600]{1,0:T(8,128)(2,1)S(1)}, u32[]{:S(2)}, u32[]{:S(2)}) %collective-permute-start.45) | collective-permute-done | bytes 512032 | tf_op jit(solution)/shard_map/ppermute | solution.py:49
  461.3 3.3 constant_dynamic-slice_fusion.9
  469.3 6.0 convolution_convert_fusion.5.up
  475.3 41.2 %attend_back.1 = bf16[2560,768]{1,0:T(8,128)(2,1)S(1)} custom-call(s32[10]{0:T(128)S(1)} %fusion.57.count, s32[10,10]{1,0:T(8,128)S(1)} %select_reduce_fusion.1.listed, s32[10]{0:T(128)S(1)} %compare_convert_fusion.3.owned, bf16[2560,768]{1,0:T(8,128)(2,1)} %add_convert_fusion.proj, bf16[2560,64]{1,0:T(8,128)(2,1)S(1)} %pad.15.q_mark, ...), custom_call_target="tpu_custom_call" | custom-call | flops 16777216000 | bytes 20971520 | tf_op jit(solution)/shard_map/attend_back/pallas_call | solution.py:420
  521.9 9.9 %convolution_convert_fusion = bf16[2560,1600]{1,0:T(8,128)(2,1)S(1)} fusion(bf16[2560,768]{1,0:T(8,128)(2,1)} %copy-done.2, bf16[1600,768]{1,0:T(8,128)(2,1)} %all-gather.5.cloned.1.call-done), kind=kOutput, calls=%fused_computation.4 | convolution fusion | flops 6295552000 | bytes 14581760 | tf_op jit(solution)/shard_map/dot_general | solution.py:661
  535.3 4.2 all-to-all-start.3
  541.0 12.6 %convolution_convert_fusion.8 = bf16[1600,768]{1,0:T(8,128)(2,1)} fusion(bf16[2560,1600]{1,0:T(8,128)(2,1)} %constant_dynamic-update-slice_fusion.25, bf16[2560,768]{1,0:T(8,128)(2,1)} %copy-done.2), kind=kOutput, calls=%fused_computation.23 | convolution fusion | flops 6292684800 | bytes 14581760 | tf_op jit(solution)/shard_map/dot_general | solution.py:664
  560.8 10.0 %collective-permute-done.56 = bf16[160,1600]{1,0:T(8,128)(2,1)S(1)} collective-permute-done((bf16[160,1600]{1,0:T(8,128)(2,1)S(1)}, bf16[160,1600]{1,0:T(8,128)(2,1)S(1)}, u32[]{:S(2)}, u32[]{:S(2)}) %collective-permute-start.56) | collective-permute-done | bytes 512032 | tf_op jit(solution)/shard_map/ppermute | solution.py:49
  576.7 6.1 collective-permute-start.59
  585.7 4.8 convolution_convert_fusion.9
  591.1 2.9 convert_reduce_fusion
  594.0 4.2 collective-permute-done.59
  601.5 15.1 %collective-permute-done.60 = bf16[64,1600]{1,0:T(8,128)(2,1)} collective-permute-done((bf16[64,1600]{1,0:T(8,128)(2,1)}, bf16[64,1600]{1,0:T(8,128)(2,1)}, u32[]{:S(2)}, u32[]{:S(2)}) %collective-permute-start.60) | collective-permute-done | bytes 204832 | tf_op jit(solution)/shard_map/ppermute | solution.py:125
  618.7 4.1 fusion.16
  626.3 3.9 fusion.19
  633.0 2.9 collective-permute-done.62
  647.9 3.5 all-to-all-start.4
  654.1 8.8 %all-to-all-done.4 = bf16[8,50,768]{2,1,0:T(8,128)(2,1)S(1)} async-done(((bf16[8,50,768]{2,1,0:T(8,128)(2,1)}), bf16[8,50,768]{2,1,0:T(8,128)(2,1)S(1)}, u32[]{:S(2)}, u32[]{:S(2)}) %all-to-all-start.4) | async-done | bytes 614432 | tf_op jit(solution)/shard_map/all_to_all | solution.py:494
  672.2 3.2 reshape_reshape.11
  681.8 2.9 reshape.576
  (505 shorter events, 232.6 us)
Async XLA Ops:
  19.4 71.3 %all-gather.5.cloned.1.call-start = ((), (), s32[]{:S(2)}) async-start(), calls=%async_computation.9 | async-start | bytes 3072000 | tf_op jit(solution)/shard_map/all_gather | solution.py:510
  31.9 130.0 %all-gather.7.cloned.1.call-start = ((), (), s32[]{:S(2)}) async-start(), calls=%async_computation.10 | async-start | bytes 6758400 | tf_op jit(solution)/shard_map/all_gather | solution.py:618
  37.7 24.5 %collective-permute-start.1 = (bf16[320,1600]{1,0:T(8,128)(2,1)}, bf16[320,1600]{1,0:T(8,128)(2,1)S(1)}, u32[]{:S(2)}, u32[]{:S(2)}) collective-permute-start(bf16[320,1600]{1,0:T(8,128)(2,1)} %get-tuple-element.319), channel_id=1, source_target_pairs={{0,2},{2,0},{1,3},{3,1},{4,6},{6,4},{5,7},{7,5},{8,10},{10,8},{9,1... | collective-permute-start | bytes 3072008 | tf_op jit(solution)/shard_map/ppermute | solution.py:49
  38.3 25.4 %collective-permute-start.3 = (bf16[320,1600]{1,0:T(8,128)(2,1)}, bf16[320,1600]{1,0:T(8,128)(2,1)S(1)}, u32[]{:S(2)}, u32[]{:S(2)}) collective-permute-start(bf16[320,1600]{1,0:T(8,128)(2,1)} %get-tuple-element.319), channel_id=1, source_target_pairs={{0,4},{4,0},{1,5},{5,1},{2,6},{6,2},{3,7},{7,3},{8,12},{12,8},{9,1... | collective-permute-start | bytes 3072008 | tf_op jit(solution)/shard_map/ppermute | solution.py:49
  38.9 25.7 %collective-permute-start = (bf16[320,1600]{1,0:T(8,128)(2,1)}, bf16[320,1600]{1,0:T(8,128)(2,1)}, u32[]{:S(2)}, u32[]{:S(2)}) collective-permute-start(bf16[320,1600]{1,0:T(8,128)(2,1)} %get-tuple-element.319), channel_id=1, source_target_pairs={{0,1},{1,0},{2,3},{3,2},{4,5},{5,4},{6,7},{7,6},{8,9},{9,8},{10,11... | collective-permute-start | bytes 3072008 | tf_op jit(solution)/shard_map/ppermute | solution.py:49
  87.4 62.1 %collective-permute-start.8 = (bf16[320,1600]{1,0:T(8,128)(2,1)}, bf16[320,1600]{1,0:T(8,128)(2,1)}, u32[]{:S(2)}, u32[]{:S(2)}) collective-permute-start(bf16[320,1600]{1,0:T(8,128)(2,1)} %param.18), channel_id=1, source_target_pairs={{0,2},{2,0},{1,3},{3,1},{4,6},{6,4},{5,7},{7,5},{8,10},{10,8},{9,1... | collective-permute-start | bytes 3072008 | tf_op jit(solution)/shard_map/ppermute | solution.py:49
  89.2 60.4 %collective-permute-start.9 = (bf16[320,1600]{1,0:T(8,128)(2,1)}, bf16[320,1600]{1,0:T(8,128)(2,1)}, u32[]{:S(2)}, u32[]{:S(2)}) collective-permute-start(bf16[320,1600]{1,0:T(8,128)(2,1)} %param.18), channel_id=1, source_target_pairs={{0,4},{4,0},{1,5},{5,1},{2,6},{6,2},{3,7},{7,3},{8,12},{12,8},{9,1... | collective-permute-start | bytes 3072008 | tf_op jit(solution)/shard_map/ppermute | solution.py:49
  105.0 43.2 %all-to-all-start.1 = ((bf16[8,50,800]{2,1,0:T(8,128)(2,1)}), bf16[8,50,800]{2,1,0:T(8,128)(2,1)S(1)}, u32[]{:S(2)}, u32[]{:S(2)}) async-start(bf16[8,50,800]{2,1,0:T(8,128)(2,1)} %reshape.575), calls=%async_computation.1 | async-start | bytes 1605632 | tf_op jit(solution)/shard_map/all_to_all | solution.py:494
  108.6 187.8 %all-gather.9.cloned.1.call-start = ((), (), s32[]{:S(2)}) async-start(), calls=%async_computation.11 | async-start | bytes 3584000 | tf_op jit(solution)/shard_map/all_gather | solution.py:510
  177.1 37.3 %collective-permute-start.26 = (bf16[160,1600]{1,0:T(8,128)(2,1)}, bf16[160,1600]{1,0:T(8,128)(2,1)}, u32[]{:S(2)}, u32[]{:S(2)}) collective-permute-start(bf16[160,1600]{1,0:T(8,128)(2,1)} %slice.209), channel_id=1, source_target_pairs={{0,4},{4,0},{1,5},{5,1},{2,6},{6,2},{3,7},{7,3},{8,12},{12,8},{9,1... | collective-permute-start | bytes 1536008 | tf_op jit(solution)/shard_map/ppermute | solution.py:49
  180.5 33.9 %collective-permute-start.27 = (bf16[160,1600]{1,0:T(8,128)(2,1)}, bf16[160,1600]{1,0:T(8,128)(2,1)}, u32[]{:S(2)}, u32[]{:S(2)}) collective-permute-start(bf16[160,1600]{1,0:T(8,128)(2,1)} %slice.210), channel_id=1, source_target_pairs={{0,2},{2,0},{1,3},{3,1},{4,6},{6,4},{5,7},{7,5},{8,10},{10,8},{9,1... | collective-permute-start | bytes 1536008 | tf_op jit(solution)/shard_map/ppermute | solution.py:49
  181.1 128.3 %all-gather.11.cloned.1.call-start = ((), (), s32[]{:S(2)}) async-start(), calls=%async_computation.12 | async-start | bytes 3328000 | tf_op jit(solution)/shard_map/all_gather | solution.py:628
  182.2 40.4 %collective-permute-start.10 = (bf16[320,1600]{1,0:T(8,128)(2,1)}, bf16[320,1600]{1,0:T(8,128)(2,1)}, u32[]{:S(2)}, u32[]{:S(2)}) collective-permute-start(bf16[320,1600]{1,0:T(8,128)(2,1)} %get-tuple-element.113), channel_id=1, source_target_pairs={{0,1},{1,0},{2,3},{3,2},{4,5},{5,4},{6,7},{7,6},{8,9},{9,8},{10,11... | collective-permute-start | bytes 3072008 | tf_op jit(solution)/shard_map/ppermute | solution.py:49
  184.5 18.4 %collective-permute-start.15 = (bf16[160,1600]{1,0:T(8,128)(2,1)S(1)}, bf16[160,1600]{1,0:T(8,128)(2,1)S(1)}, u32[]{:S(2)}, u32[]{:S(2)}) collective-permute-start(bf16[160,1600]{1,0:T(8,128)(2,1)S(1)} %get-tuple-element.121), channel_id=1, source_target_pairs={{0,4},{4,0},{1,5},{5,1},{2,6},{6,2},{3,7},{7,3},{8,12},{12,8},{9,1... | collective-permute-start | bytes 1536008 | tf_op jit(solution)/shard_map/ppermute | solution.py:49
  187.6 18.5 %collective-permute-start.13 = (bf16[160,1600]{1,0:T(8,128)(2,1)S(1)}, bf16[160,1600]{1,0:T(8,128)(2,1)S(1)}, u32[]{:S(2)}, u32[]{:S(2)}) collective-permute-start(bf16[160,1600]{1,0:T(8,128)(2,1)S(1)} %get-tuple-element.118), channel_id=1, source_target_pairs={{0,2},{2,0},{1,3},{3,1},{4,6},{6,4},{5,7},{7,5},{8,10},{10,8},{9,1... | collective-permute-start | bytes 1536008 | tf_op jit(solution)/shard_map/ppermute | solution.py:49
  207.2 24.9 %collective-permute-start.16 = (bf16[320,1600]{1,0:T(8,128)(2,1)}, bf16[320,1600]{1,0:T(8,128)(2,1)}, u32[]{:S(2)}, u32[]{:S(2)}) collective-permute-start(bf16[320,1600]{1,0:T(8,128)(2,1)} %pad_maximum_fusion.2), channel_id=1, source_target_pairs={{0,2},{2,0},{1,3},{3,1},{4,6},{6,4},{5,7},{7,5},{8,10},{10,8},{9,1... | collective-permute-start | bytes 3072008 | tf_op jit(solution)/shard_map/ppermute | solution.py:49
  207.8 24.7 %collective-permute-start.17 = (bf16[320,1600]{1,0:T(8,128)(2,1)}, bf16[320,1600]{1,0:T(8,128)(2,1)}, u32[]{:S(2)}, u32[]{:S(2)}) collective-permute-start(bf16[320,1600]{1,0:T(8,128)(2,1)} %pad_maximum_fusion.1), channel_id=1, source_target_pairs={{0,4},{4,0},{1,5},{5,1},{2,6},{6,2},{3,7},{7,3},{8,12},{12,8},{9,1... | collective-permute-start | bytes 3072008 | tf_op jit(solution)/shard_map/ppermute | solution.py:49
  215.7 23.7 %collective-permute-start.28 = (bf16[320,1600]{1,0:T(8,128)(2,1)}, bf16[320,1600]{1,0:T(8,128)(2,1)S(1)}, u32[]{:S(2)}, u32[]{:S(2)}) collective-permute-start(bf16[320,1600]{1,0:T(8,128)(2,1)} %param.18), channel_id=1, source_target_pairs={{0,1},{1,0},{2,3},{3,2},{4,5},{5,4},{6,7},{7,6},{8,9},{9,8},{10,11... | collective-permute-start | bytes 3072008 | tf_op jit(solution)/shard_map/ppermute | solution.py:49
  215.8 27.6 %collective-permute-start.29 = (bf16[320,1600]{1,0:T(8,128)(2,1)}, bf16[320,1600]{1,0:T(8,128)(2,1)S(1)}, u32[]{:S(2)}, u32[]{:S(2)}) collective-permute-start(bf16[320,1600]{1,0:T(8,128)(2,1)} %collective-permute-done.8), channel_id=1, source_target_pairs={{0,1},{1,0},{2,3},{3,2},{4,5},{5,4},{6,7},{7,6},{8,9},{9,8},{10,11... | collective-permute-start | bytes 3072008 | tf_op jit(solution)/shard_map/ppermute | solution.py:49
  222.6 24.2 %collective-permute-start.30 = (bf16[320,1600]{1,0:T(8,128)(2,1)}, bf16[320,1600]{1,0:T(8,128)(2,1)S(1)}, u32[]{:S(2)}, u32[]{:S(2)}) collective-permute-start(bf16[320,1600]{1,0:T(8,128)(2,1)} %collective-permute-done.9), channel_id=1, source_target_pairs={{0,1},{1,0},{2,3},{3,2},{4,5},{5,4},{6,7},{7,6},{8,9},{9,8},{10,11... | collective-permute-start | bytes 3072008 | tf_op jit(solution)/shard_map/ppermute | solution.py:49
  232.2 31.8 %collective-permute-start.31 = (bf16[320,1600]{1,0:T(8,128)(2,1)S(1)}, bf16[320,1600]{1,0:T(8,128)(2,1)S(1)}, u32[]{:S(2)}, u32[]{:S(2)}) collective-permute-start(bf16[320,1600]{1,0:T(8,128)(2,1)S(1)} %pad_maximum_fusion.3), channel_id=1, source_target_pairs={{0,1},{1,0},{2,3},{3,2},{4,5},{5,4},{6,7},{7,6},{8,9},{9,8},{10,11... | collective-permute-start | bytes 3072008 | tf_op jit(solution)/shard_map/ppermute | solution.py:49
  237.9 26.0 %collective-permute-start.19 = (bf16[320,1600]{1,0:T(8,128)(2,1)}, bf16[320,1600]{1,0:T(8,128)(2,1)}, u32[]{:S(2)}, u32[]{:S(2)}) collective-permute-start(bf16[320,1600]{1,0:T(8,128)(2,1)} %get-tuple-element.315), channel_id=1, source_target_pairs={{0,2},{2,0},{1,3},{3,1},{4,6},{6,4},{5,7},{7,5},{8,10},{10,8},{9,1... | collective-permute-start | bytes 3072008 | tf_op jit(solution)/shard_map/ppermute | solution.py:49
  239.4 29.0 %collective-permute-start.21 = (bf16[320,1600]{1,0:T(8,128)(2,1)}, bf16[320,1600]{1,0:T(8,128)(2,1)}, u32[]{:S(2)}, u32[]{:S(2)}) collective-permute-start(bf16[320,1600]{1,0:T(8,128)(2,1)} %get-tuple-element.315), channel_id=1, source_target_pairs={{0,4},{4,0},{1,5},{5,1},{2,6},{6,2},{3,7},{7,3},{8,12},{12,8},{9,1... | collective-permute-start | bytes 3072008 | tf_op jit(solution)/shard_map/ppermute | solution.py:49
  243.3 27.5 %collective-permute-start.18 = (bf16[320,1600]{1,0:T(8,128)(2,1)}, bf16[320,1600]{1,0:T(8,128)(2,1)}, u32[]{:S(2)}, u32[]{:S(2)}) collective-permute-start(bf16[320,1600]{1,0:T(8,128)(2,1)} %get-tuple-element.315), channel_id=1, source_target_pairs={{0,1},{1,0},{2,3},{3,2},{4,5},{5,4},{6,7},{7,6},{8,9},{9,8},{10,11... | collective-permute-start | bytes 3072008 | tf_op jit(solution)/shard_map/ppermute | solution.py:49
  264.0 19.9 %collective-permute-start.20 = (bf16[320,1600]{1,0:T(8,128)(2,1)}, bf16[320,1600]{1,0:T(8,128)(2,1)}, u32[]{:S(2)}, u32[]{:S(2)}) collective-permute-start(bf16[320,1600]{1,0:T(8,128)(2,1)} %collective-permute-done.19), channel_id=1, source_target_pairs={{0,1},{1,0},{2,3},{3,2},{4,5},{5,4},{6,7},{7,6},{8,9},{9,8},{10,11... | collective-permute-start | bytes 3072008 | tf_op jit(solution)/shard_map/ppermute | solution.py:49
  270.9 17.7 %collective-permute-start.22 = (bf16[320,1600]{1,0:T(8,128)(2,1)}, bf16[320,1600]{1,0:T(8,128)(2,1)S(1)}, u32[]{:S(2)}, u32[]{:S(2)}) collective-permute-start(bf16[320,1600]{1,0:T(8,128)(2,1)} %collective-permute-done.21), channel_id=1, source_target_pairs={{0,1},{1,0},{2,3},{3,2},{4,5},{5,4},{6,7},{7,6},{8,9},{9,8},{10,11... | collective-permute-start | bytes 3072008 | tf_op jit(solution)/shard_map/ppermute | solution.py:49
  291.8 49.6 %all-to-all-start.2 = ((bf16[8,50,2560]{2,1,0:T(8,128)(2,1)}), bf16[8,50,2560]{2,1,0:T(8,128)(2,1)}, u32[]{:S(2)}, u32[]{:S(2)}) async-start(bf16[8,50,2560]{2,1,0:T(8,128)(2,1)} %reshape.558), calls=%async_computation.2 | async-start | bytes 4587520 | tf_op jit(solution)/shard_map/all_to_all | solution.py:494
  296.2 222.2 %reduce-scatter.9.cloned.1.call-start = ((), (), s32[]{:S(2)}) async-start(), calls=%async_computation.14 | async-start | bytes 3584000 | tf_op jit(solution)/shard_map/reduce_scatter | solution.py:517
  346.4 21.4 %collective-permute-start.32 = (bf16[320,1600]{1,0:T(8,128)(2,1)S(1)}, bf16[320,1600]{1,0:T(8,128)(2,1)S(1)}, u32[]{:S(2)}, u32[]{:S(2)}) collective-permute-start(bf16[320,1600]{1,0:T(8,128)(2,1)S(1)} %get-tuple-element.136), channel_id=1, source_target_pairs={{0,1},{1,0},{2,3},{3,2},{4,5},{5,4},{6,7},{7,6},{8,9},{9,8},{10,11... | collective-permute-start | bytes 3072008 | tf_op jit(solution)/shard_map/ppermute | solution.py:49
  364.9 24.5 %collective-permute-start.38 = (bf16[320,1600]{1,0:T(8,128)(2,1)S(1)}, bf16[320,1600]{1,0:T(8,128)(2,1)S(1)}, u32[]{:S(2)}, u32[]{:S(2)}) collective-permute-start(bf16[320,1600]{1,0:T(8,128)(2,1)S(1)} %pad_maximum_fusion.5), channel_id=1, source_target_pairs={{0,2},{2,0},{1,3},{3,1},{4,6},{6,4},{5,7},{7,5},{8,10},{10,8},{9,1... | collective-permute-start | bytes 3072008 | tf_op jit(solution)/shard_map/ppermute | solution.py:49
  366.5 24.1 %collective-permute-start.39 = (bf16[320,1600]{1,0:T(8,128)(2,1)S(1)}, bf16[320,1600]{1,0:T(8,128)(2,1)S(1)}, u32[]{:S(2)}, u32[]{:S(2)}) collective-permute-start(bf16[320,1600]{1,0:T(8,128)(2,1)S(1)} %pad_maximum_fusion.4), channel_id=1, source_target_pairs={{0,4},{4,0},{1,5},{5,1},{2,6},{6,2},{3,7},{7,3},{8,12},{12,8},{9,1... | collective-permute-start | bytes 3072008 | tf_op jit(solution)/shard_map/ppermute | solution.py:49
  397.5 38.6 %collective-permute-start.41 = (bf16[320,1600]{1,0:T(8,128)(2,1)S(1)}, bf16[320,1600]{1,0:T(8,128)(2,1)}, u32[]{:S(2)}, u32[]{:S(2)}) collective-permute-start(bf16[320,1600]{1,0:T(8,128)(2,1)S(1)} %get-tuple-element.310), channel_id=1, source_target_pairs={{0,2},{2,0},{1,3},{3,1},{4,6},{6,4},{5,7},{7,5},{8,10},{10,8},{9,1... | collective-permute-start | bytes 3072008 | tf_op jit(solution)/shard_map/ppermute | solution.py:49
  398.1 41.0 %collective-permute-start.43 = (bf16[320,1600]{1,0:T(8,128)(2,1)S(1)}, bf16[320,1600]{1,0:T(8,128)(2,1)S(1)}, u32[]{:S(2)}, u32[]{:S(2)}) collective-permute-start(bf16[320,1600]{1,0:T(8,128)(2,1)S(1)} %get-tuple-element.310), channel_id=1, source_target_pairs={{0,4},{4,0},{1,5},{5,1},{2,6},{6,2},{3,7},{7,3},{8,12},{12,8},{9,1... | collective-permute-start | bytes 3072008 | tf_op jit(solution)/shard_map/ppermute | solution.py:49
  399.8 40.8 %collective-permute-start.40 = (bf16[320,1600]{1,0:T(8,128)(2,1)S(1)}, bf16[320,1600]{1,0:T(8,128)(2,1)}, u32[]{:S(2)}, u32[]{:S(2)}) collective-permute-start(bf16[320,1600]{1,0:T(8,128)(2,1)S(1)} %get-tuple-element.310), channel_id=1, source_target_pairs={{0,1},{1,0},{2,3},{3,2},{4,5},{5,4},{6,7},{7,6},{8,9},{9,8},{10,11... | collective-permute-start | bytes 3072008 | tf_op jit(solution)/shard_map/ppermute | solution.py:49
  410.8 130.1 %reduce-scatter.7.cloned.1.call-start = ((), (), s32[]{:S(2)}) async-start(), calls=%async_computation.13 | async-start | bytes 9584640 | tf_op jit(solution)/shard_map/reduce_scatter | solution.py:689
  464.6 56.0 %collective-permute-start.48 = (bf16[200,1600]{1,0:T(8,128)(2,1)}, bf16[200,1600]{1,0:T(8,128)(2,1)S(1)}, u32[]{:S(2)}, u32[]{:S(2)}) collective-permute-start(bf16[200,1600]{1,0:T(8,128)(2,1)} %get-tuple-element.348), channel_id=1, source_target_pairs={{0,8},{8,16},{16,24},{24,0},{1,9},{9,17},{17,25},{25,1},{2,10},{10... | collective-permute-start | bytes 1920008 | tf_op jit(solution)/shard_map/ppermute | solution.py:120
  466.0 54.7 %collective-permute-start.49 = (bf16[200,1600]{1,0:T(8,128)(2,1)}, bf16[200,1600]{1,0:T(8,128)(2,1)S(1)}, u32[]{:S(2)}, u32[]{:S(2)}) collective-permute-start(bf16[200,1600]{1,0:T(8,128)(2,1)} %get-tuple-element.347), channel_id=1, source_target_pairs={{0,16},{8,24},{16,0},{24,8},{1,17},{9,25},{17,1},{25,9},{2,18},{10... | collective-permute-start | bytes 1920008 | tf_op jit(solution)/shard_map/ppermute | solution.py:120
  466.9 53.8 %collective-permute-start.50 = (bf16[200,1600]{1,0:T(8,128)(2,1)}, bf16[200,1600]{1,0:T(8,128)(2,1)S(1)}, u32[]{:S(2)}, u32[]{:S(2)}) collective-permute-start(bf16[200,1600]{1,0:T(8,128)(2,1)} %get-tuple-element.346), channel_id=1, source_target_pairs={{0,24},{8,0},{16,8},{24,16},{1,25},{9,1},{17,9},{25,17},{2,26},{10... | collective-permute-start | bytes 1920008 | tf_op jit(solution)/shard_map/ppermute | solution.py:120
  534.3 19.3 %collective-permute-start.51 = (bf16[320,1600]{1,0:T(8,128)(2,1)}, bf16[320,1600]{1,0:T(8,128)(2,1)}, u32[]{:S(2)}, u32[]{:S(2)}) collective-permute-start(bf16[320,1600]{1,0:T(8,128)(2,1)} %get-tuple-element.156), channel_id=1, source_target_pairs={{0,1},{1,0},{2,3},{3,2},{4,5},{5,4},{6,7},{7,6},{8,9},{9,8},{10,11... | collective-permute-start | bytes 3072008 | tf_op jit(solution)/shard_map/ppermute | solution.py:49
  534.3 19.3 %collective-permute-start.52 = (bf16[320,1600]{1,0:T(8,128)(2,1)}, bf16[320,1600]{1,0:T(8,128)(2,1)}, u32[]{:S(2)}, u32[]{:S(2)}) collective-permute-start(bf16[320,1600]{1,0:T(8,128)(2,1)} %get-tuple-element.157), channel_id=1, source_target_pairs={{0,1},{1,0},{2,3},{3,2},{4,5},{5,4},{6,7},{7,6},{8,9},{9,8},{10,11... | collective-permute-start | bytes 3072008 | tf_op jit(solution)/shard_map/ppermute | solution.py:49
  534.8 18.8 %collective-permute-start.53 = (bf16[320,1600]{1,0:T(8,128)(2,1)}, bf16[320,1600]{1,0:T(8,128)(2,1)}, u32[]{:S(2)}, u32[]{:S(2)}) collective-permute-start(bf16[320,1600]{1,0:T(8,128)(2,1)} %get-tuple-element.158), channel_id=1, source_target_pairs={{0,1},{1,0},{2,3},{3,2},{4,5},{5,4},{6,7},{7,6},{8,9},{9,8},{10,11... | collective-permute-start | bytes 3072008 | tf_op jit(solution)/shard_map/ppermute | solution.py:49
  534.8 18.8 %collective-permute-start.54 = (bf16[320,1600]{1,0:T(8,128)(2,1)}, bf16[320,1600]{1,0:T(8,128)(2,1)}, u32[]{:S(2)}, u32[]{:S(2)}) collective-permute-start(bf16[320,1600]{1,0:T(8,128)(2,1)} %get-tuple-element.159), channel_id=1, source_target_pairs={{0,1},{1,0},{2,3},{3,2},{4,5},{5,4},{6,7},{7,6},{8,9},{9,8},{10,11... | collective-permute-start | bytes 3072008 | tf_op jit(solution)/shard_map/ppermute | solution.py:49
  535.3 18.3 %all-to-all-start.3 = ((bf16[8,50,800]{2,1,0:T(8,128)(2,1)}), bf16[8,50,800]{2,1,0:T(8,128)(2,1)}, u32[]{:S(2)}, u32[]{:S(2)}) async-start(bf16[8,50,800]{2,1,0:T(8,128)(2,1)} %reshape.559), calls=%async_computation.5 | async-start | bytes 1605632 | tf_op jit(solution)/shard_map/all_to_all | solution.py:494
  539.6 106.3 %reduce-scatter.11.cloned.1.call-start = ((), (), s32[]{:S(2)}) async-start(), calls=%async_computation.15 | async-start | bytes 3072000 | tf_op jit(solution)/shard_map/reduce_scatter | solution.py:517
  573.1 44.5 %collective-permute-start.57 = (bf16[320,1600]{1,0:T(8,128)(2,1)S(1)}, bf16[320,1600]{1,0:T(8,128)(2,1)S(1)}, u32[]{:S(2)}, u32[]{:S(2)}) collective-permute-start(bf16[320,1600]{1,0:T(8,128)(2,1)S(1)} %pad_maximum_fusion.7), channel_id=1, source_target_pairs={{0,2},{2,0},{1,3},{3,1},{4,6},{6,4},{5,7},{7,5},{8,10},{10,8},{9,1... | collective-permute-start | bytes 3072008 | tf_op jit(solution)/shard_map/ppermute | solution.py:49
  574.3 44.3 %collective-permute-start.58 = (bf16[320,1600]{1,0:T(8,128)(2,1)}, bf16[320,1600]{1,0:T(8,128)(2,1)}, u32[]{:S(2)}, u32[]{:S(2)}) collective-permute-start(bf16[320,1600]{1,0:T(8,128)(2,1)} %pad_maximum_fusion.6), channel_id=1, source_target_pairs={{0,4},{4,0},{1,5},{5,1},{2,6},{6,2},{3,7},{7,3},{8,12},{12,8},{9,1... | collective-permute-start | bytes 3072008 | tf_op jit(solution)/shard_map/ppermute | solution.py:49
  576.7 21.5 %collective-permute-start.59 = (bf16[64,1600]{1,0:T(8,128)(2,1)S(1)}, bf16[64,1600]{1,0:T(8,128)(2,1)}, u32[]{:S(2)}, u32[]{:S(2)}) collective-permute-start(bf16[64,1600]{1,0:T(8,128)(2,1)S(1)} %convolution_convert_fusion.10), channel_id=1, source_target_pairs={{0,8},{8,0},{16,24},{24,16},{1,9},{9,1},{17,25},{25,17},{2,10},{10... | collective-permute-start | bytes 614408 | tf_op jit(solution)/shard_map/ppermute | solution.py:125
  651.5 40.9 %reduce-scatter.13.cloned.1.call-start = ((), (), s32[]{:S(2)}) async-start(), calls=%async_computation.16 | async-start | bytes 1064960 | tf_op jit(solution)/shard_map/reduce_scatter | solution.py:717
  (97 other events, 967.6 us)
Sparse Core Ops, SparseCore 0:
  32.0 51.4 all-gather.4
  86.4 75.5 all-gather.6
  181.2 57.3 all-gather.8
  240.0 54.1 all-gather.10
  411.0 54.6 reduce-scatter.8
  469.0 71.8 reduce-scatter.6
  553.7 62.7 reduce-scatter.10
  654.6 25.1 reduce-scatter.12
